TPU v7x, 512 devices: a whole 4x4x16 slice. The times are simulated.
512 devices in a mesh: gx: 32 (over z, core), gy: 16 (over x, y).
Axes of the slice: x: 4, y: 4, z: 16, core: 2. Of those that a mesh axis runs over, the one named last changes fastest.
Arguments:
- probes: bfloat16 [8, 4194304], P(None, ('gx', 'gy')), may hold values from -6 to 6
- cells: int32 [3, 4194304], P(None, ('gx', 'gy')), may hold values from 0 to 1023, as said below
- fractions: float32 [3, 4194304], P(None, ('gx', 'gy')), may hold values from 0 to 1
- counts: int32 [32, 16], P('gx', 'gy'), may hold values from 0 to 64, as said below
- kx: bfloat16 [1024, 1024], P('gx'), may hold values from 0 to 1
- ky: bfloat16 [1024, 1024], P('gy'), may hold values from 0 to 1
- kt: float32 [4, 4], replicated, may hold values from 0.25 to 1
Outputs:
- applied: bfloat16 [8, 4194304], P(None, ('gx', 'gy'))
Inputs may be any that keep to these rules, and one draw needn't show every extreme that they name: cells[0] lies in the x rows 32 * i to 32 * i + 31 and cells[1] in the y columns 64 * j to 64 * j + 63, where the slot lies on the device at index i of gx and j of gy; cells[2] is below 3. `counts`: slots of blocks at or past a device's count hold no observation; some device has 64 live blocks.
All inputs are finite; a program needn't handle non-finite values.
Results may differ from a plain program's by a relative error of at most 0.002.
The roundings to bfloat16 on the way count: a program that leaves them out, or rounds other values in their place, can miss the bound.
Values may be sent and summed in bfloat16 or wider, within the bound.
No kernel may reach another device: no remote copies, remote signals or barrier semaphores. Data moves between devices by JAX's collectives and lax.ppermute only.
A program may use at most 64 MiB of HBM per device.

v0:
```python
import jax
import jax.numpy as jnp
from jax import lax
from jax.sharding import PartitionSpec as P

DAYS = 4
PROBES = 8
BLOCK = 128


def extended_2(block, sides, width):
    for axis, dim in sides:
        count = lax.axis_size(axis)
        forward = [(i, i + 1) for i in range(count - 1)]
        backward = [(target, source) for source, target in forward]
        low = lax.ppermute(
            lax.slice_in_dim(block, block.shape[dim] - width, None, axis=dim), axis, forward
        )
        high = lax.ppermute(lax.slice_in_dim(block, 0, width, axis=dim), axis, backward)
        block = jnp.concatenate([low, block, high], axis=dim)
    return block


def keys_weights(fraction):
    first = ((-0.5 * fraction + 1.0) * fraction - 0.5) * fraction
    second = (1.5 * fraction - 2.5) * fraction * fraction + 1.0
    third = ((-1.5 * fraction + 2.0) * fraction + 0.5) * fraction
    fourth = (0.5 * fraction - 0.5) * fraction * fraction
    return (first, second, third, fourth)


def spread(cell_index, weights, extent):
    column = lax.broadcasted_iota(jnp.int32, (cell_index.shape[0], extent), 1)
    result = jnp.zeros((cell_index.shape[0], extent), jnp.float32)
    for offset_k, weight in enumerate(weights):
        result = result + jnp.where(
            column == (cell_index + offset_k)[:, None], weight[:, None], 0.0
        )
    return result


def body(probes, cells, fractions, counts, kx, ky, kt):
    tile_rows = kx.shape[0]
    tile_cols = ky.shape[0]
    channels = DAYS * PROBES
    points = probes.shape[1]
    row_start = lax.axis_index("gx") * tile_rows
    col_start = lax.axis_index("gy") * tile_cols
    weights_x = spread(cells[0] - row_start, keys_weights(fractions[0]), tile_rows + 3)
    weights_y = spread(
        cells[1] - col_start,
        tuple(
            (
                w_part.astype(jnp.bfloat16).astype(jnp.float32)
                for w_part in keys_weights(fractions[1])
            )
        ),
        tile_cols + 3,
    ).astype(jnp.bfloat16)
    weights_t = spread(cells[2], (1.0 - fractions[2], fractions[2]), DAYS)
    live_mask = (lax.iota(jnp.int32, points) // BLOCK < counts[0, 0]).astype(jnp.float32)
    group_size = min(1024, points)
    group_count = points // group_size

    def scatter_group(number, running):
        offset = number * group_size
        x_part = lax.dynamic_slice_in_dim(weights_x, offset, group_size, 0)
        y_part = lax.dynamic_slice_in_dim(weights_y, offset, group_size, 0)
        t_part = lax.dynamic_slice_in_dim(weights_t, offset, group_size, 0)
        mask_part = lax.dynamic_slice_in_dim(live_mask, offset, group_size, 0)
        probe_part = (
            lax.dynamic_slice_in_dim(probes, offset, group_size, 1).astype(jnp.float32)
            * mask_part[None, :]
        )
        timed_values = t_part[:, :, None] * probe_part.T[:, None, :]
        weighted = (timed_values.reshape(group_size, 1, channels) * x_part[:, :, None]).astype(
            jnp.bfloat16
        )
        return running + jnp.einsum(
            "pac,pb->acb", weighted, y_part, preferred_element_type=jnp.float32
        )

    extended = lax.fori_loop(
        0,
        group_count,
        scatter_group,
        jnp.zeros((tile_rows + 3, channels, tile_cols + 3), jnp.float32),
    )
    rim_rows = jnp.concatenate([extended[0:1], extended[tile_rows + 1 : tile_rows + 3]], axis=0)
    received = extended_2(rim_rows, (("gx", 0),), 2)
    core_sum = extended[1 : tile_rows + 1]
    core_sum = core_sum + jnp.pad(received[0:2], ((0, tile_rows - 2), (0, 0), (0, 0)))
    core_sum = core_sum + jnp.pad(received[5:6], ((tile_rows - 1, 0), (0, 0), (0, 0)))
    rim_cols = jnp.concatenate(
        [core_sum[:, :, 0:1], core_sum[:, :, tile_cols + 1 : tile_cols + 3]], axis=2
    )
    received = extended_2(rim_cols, (("gy", 2),), 2)
    grid_sum = core_sum[:, :, 1 : tile_cols + 1]
    grid_sum = grid_sum + jnp.pad(received[:, :, 0:2], ((0, 0), (0, 0), (0, tile_cols - 2)))
    grid_sum = grid_sum + jnp.pad(received[:, :, 5:6], ((0, 0), (0, 0), (tile_cols - 1, 0)))
    grid_sum = grid_sum.astype(jnp.bfloat16)
    portion = lax.all_gather(grid_sum, "gx", axis=0, tiled=True)
    kernel_part = kx
    mixed_x = jnp.dot(
        kernel_part,
        portion.reshape(portion.shape[0], channels * tile_cols),
        preferred_element_type=jnp.float32,
    )
    mixed_x = mixed_x.reshape(tile_rows, channels, tile_cols).astype(jnp.bfloat16)
    kernel_part = ky
    crossed = jnp.einsum(
        "xcn,yn->xcy",
        lax.all_gather(mixed_x, "gy", axis=2, tiled=True),
        kernel_part,
        preferred_element_type=jnp.float32,
    )
    crossed = crossed.reshape(tile_rows, DAYS, PROBES, tile_cols)
    smooth = jnp.einsum("st,xtqy->xsqy", kt, crossed, precision=lax.Precision.HIGHEST)
    smooth = smooth.reshape(tile_rows, channels, tile_cols).astype(jnp.bfloat16)
    padded = extended_2(smooth, (("gx", 0), ("gy", 2)), 2)
    window = padded[1:, :, 1:]

    def gather_group(number, result):
        offset = number * group_size
        x_part = lax.dynamic_slice_in_dim(weights_x, offset, group_size, 0)
        y_part = lax.dynamic_slice_in_dim(weights_y, offset, group_size, 0)
        t_part = lax.dynamic_slice_in_dim(weights_t, offset, group_size, 0)
        mask_part = lax.dynamic_slice_in_dim(live_mask, offset, group_size, 0)
        hidden = jnp.einsum("pb,acb->pac", y_part, window, preferred_element_type=jnp.float32)
        hidden = hidden.reshape(group_size, tile_rows + 3, DAYS, PROBES)
        summed = jnp.einsum(
            "pa,pt,patq->qp", x_part, t_part, hidden, precision=lax.Precision.HIGHEST
        )
        summed = (summed * mask_part[None, :]).astype(jnp.bfloat16)
        return lax.dynamic_update_slice_in_dim(result, summed, offset, 1)

    return lax.fori_loop(0, group_count, gather_group, jnp.zeros((PROBES, points), jnp.bfloat16))


def solution(mesh):
    return jax.shard_map(
        body,
        mesh=mesh,
        in_specs=(
            P(None, ("gx", "gy")),
            P(None, ("gx", "gy")),
            P(None, ("gx", "gy")),
            P("gx", "gy"),
            P("gx", None),
            P("gy", None),
            P(),
        ),
        out_specs=P(None, ("gx", "gy")),
        check_vma=False,
    )
```

profile of v0, /device:TPU:1, one launch (start us, length us, event | category | flops | bytes accessed | tf_op | source)
XLA Modules:
  0.0 303.9 jit_solution(14837915549284763806)
XLA Ops:
  11.1 26.3 %while.28 = (s32[]{:T(128)}, f32[35,32,67]{2,1,0:T(8,128)}, f32[8192,4]{0,1:T(4,128)S(1)}, bf16[8,8192]{1,0:T(8,128)(2,1)}, f32[8192]{0:T(1024)S(1)}, /*index=5*...) while((s32[]{:T(128)}, f32[35,32,67]{2,1,0:T(8,128)}, ...), condition=%wide.region_1.2_spmd.clone, body=%wide.region_0.1_spmd.clone.sunk | while | flops 156174912 | bytes 1604025 | solution.py:83
  14.3 2.6 fusion.56
  17.7 2.6 fusion.56
  21.1 2.6 fusion.56
  24.5 2.6 fusion.56
  27.9 2.6 fusion.56
  31.4 2.6 fusion.56
  34.8 2.6 fusion.56
  38.9 8.7 %collective-permute-start.1 = (f32[2,32,67]{2,1,0:T(8,128)S(1)}, f32[2,32,67]{2,1,0:T(8,128)S(1)}, u32[]{:S(2)}, u32[]{:S(2)}) collective-permute-start(f32[2,32,67]{2,1,0:T(8,128)S(1)} %pad_maximum_fusion.6), channel_id=1, source_target_pairs={{16,0},{32,16},{48,32},{64,48},{80,64},{96,80},{112,96},{128,112},... | collective-permute-start | bytes 51464 | tf_op jit(solution)/shard_map/ppermute | solution.py:19
  47.6 1.9 collective-permute-start
  54.9 4.0 %collective-permute-start.2 = (f32[32,32,2]{2,1,0:T(8,128)S(1)}, f32[32,32,2]{2,1,0:T(8,128)S(1)}, u32[]{:S(2)}, u32[]{:S(2)}) collective-permute-start(f32[32,32,2]{2,1,0:T(8,128)S(1)} %slice.95), channel_id=1, source_target_pairs={{0,1},{1,2},{2,3},{3,4},{4,5},{5,6},{6,7},{7,8},{8,9},{9,10},{10,1... | collective-permute-start | bytes 24584 | tf_op jit(solution)/shard_map/ppermute | solution.py:16
  59.0 10.1 %collective-permute-done.3 = f32[32,32,2]{2,1,0:T(8,128)S(1)} collective-permute-done((f32[32,32,2]{2,1,0:T(8,128)}, f32[32,32,2]{2,1,0:T(8,128)S(1)}, u32[]{:S(2)}, u32[]{:S(2)}) %collective-permute-start.3) | collective-permute-done | bytes 8224 | tf_op jit(solution)/shard_map/ppermute | solution.py:19
  70.9 83.0 %all-gather.3.cloned.1.call-done = bf16[1024,32,64]{2,1,0:T(8,128)(2,1)} async-done(((bf16[32,32,64]{2,1,0:T(8,128)(2,1)}), bf16[1024,32,64]{2,1,0:T(8,128)(2,1)}) %all-gather.3.cloned.1.call-update) | async-done | bytes 4194320 | tf_op jit(solution)/shard_map/all_gather | solution.py:102
  153.9 9.8 %copy.43 = bf16[1024,32,64]{0,2,1:T(8,128)(2,1)} copy(bf16[1024,32,64]{2,1,0:T(8,128)(2,1)} %all-gather.3.cloned.1.call-done) | data formatting | bytes 8388608 | tf_op jit(solution)/shard_map/all_gather | solution.py:102
  163.7 3.5 %fusion.15 = bf16[32,2048]{1,0:T(8,128)(2,1)S(1)} fusion(bf16[1024,2048]{0,1:T(8,128)(2,1)} %bitcast.74, bf16[32,1024]{1,0:T(8,128)(2,1)S(1)} %copy-done.3), kind=kOutput, calls=%fused_computation.31 | convolution fusion | flops 134283264 | bytes 4390912 | tf_op jit(solution)/shard_map/dot_general | solution.py:104
  169.0 82.0 %all-gather.5.cloned.1.call-done = bf16[32,32,1024]{1,0,2:T(8,128)(2,1)} async-done(((bf16[32,32,64]{1,0,2:T(8,128)(2,1)}), bf16[32,32,1024]{1,0,2:T(8,128)(2,1)}) %all-gather.5.cloned.1.call-update) | async-done | bytes 2097168 | tf_op jit(solution)/shard_map/all_gather | solution.py:113
  251.1 6.9 %fusion.16 = f32[32,4,8,64]{3,2,1,0:T(8,128)S(1)} fusion(bf16[32,32,1024]{1,0,2:T(8,128)(2,1)} %all-gather.5.cloned.1.call-done, bf16[64,1024]{1,0:T(8,128)(2,1)S(1)} %copy-done), kind=kOutput, calls=%fused_computation.37 | convolution fusion | flops 134217728 | bytes 2490368 | tf_op jit(solution)/shard_map/xcn,yn->xcy/dot_general | solution.py:111
  259.1 3.9 %collective-permute-start.4 = (bf16[2,32,64]{2,1,0:T(8,128)(2,1)S(1)}, bf16[2,32,64]{2,1,0:T(8,128)(2,1)S(1)}, u32[]{:S(2)}, u32[]{:S(2)}) collective-permute-start(bf16[2,32,64]{2,1,0:T(8,128)(2,1)S(1)} %bitcast.89), channel_id=1, source_target_pairs={{0,16},{16,32},{32,48},{48,64},{64,80},{80,96},{96,112},{112,128},... | collective-permute-start | bytes 24584 | tf_op jit(solution)/shard_map/ppermute | solution.py:16
  263.0 1.9 collective-permute-start.5
  265.0 3.1 %collective-permute-done.5 = bf16[2,32,64]{2,1,0:T(8,128)(2,1)S(1)} collective-permute-done((bf16[2,32,64]{2,1,0:T(8,128)(2,1)S(1)}, bf16[2,32,64]{2,1,0:T(8,128)(2,1)S(1)}, u32[]{:S(2)}, u32[]{:S(2)}) %collective-permute-start.5) | collective-permute-done | bytes 8224 | tf_op jit(solution)/shard_map/ppermute | solution.py:19
  268.3 3.1 %collective-permute-start.6 = (bf16[36,32,2]{2,1,0:T(8,128)(2,1)S(1)}, bf16[36,32,2]{2,1,0:T(8,128)(2,1)S(1)}, u32[]{:S(2)}, u32[]{:S(2)}) collective-permute-start(bf16[36,32,2]{2,1,0:T(8,128)(2,1)S(1)} %get-tuple-element.342), channel_id=1, source_target_pairs={{0,1},{1,2},{2,3},{3,4},{4,5},{5,6},{6,7},{7,8},{8,9},{9,10},{10,1... | collective-permute-start | bytes 13832 | tf_op jit(solution)/shard_map/ppermute | solution.py:16
  272.6 4.0 %collective-permute-done.6 = bf16[36,32,2]{2,1,0:T(8,128)(2,1)S(1)} collective-permute-done((bf16[36,32,2]{2,1,0:T(8,128)(2,1)S(1)}, bf16[36,32,2]{2,1,0:T(8,128)(2,1)S(1)}, u32[]{:S(2)}, u32[]{:S(2)}) %collective-permute-start.6) | collective-permute-done | bytes 4640 | tf_op jit(solution)/shard_map/ppermute | solution.py:16
  276.6 4.1 %collective-permute-done.7 = bf16[36,32,2]{2,1,0:T(8,128)(2,1)S(1)} collective-permute-done((bf16[36,32,2]{2,1,0:T(8,128)(2,1)S(1)}, bf16[36,32,2]{2,1,0:T(8,128)(2,1)S(1)}, u32[]{:S(2)}, u32[]{:S(2)}) %collective-permute-start.7) | collective-permute-done | bytes 4640 | tf_op jit(solution)/shard_map/ppermute | solution.py:19
  281.2 15.2 %while.27 = (s32[]{:T(128)}, bf16[8,8192]{1,0:T(8,128)(2,1)S(1)}, f32[8192,35]{0,1:T(8,128)S(1)}, bf16[8192,67]{0,1:T(8,128)(2,1)}, bf16[35,32,67]{2,0,1:T(8,128...) while((s32[]{:T(128)}, bf16[8,8192]{1,0:T(8,128)(2,1)S(1)}, ...), condition=%wide.region_3.4_spmd, body=%wide.region_2.3_spmd.sunk | while | flops 156016640 | bytes 1133295 | solution.py:137
  281.3 1.8 multiply_reduce_fusion.2
  283.2 1.8 multiply_reduce_fusion.2
  285.1 1.8 multiply_reduce_fusion.2
  287.0 1.8 multiply_reduce_fusion.2
  288.9 1.8 multiply_reduce_fusion.2
  290.8 1.8 multiply_reduce_fusion.2
  292.7 1.8 multiply_reduce_fusion.2
  294.5 1.8 multiply_reduce_fusion.2
  (137 shorter events, 26.3 us)
Async XLA Ops:
  6.5 244.5 %copy-start = (bf16[64,1024]{1,0:T(8,128)(2,1)S(1)}, bf16[64,1024]{1,0:T(8,128)(2,1)}, u32[]{:S(2)}) copy-start(bf16[64,1024]{1,0:T(8,128)(2,1)} %param.16) | copy-start | bytes 393220
  6.5 147.3 %all-gather.3.cloned.1.call-start = ((), (), s32[]{:S(2)}) async-start(), calls=%async_computation | async-start | bytes 8650752 | tf_op jit(solution)/shard_map/all_gather | solution.py:102
  37.4 13.3 %copy-start.1 = (bf16[8192,67]{0,1:T(8,128)(2,1)}, bf16[8192,67]{0,1:T(8,128)(2,1)S(1)}, u32[]{:S(2)}) copy-start(bf16[8192,67]{0,1:T(8,128)(2,1)S(1)} %get-tuple-element.525) | copy-start | bytes 3293188
  38.9 10.7 %collective-permute-start.1 = (f32[2,32,67]{2,1,0:T(8,128)S(1)}, f32[2,32,67]{2,1,0:T(8,128)S(1)}, u32[]{:S(2)}, u32[]{:S(2)}) collective-permute-start(f32[2,32,67]{2,1,0:T(8,128)S(1)} %pad_maximum_fusion.6), channel_id=1, source_target_pairs={{16,0},{32,16},{48,32},{64,48},{80,64},{96,80},{112,96},{128,112},... | collective-permute-start | bytes 51464 | tf_op jit(solution)/shard_map/ppermute | solution.py:19
  47.6 3.1 %collective-permute-start = (f32[2,32,67]{2,1,0:T(8,128)S(1)}, f32[2,32,67]{2,1,0:T(8,128)S(1)}, u32[]{:S(2)}, u32[]{:S(2)}) collective-permute-start(f32[2,32,67]{2,1,0:T(8,128)S(1)} %slice.77), channel_id=1, source_target_pairs={{0,16},{16,32},{32,48},{48,64},{64,80},{80,96},{96,112},{112,128},... | collective-permute-start | bytes 51464 | tf_op jit(solution)/shard_map/ppermute | solution.py:16
  53.7 15.4 %collective-permute-start.3 = (f32[32,32,2]{2,1,0:T(8,128)}, f32[32,32,2]{2,1,0:T(8,128)S(1)}, u32[]{:S(2)}, u32[]{:S(2)}) collective-permute-start(f32[32,32,2]{2,1,0:T(8,128)} %copy.42), channel_id=1, source_target_pairs={{1,0},{2,1},{3,2},{4,3},{5,4},{6,5},{7,6},{8,7},{9,8},{10,9},{11,1... | collective-permute-start | bytes 24584 | tf_op jit(solution)/shard_map/ppermute | solution.py:19
  54.9 14.8 %collective-permute-start.2 = (f32[32,32,2]{2,1,0:T(8,128)S(1)}, f32[32,32,2]{2,1,0:T(8,128)S(1)}, u32[]{:S(2)}, u32[]{:S(2)}) collective-permute-start(f32[32,32,2]{2,1,0:T(8,128)S(1)} %slice.95), channel_id=1, source_target_pairs={{0,1},{1,2},{2,3},{3,4},{4,5},{5,6},{6,7},{7,8},{8,9},{9,10},{10,1... | collective-permute-start | bytes 24584 | tf_op jit(solution)/shard_map/ppermute | solution.py:16
  70.8 92.8 %copy-start.3 = (bf16[32,1024]{1,0:T(8,128)(2,1)S(1)}, bf16[32,1024]{1,0:T(8,128)(2,1)}, u32[]{:S(2)}) copy-start(bf16[32,1024]{1,0:T(8,128)(2,1)} %param.15) | copy-start | bytes 196612
  70.8 180.2 %all-gather.5.cloned.1.call-start = ((), (), s32[]{:S(2)}) async-start(), calls=%async_computation.1 | async-start | bytes 8912896 | tf_op jit(solution)/shard_map/all_gather | solution.py:113
  169.0 88.9 %copy-start.4 = (f32[4,4]{1,0:T(4,128)S(1)}, f32[4,4]{1,0:T(4,128)}, u32[]{:S(2)}) copy-start(f32[4,4]{1,0:T(4,128)} %param.17) | copy-start | bytes 196
  259.1 5.9 %collective-permute-start.4 = (bf16[2,32,64]{2,1,0:T(8,128)(2,1)S(1)}, bf16[2,32,64]{2,1,0:T(8,128)(2,1)S(1)}, u32[]{:S(2)}, u32[]{:S(2)}) collective-permute-start(bf16[2,32,64]{2,1,0:T(8,128)(2,1)S(1)} %bitcast.89), channel_id=1, source_target_pairs={{0,16},{16,32},{32,48},{48,64},{64,80},{80,96},{96,112},{112,128},... | collective-permute-start | bytes 24584 | tf_op jit(solution)/shard_map/ppermute | solution.py:16
  263.0 5.1 %collective-permute-start.5 = (bf16[2,32,64]{2,1,0:T(8,128)(2,1)S(1)}, bf16[2,32,64]{2,1,0:T(8,128)(2,1)S(1)}, u32[]{:S(2)}, u32[]{:S(2)}) collective-permute-start(bf16[2,32,64]{2,1,0:T(8,128)(2,1)S(1)} %bitcast.90), channel_id=1, source_target_pairs={{16,0},{32,16},{48,32},{64,48},{80,64},{96,80},{112,96},{128,112},... | collective-permute-start | bytes 24584 | tf_op jit(solution)/shard_map/ppermute | solution.py:19
  268.3 8.4 %collective-permute-start.6 = (bf16[36,32,2]{2,1,0:T(8,128)(2,1)S(1)}, bf16[36,32,2]{2,1,0:T(8,128)(2,1)S(1)}, u32[]{:S(2)}, u32[]{:S(2)}) collective-permute-start(bf16[36,32,2]{2,1,0:T(8,128)(2,1)S(1)} %get-tuple-element.342), channel_id=1, source_target_pairs={{0,1},{1,2},{2,3},{3,4},{4,5},{5,6},{6,7},{7,8},{8,9},{9,10},{10,1... | collective-permute-start | bytes 13832 | tf_op jit(solution)/shard_map/ppermute | solution.py:16
  271.3 9.4 %collective-permute-start.7 = (bf16[36,32,2]{2,1,0:T(8,128)(2,1)S(1)}, bf16[36,32,2]{2,1,0:T(8,128)(2,1)S(1)}, u32[]{:S(2)}, u32[]{:S(2)}) collective-permute-start(bf16[36,32,2]{2,1,0:T(8,128)(2,1)S(1)} %get-tuple-element.343), channel_id=1, source_target_pairs={{1,0},{2,1},{3,2},{4,3},{5,4},{6,5},{7,6},{8,7},{9,8},{10,9},{11,1... | collective-permute-start | bytes 13832 | tf_op jit(solution)/shard_map/ppermute | solution.py:19
  296.4 0.7 copy-start.2
Sparse Core Ops, SparseCore 0:
  71.0 82.8 all-gather.2
  169.1 81.8 all-gather.4
where the time goes:
time: 307 us; the launch traced here: 304 us
  waiting for transfers between devices  188 us (61%)
  matrix products  45.6 us (15%)
  starting transfers between devices  26.2 us (9%)
  local copies, waits for them, and re-layouts  17.6 us (6%)
  between operations  14.4 us (5%)
  other arithmetic  11.4 us (4%)
    all_gather x1, waiting for transfers between devices, body(): portion = lax.all_gather(grid_sum, 'gx', axis=0, tiled=True)  83 us
    all_gather x1, waiting for transfers between devices, body(): lax.all_gather(mixed_x, 'gy', axis=2, tiled=True)  82 us
    dot_general x8, matrix products, scatter_group(): jnp.einsum('pac,pb->acb', weighted, y_part, preferred_element_type=jnp.fl...  20 us
    ppermute x4, waiting for transfers between devices, extended_2(): lax.ppermute(lax.slice_in_dim(block, 0, width, axis=dim), axis, backward)  17.3 us
    dot_general x8, matrix products, gather_group(): jnp.einsum('pb,acb->pac', y_part, window, preferred_element_type=jnp.floa...  14.1 us
    ppermute x4, starting transfers between devices, extended_2(): lax.ppermute(lax.slice_in_dim(block, 0, width, axis=dim), axis, backward)  13.2 us
    ppermute x4, starting transfers between devices, extended_2(): lax.ppermute(lax.slice_in_dim(block, block.shape[dim] - width, None, axis...  12.9 us
    all_gather x1, local copies, waits for them, and re-layouts, body(): portion = lax.all_gather(grid_sum, 'gx', axis=0, tiled=True)  9.78 us
  transfers between devices with their start and end apart: 10, of which 8 were waited for; matrix products, arithmetic and copies ran while one was open for 0% of the time, Pallas kernels for 0%

commit v1 on v0

v1 whole, which is shorter than its diff:
```python
import jax
import jax.numpy as jnp
from jax import lax
from jax.experimental import pallas as pl
from jax.experimental.pallas import tpu as pltpu
from jax.sharding import Mesh
from jax.sharding import PartitionSpec as P

DAYS = 4
PROBES = 8
BLOCK = 128
ROWS = 32
COLS = 64
XP = 40
YP = 80
CHUNK = 512
AXES = ("zh", "zl", "c", "x", "y")
GX = ("zh", "zl", "c")
NEAR = ("zl", "c")
GY = ("x", "y")
HIGH = lax.Precision.HIGHEST


def keys_weights(fraction):
    first = ((-0.5 * fraction + 1.0) * fraction - 0.5) * fraction
    second = (1.5 * fraction - 2.5) * fraction * fraction + 1.0
    third = ((-1.5 * fraction + 2.0) * fraction + 0.5) * fraction
    fourth = (0.5 * fraction - 0.5) * fraction * fraction
    return (first, second, third, fourth)


def spread(cell, weights, extent):
    row = lax.broadcasted_iota(jnp.int32, (extent, cell.shape[1]), 0) - cell
    result = jnp.where(row == 3, weights[3], 0.0)
    for k in (2, 1, 0):
        result = jnp.where(row == k, weights[k], result)
    return result


def point_factors(cells_ref, fractions_ref, where):
    x_part = spread(
        cells_ref[0:1, where] % ROWS, keys_weights(fractions_ref[0:1, where]), XP
    )
    y_part = spread(
        cells_ref[1:2, where] % COLS, keys_weights(fractions_ref[1:2, where]), YP
    )
    day = cells_ref[2:3, where]
    y_days = [jnp.where(day == d, y_part, 0.0) for d in range(DAYS - 1)]
    y_days.append(jnp.zeros((256 - 3 * YP, y_part.shape[1]), jnp.float32))
    y_days = jnp.concatenate(y_days, axis=0).astype(jnp.bfloat16)
    late = fractions_ref[2:3, where]
    return x_part, y_days, 1.0 - late, late


def live_lanes(count_ref, start, size):
    slot = start + lax.broadcasted_iota(jnp.int32, (1, size), 1)
    return slot // BLOCK < count_ref[0, 0]


def scatter_kernel(count_ref, probes_ref, cells_ref, fractions_ref, core_ref, rim_ref, acc_ref):
    points = probes_ref.shape[1]
    acc_ref[...] = jnp.zeros_like(acc_ref)

    def step(number, carry):
        start = pl.multiple_of(number * CHUNK, CHUNK)
        where = pl.ds(start, CHUNK)
        x_part, y_days, early, late = point_factors(cells_ref, fractions_ref, where)
        values = jnp.where(
            live_lanes(count_ref, start, CHUNK), probes_ref[:, where].astype(jnp.float32), 0.0
        )
        parts = []
        for weight in (early, late):
            timed = weight * values
            for q in range(PROBES):
                parts.append(timed[q : q + 1] * x_part)
        weighted = jnp.concatenate(parts, axis=0).astype(jnp.bfloat16)
        acc_ref[...] += lax.dot_general(
            weighted, y_days, (((1,), (1,)), ((), ())), preferred_element_type=jnp.float32
        )
        return carry

    lax.fori_loop(0, points // CHUNK, step, 0)
    rows = PROBES * XP
    blank = jnp.zeros((rows, 128), jnp.float32)
    first = jnp.concatenate([acc_ref[0:rows, :], blank], axis=1)
    second = jnp.concatenate([acc_ref[rows : 2 * rows, :], blank], axis=1)
    total = first + pltpu.roll(second, YP, 1)
    lane = lax.broadcasted_iota(jnp.int32, (rows, 384), 1)
    core = pltpu.roll(total, 383, 1)
    for t in range(1, DAYS):
        core = jnp.where(lane // COLS == t, pltpu.roll(total, 384 - (16 * t + 1), 1), core)
    core_ref[...] = core[:, 0:256]
    out_row = lax.broadcasted_iota(jnp.int32, (16, 384), 0)
    in_lane = lax.broadcasted_iota(jnp.int32, (16, 384), 1)
    low = (out_row < DAYS) & (in_lane == YP * out_row)
    high_row = out_row - 8
    high = (high_row >= 0) & (in_lane == YP * (high_row // 2) + (COLS + 1) + high_row % 2)
    pick = jnp.where(low | high, 1.0, 0.0)
    rim_ref[...] = lax.dot_general(
        pick, total, (((1,), (1,)), ((), ())), precision=HIGH, preferred_element_type=jnp.float32
    )


def scatter(counts, probes, cells, fractions):
    rows = PROBES * XP
    return pl.pallas_call(
        scatter_kernel,
        out_shape=(
            jax.ShapeDtypeStruct((rows, 256), jnp.float32),
            jax.ShapeDtypeStruct((16, rows), jnp.float32),
        ),
        in_specs=[
            pl.BlockSpec(memory_space=pltpu.SMEM),
            pl.BlockSpec(memory_space=pltpu.VMEM),
            pl.BlockSpec(memory_space=pltpu.VMEM),
            pl.BlockSpec(memory_space=pltpu.VMEM),
        ],
        scratch_shapes=[pltpu.VMEM((2 * rows, 256), jnp.float32)],
        name="scatter",
    )(counts, probes, cells, fractions)


def add_cols_kernel(core_ref, low_ref, high_ref, out_ref, first_ref, last_ref):
    row = lax.broadcasted_iota(jnp.int32, (16, 256), 0)
    lane = lax.broadcasted_iota(jnp.int32, (16, 256), 1)
    high_row = row - 8
    put = (row < DAYS) & (lane == COLS * row + (COLS - 1))
    put = put | ((high_row >= 0) & (lane == COLS * (high_row // 2) + high_row % 2))
    received = jnp.concatenate([low_ref[...], high_ref[...]], axis=0)
    out_ref[...] = core_ref[...] + lax.dot_general(
        received,
        jnp.where(put, 1.0, 0.0),
        (((0,), (0,)), ((), ())),
        precision=HIGH,
        preferred_element_type=jnp.float32,
    )
    first, last = [], []
    for q in range(PROBES):
        first.append(out_ref[q * XP : q * XP + 1, :])
        last.append(out_ref[q * XP + ROWS + 1 : q * XP + ROWS + 3, :])
    first_ref[...] = jnp.concatenate(first, axis=0)
    last_ref[...] = jnp.concatenate(last, axis=0)


def add_cols(core, low, high):
    return pl.pallas_call(
        add_cols_kernel,
        out_shape=(
            jax.ShapeDtypeStruct(core.shape, jnp.float32),
            jax.ShapeDtypeStruct((PROBES, 256), jnp.float32),
            jax.ShapeDtypeStruct((2 * PROBES, 256), jnp.float32),
        ),
        name="add_cols",
    )(core, low, high)


def add_rows_kernel(core_ref, first_ref, last_ref, out_ref):
    row = lax.broadcasted_iota(jnp.int32, (ROWS, 256), 0)
    for q in range(PROBES):
        tile = core_ref[q * XP + 1 : q * XP + 1 + ROWS, :]
        extra = jnp.where(row == ROWS - 1, first_ref[q : q + 1, :], 0.0)
        extra = jnp.where(row == 0, last_ref[2 * q : 2 * q + 1, :], extra)
        extra = jnp.where(row == 1, last_ref[2 * q + 1 : 2 * q + 2, :], extra)
        tile = (tile + extra).astype(jnp.bfloat16)
        for copy in range(4):
            out_ref[copy * PROBES + q] = tile


def add_rows(core, first, last):
    return pl.pallas_call(
        add_rows_kernel,
        out_shape=jax.ShapeDtypeStruct((4 * PROBES, ROWS, 256), jnp.bfloat16),
        name="add_rows",
    )(core, first, last)


def mix_x_kernel(place_ref, grid_ref, k0_ref, k1_ref, k2_ref, k3_ref, out_ref, rows_ref):
    zl, core = place_ref[0], place_ref[1]
    kernel = jnp.concatenate([k0_ref[...], k1_ref[...], k2_ref[...], k3_ref[...]], axis=0)
    mixed = jnp.dot(kernel, grid_ref[...], preferred_element_type=jnp.float32)
    rows_ref[0:8, :] = jnp.zeros((8, 256), jnp.float32)
    rows_ref[264:272, :] = jnp.zeros((8, 256), jnp.float32)
    for shift in range(4):
        source = (zl + 4 - shift) % 4
        for half in range(2):
            from_core = core if half == 0 else 1 - core
            base = (2 * shift + half) * XP
            target = pl.multiple_of(8 + ROWS * (2 * source + from_core), 8)
            rows_ref[pl.ds(target, ROWS), :] = mixed[base : base + ROWS]

            @pl.when((source == 3) & (from_core == 1))
            def _():
                rows_ref[7:8, :] = mixed[base + ROWS : base + ROWS + 1]

            @pl.when((source == 0) & (from_core == 0))
            def _():
                rows_ref[264:266, :] = mixed[base + ROWS + 1 : base + ROWS + 3]

    for tile in range(8):
        out_ref[tile] = rows_ref[7 + ROWS * tile : 7 + ROWS * tile + XP, :].astype(jnp.bfloat16)


def mix_x(place, grid, pieces):
    return pl.pallas_call(
        mix_x_kernel,
        out_shape=jax.ShapeDtypeStruct((8, XP, 256), jnp.bfloat16),
        in_specs=[pl.BlockSpec(memory_space=pltpu.SMEM)]
        + [pl.BlockSpec(memory_space=pltpu.VMEM)] * 5,
        scratch_shapes=[pltpu.VMEM((272, 256), jnp.float32)],
        name="mix_x",
    )(place, grid, *pieces)


def gather_kernel(
    count_ref, kt_ref, mixed_ref, ky_ref, cells_ref, fractions_ref, out_ref, window_ref
):
    points = out_ref.shape[1]
    rows = PROBES * XP
    lane = lax.broadcasted_iota(jnp.int32, (YP, 128), 1)
    gap = jnp.zeros((128 - YP, 256), jnp.float32)
    crossed = [jnp.zeros((rows, 256), jnp.float32) for _ in range(2)]
    for pair in range(8):
        here = ky_ref[:, 128 * pair : 128 * pair + 128].astype(jnp.float32)
        turned = pltpu.roll(here, COLS, 1)
        low, high = lane < COLS, lane >= COLS
        even = jnp.concatenate([jnp.where(low, here, 0.0), jnp.where(low, turned, 0.0)], axis=1)
        odd = jnp.concatenate([jnp.where(high, turned, 0.0), jnp.where(high, here, 0.0)], axis=1)
        kernel = jnp.concatenate([even, gap, odd, gap], axis=0).astype(jnp.bfloat16)
        for half in range(2):
            side = slice(128 * half, 128 * half + 128)
            left = jnp.concatenate(
                [mixed_ref[2 * pair, :, side], mixed_ref[2 * pair + 1, :, side]], axis=1
            )
            crossed[half] += lax.dot_general(
                left, kernel, (((1,), (1,)), ((), ())), preferred_element_type=jnp.float32
            )
    by_day = [crossed[t // 2][:, 128 * (t % 2) : 128 * (t % 2) + 128] for t in range(DAYS)]
    blank = jnp.zeros((rows, 128), jnp.float32)
    smooth = []
    for s in range(DAYS):
        total = kt_ref[s, 0] * by_day[0]
        for t in range(1, DAYS):
            total = total + kt_ref[s, t] * by_day[t]
        total = total.astype(jnp.bfloat16).astype(jnp.float32)
        smooth.append(jnp.concatenate([total, blank], axis=1))
    for late in range(2):
        window = smooth[late] + pltpu.roll(smooth[late + 1], YP, 1)
        window = window + pltpu.roll(smooth[late + 2], 2 * YP, 1)
        window_ref[late * rows : (late + 1) * rows, :] = window.astype(jnp.bfloat16)

    def step(number, carry):
        start = pl.multiple_of(number * CHUNK, CHUNK)
        where = pl.ds(start, CHUNK)
        x_part, y_days, early, late = point_factors(cells_ref, fractions_ref, where)
        hidden = jnp.dot(window_ref[...], y_days, preferred_element_type=jnp.float32)
        timed = early * hidden[0:rows] + late * hidden[rows : 2 * rows]
        sums = []
        for q in range(PROBES):
            sums.append(
                jnp.sum(timed[q * XP : (q + 1) * XP] * x_part, axis=0, keepdims=True)
            )
        result = jnp.concatenate(sums, axis=0)
        result = jnp.where(live_lanes(count_ref, start, CHUNK), result, 0.0)
        out_ref[:, where] = result.astype(jnp.bfloat16)
        return carry

    lax.fori_loop(0, points // CHUNK, step, 0)


def gather(counts, kt, mixed, ky, cells, fractions):
    rows = PROBES * XP
    return pl.pallas_call(
        gather_kernel,
        out_shape=jax.ShapeDtypeStruct((PROBES, cells.shape[1]), jnp.bfloat16),
        in_specs=[pl.BlockSpec(memory_space=pltpu.SMEM)] * 2
        + [pl.BlockSpec(memory_space=pltpu.VMEM)] * 4,
        scratch_shapes=[pltpu.VMEM((2 * rows, 256), jnp.bfloat16)],
        name="gather",
    )(counts, kt, mixed, ky, cells, fractions)


def up(count):
    return [(i, i + 1) for i in range(count - 1)]


def down(count):
    return [(i + 1, i) for i in range(count - 1)]


def body(probes, cells, fractions, counts, kx, ky, kt):
    before = lax.ppermute(kx[ROWS - 1 : ROWS], "zh", up(4))
    after = lax.ppermute(kx[0:2], "zh", down(4))
    own = jnp.concatenate([kx, before, after, jnp.zeros((XP - ROWS - 3, 1024), kx.dtype)], axis=0)
    other = lax.ppermute(own, "c", [(0, 1), (1, 0)])
    pair = jnp.concatenate([own, other], axis=0)
    pieces = [pair]
    for shift in range(1, 4):
        pieces.append(lax.ppermute(pair, "zl", [(i, (i + shift) % 4) for i in range(4)]))
    left = lax.ppermute(ky[COLS - 1 : COLS], GY, up(16))
    right = lax.ppermute(ky[0:2], GY, down(16))
    ky_wide = jnp.concatenate(
        [left, ky, right, jnp.zeros((YP - COLS - 3, 1024), ky.dtype)], axis=0
    )

    core, rim = scatter(counts, probes, cells, fractions)
    low = lax.ppermute(rim[0:8], GY, down(16))
    high = lax.ppermute(rim[8:16], GY, up(16))
    core, first, last = add_cols(core, low, high)
    first = lax.ppermute(first, GX, down(32))
    last = lax.ppermute(last, GX, up(32))
    grid = add_rows(core, first, last)
    grid = lax.all_to_all(grid, GX, 0, 0, tiled=True)
    place = jnp.stack([lax.axis_index("zl"), lax.axis_index("c")]).astype(jnp.int32)
    mixed = mix_x(place, grid.reshape(32 * ROWS, 256), pieces)
    mixed = lax.all_to_all(mixed, NEAR, 0, 0, tiled=True)
    mixed = jnp.broadcast_to(mixed.reshape(1, PROBES * XP, 256), (16, PROBES * XP, 256))
    mixed = lax.all_to_all(mixed, GY, 0, 0, tiled=True)
    return gather(counts, kt, mixed, ky_wide, cells, fractions)


def solution(mesh):
    fine = Mesh(mesh.devices.reshape(4, 4, 2, 4, 4), AXES)
    return jax.shard_map(
        body,
        mesh=fine,
        in_specs=(
            P(None, AXES),
            P(None, AXES),
            P(None, AXES),
            P(GX, GY),
            P(GX, None),
            P(GY, None),
            P(),
        ),
        out_specs=P(None, AXES),
        check_vma=False,
    )
```

time: 307 us -> 173 us (0.56)
  the two profiles are of different devices: /device:TPU:1 before, /device:TPU:128 now
where the time goes in v1:
time: 173 us; the launch traced here: 172 us
  starting transfers between devices  63.8 us (37%)
  waiting for transfers between devices  60.4 us (35%)
  Pallas kernels  27.1 us (16%)
  blocking collectives  11.9 us (7%)
  local copies, waits for them, and re-layouts  6.23 us (4%)
    all_to_all x1, starting transfers between devices, body(): grid = lax.all_to_all(grid, GX, 0, 0, tiled=True)  14.2 us
    ppermute x1, waiting for transfers between devices, body(): left = lax.ppermute(ky[COLS - 1:COLS], GY, up(16))  13.7 us
    ppermute x1, waiting for transfers between devices, body(): before = lax.ppermute(kx[ROWS - 1:ROWS], 'zh', up(4))  13.3 us
    all_to_all x1, blocking collectives, body(): mixed = lax.all_to_all(mixed, NEAR, 0, 0, tiled=True)  11.9 us
    pallas_call x1, Pallas kernels, gather(): pl.pallas_call(gather_kernel, out_shape=jax.ShapeDtypeStruct((PROBES, cel...  10.7 us
    all_to_all x1, starting transfers between devices, body(): mixed = lax.all_to_all(mixed, GY, 0, 0, tiled=True)  9.93 us
    pallas_call x1, Pallas kernels, scatter(): pl.pallas_call(scatter_kernel, out_shape=(jax.ShapeDtypeStruct((rows, 256...  9.91 us
    all_to_all x1, waiting for transfers between devices, body(): mixed = lax.all_to_all(mixed, GY, 0, 0, tiled=True)  9.8 us
  transfers between devices with their start and end apart: 14, of which 11 were waited for; matrix products, arithmetic and copies ran while one was open for 1% of the time, Pallas kernels for 0%

profile of v1, /device:TPU:128, one launch (start us, length us, event | category | flops | bytes accessed | tf_op | source)
XLA Modules:
  0.0 171.8 jit_solution(1077874802583126434)
XLA Ops:
  0.7 9.9 %scatter.1 = (f32[320,256]{1,0:T(8,128)}, f32[16,320]{1,0:T(8,128)}) custom-call(s32[1,1]{1,0:T(1,128)S(6)} %copy.8.count_ref, bf16[8,8192]{1,0:T(8,128)(2,1)} %probes_ref.1, s32[3,8192]{1,0:T(4,128)} %cells_ref.3, f32[3,8192]{1,0:T(4,128)} %fractions_ref.3), custom_call_target="tpu_custom_call" | custom-call | tf_op jit(solution)/shard_map/scatter/pallas_call | solution.py:106
  11.3 1.3 collective-permute-start
  12.6 4.5 %collective-permute-start.1 = (f32[8,320]{1,0:T(8,128)S(1)}, f32[8,320]{1,0:T(8,128)S(1)}, u32[]{:S(2)}, u32[]{:S(2)}) collective-permute-start(f32[8,320]{1,0:T(8,128)S(1)} %get-tuple-element.15), channel_id=1, source_target_pairs={{0,1},{1,2},{2,3},{3,4},{4,5},{5,6},{6,7},{7,8},{8,9},{9,10},{10,1... | collective-permute-start | bytes 30728 | tf_op jit(solution)/shard_map/ppermute | solution.py:307
  17.2 1.4 collective-permute-done.1.high_ref
  19.1 2.2 %add_cols.1 = (f32[320,256]{1,0:T(8,128)}, f32[8,256]{1,0:T(8,128)}, f32[16,256]{1,0:T(8,128)}) custom-call(f32[320,256]{1,0:T(8,128)} %get-tuple-element.10.core_ref, f32[8,320]{1,0:T(8,128)} %copy-done.9, f32[8,320]{1,0:T(8,128)} %copy-done.10), custom_call_target="tpu_custom_call" | custom-call | tf_op jit(solution)/shard_map/add_cols/pallas_call | solution.py:146
  21.4 1.9 %collective-permute-start.3 = (f32[16,256]{1,0:T(8,128)}, f32[16,256]{1,0:T(8,128)S(1)}, u32[]{:S(2)}, u32[]{:S(2)}) collective-permute-start(f32[16,256]{1,0:T(8,128)} %get-tuple-element.14), channel_id=1, source_target_pairs={{0,16},{16,32},{32,48},{48,64},{64,80},{80,96},{96,112},{112,128},... | collective-permute-start | bytes 49160 | tf_op jit(solution)/shard_map/ppermute | solution.py:310
  23.3 4.9 %collective-permute-start.2 = (f32[8,256]{1,0:T(8,128)}, f32[8,256]{1,0:T(8,128)S(1)}, u32[]{:S(2)}, u32[]{:S(2)}) collective-permute-start(f32[8,256]{1,0:T(8,128)} %get-tuple-element.13), channel_id=1, source_target_pairs={{16,0},{32,16},{48,32},{64,48},{80,64},{96,80},{112,96},{128,112},... | collective-permute-start | bytes 24584 | tf_op jit(solution)/shard_map/ppermute | solution.py:309
  28.1 1.6 collective-permute-done.2.first_ref
  30.3 1.9 %add_rows.1 = bf16[32,32,256]{2,1,0:T(8,128)(2,1)} custom-call(f32[320,256]{1,0:T(8,128)} %get-tuple-element.12.core_ref, f32[8,256]{1,0:T(8,128)} %copy-done.11, f32[16,256]{1,0:T(8,128)} %copy-done.8), custom_call_target="tpu_custom_call" | custom-call | tf_op jit(solution)/shard_map/add_rows/pallas_call | solution.py:170
  32.2 14.2 %all-to-all-start = ((bf16[32,32,256]{2,1,0:T(8,128)(2,1)}), bf16[32,32,256]{2,1,0:T(8,128)(2,1)S(1)}, u32[]{:S(2)}, u32[]{:S(2)}) async-start(bf16[32,32,256]{2,1,0:T(8,128)(2,1)} %add_rows.1), calls=%async_computation | async-start | bytes 1048576 | tf_op jit(solution)/shard_map/all_to_all | solution.py:312
  46.5 2.1 %collective-permute-start.5 = (bf16[2,1024]{1,0:T(2,128)(2,1)S(1)}, bf16[2,1024]{1,0:T(2,128)(2,1)S(1)}, u32[]{:S(2)}, u32[]{:S(2)}) collective-permute-start(bf16[2,1024]{1,0:T(2,128)(2,1)S(1)} %slice.21), channel_id=1, source_target_pairs={{128,0},{256,128},{384,256},{129,1},{257,129},{385,257},{130,2},{2... | collective-permute-start | bytes 12296 | tf_op jit(solution)/shard_map/ppermute | solution.py:292
  48.6 7.6 %collective-permute-start.4 = (bf16[1,1024]{1,0:T(2,128)(2,1)S(1)}, bf16[1,1024]{1,0:T(2,128)(2,1)S(1)}, u32[]{:S(2)}, u32[]{:S(2)}) collective-permute-start(bf16[1,1024]{1,0:T(2,128)(2,1)S(1)} %slice.20), channel_id=1, source_target_pairs={{0,128},{128,256},{256,384},{1,129},{129,257},{257,385},{2,130},{1... | collective-permute-start | bytes 6152 | tf_op jit(solution)/shard_map/ppermute | solution.py:291
  56.2 13.3 %collective-permute-done.4 = bf16[1,1024]{1,0:T(2,128)(2,1)S(1)} collective-permute-done((bf16[1,1024]{1,0:T(2,128)(2,1)S(1)}, bf16[1,1024]{1,0:T(2,128)(2,1)S(1)}, u32[]{:S(2)}, u32[]{:S(2)}) %collective-permute-start.4) | collective-permute-done | bytes 2080 | tf_op jit(solution)/shard_map/ppermute | solution.py:291
  69.5 6.1 %collective-permute-done.5 = bf16[2,1024]{1,0:T(2,128)(2,1)S(1)} collective-permute-done((bf16[2,1024]{1,0:T(2,128)(2,1)S(1)}, bf16[2,1024]{1,0:T(2,128)(2,1)S(1)}, u32[]{:S(2)}, u32[]{:S(2)}) %collective-permute-start.5) | collective-permute-done | bytes 4128 | tf_op jit(solution)/shard_map/ppermute | solution.py:292
  75.6 1.9 %collective-permute-start.6 = (bf16[40,1024]{1,0:T(8,128)(2,1)S(1)}, bf16[40,1024]{1,0:T(8,128)(2,1)S(1)}, u32[]{:S(2)}, u32[]{:S(2)}) collective-permute-start(bf16[40,1024]{1,0:T(8,128)(2,1)S(1)} %pad_maximum_fusion), channel_id=1, source_target_pairs={{0,16},{16,0},{1,17},{17,1},{2,18},{18,2},{3,19},{19,3},{4,20},{20... | collective-permute-start | bytes 245768 | tf_op jit(solution)/shard_map/ppermute | solution.py:294
  77.6 1.2 collective-permute-done.6
  78.8 2.3 %collective-permute-start.7 = (bf16[80,1024]{1,0:T(8,128)(2,1)S(1)}, bf16[80,1024]{1,0:T(8,128)(2,1)S(1)}, u32[]{:S(2)}, u32[]{:S(2)}) collective-permute-start(bf16[80,1024]{1,0:T(8,128)(2,1)S(1)} %concatenate.11.k0_ref), channel_id=1, source_target_pairs={{0,32},{32,64},{64,96},{96,0},{1,33},{33,65},{65,97},{97,1},{2,34}... | collective-permute-start | bytes 491528 | tf_op jit(solution)/shard_map/ppermute | solution.py:298
  81.2 2.0 %collective-permute-start.8 = (bf16[80,1024]{1,0:T(8,128)(2,1)S(1)}, bf16[80,1024]{1,0:T(8,128)(2,1)S(1)}, u32[]{:S(2)}, u32[]{:S(2)}) collective-permute-start(bf16[80,1024]{1,0:T(8,128)(2,1)S(1)} %concatenate.11.k0_ref), channel_id=1, source_target_pairs={{0,64},{32,96},{64,0},{96,32},{1,65},{33,97},{65,1},{97,33},{2,66}... | collective-permute-start | bytes 491528 | tf_op jit(solution)/shard_map/ppermute | solution.py:298
  83.1 5.3 %collective-permute-start.9 = (bf16[80,1024]{1,0:T(8,128)(2,1)S(1)}, bf16[80,1024]{1,0:T(8,128)(2,1)S(1)}, u32[]{:S(2)}, u32[]{:S(2)}) collective-permute-start(bf16[80,1024]{1,0:T(8,128)(2,1)S(1)} %concatenate.11.k0_ref), channel_id=1, source_target_pairs={{0,96},{32,0},{64,32},{96,64},{1,97},{33,1},{65,33},{97,65},{2,98}... | collective-permute-start | bytes 491528 | tf_op jit(solution)/shard_map/ppermute | solution.py:298
  89.7 6.2 %collective-permute-done.8.k2_ref = bf16[80,1024]{1,0:T(8,128)(2,1)S(1)} collective-permute-done((bf16[80,1024]{1,0:T(8,128)(2,1)S(1)}, bf16[80,1024]{1,0:T(8,128)(2,1)S(1)}, u32[]{:S(2)}, u32[]{:S(2)}) %collective-permute-start.8) | collective-permute-done | bytes 163872 | tf_op jit(solution)/shard_map/ppermute | solution.py:298
  97.4 2.4 %mix_x.1 = bf16[8,40,256]{2,1,0:T(8,128)(2,1)} custom-call(s32[2]{0:T(128)} %pad_add_fusion.place_ref, bf16[1024,256]{1,0:T(8,128)(2,1)} %bitcast.4, bf16[80,1024]{1,0:T(8,128)(2,1)} %copy-done.2, bf16[80,1024]{1,0:T(8,128)(2,1)} %copy-done.4, bf16[80,1024]{1,0:T(8,128)(2,1)} %copy-done.5, bf16[80,1024]{1,0:T(8,128)(2,1)} %copy-done.6), custom_call_target="tpu_custom_call" | custom-call | tf_op jit(solution)/shard_map/mix_x/pallas_call | solution.py:204
  99.8 11.9 %all_to_all.15 = bf16[8,40,256]{2,1,0:T(8,128)(2,1)S(1)} all-to-all(bf16[8,40,256]{2,1,0:T(8,128)(2,1)} %mix_x.1), channel_id=1, replica_groups=mesh['zh'=4,'zl'=4,'c'=2,'x'=4,'y'=4] {'zl','c'}, dimensions={0} | all-to-all | bytes 327680 | tf_op jit(solution)/shard_map/all_to_all | solution.py:315
  111.7 1.8 %broadcast_in_dim.15 = bf16[16,320,256]{2,1,0:T(8,128)(2,1)} broadcast(bf16[320,256]{1,0:T(8,128)(2,1)S(1)} %bitcast.5), dimensions={1,2} | broadcast | bytes 2785280 | tf_op jit(solution)/shard_map/broadcast_in_dim | solution.py:316
  113.5 9.9 %all-to-all-start.2 = ((bf16[16,320,256]{2,1,0:T(8,128)(2,1)}), bf16[16,320,256]{2,1,0:T(8,128)(2,1)S(1)}, u32[]{:S(2)}, u32[]{:S(2)}) async-start(bf16[16,320,256]{2,1,0:T(8,128)(2,1)} %broadcast_in_dim.15), calls=%async_computation.2 | async-start | bytes 5242880 | tf_op jit(solution)/shard_map/all_to_all | solution.py:317
  123.5 1.3 collective-permute-start.11
  124.8 4.5 %collective-permute-start.10 = (bf16[1,1024]{1,0:T(2,128)(2,1)S(1)}, bf16[1,1024]{1,0:T(2,128)(2,1)S(1)}, u32[]{:S(2)}, u32[]{:S(2)}) collective-permute-start(bf16[1,1024]{1,0:T(2,128)(2,1)S(1)} %slice.22), channel_id=1, source_target_pairs={{0,1},{1,2},{2,3},{3,4},{4,5},{5,6},{6,7},{7,8},{8,9},{9,10},{10,1... | collective-permute-start | bytes 6152 | tf_op jit(solution)/shard_map/ppermute | solution.py:299
  129.4 13.7 %collective-permute-done.10 = bf16[1,1024]{1,0:T(2,128)(2,1)S(1)} collective-permute-done((bf16[1,1024]{1,0:T(2,128)(2,1)S(1)}, bf16[1,1024]{1,0:T(2,128)(2,1)S(1)}, u32[]{:S(2)}, u32[]{:S(2)}) %collective-permute-start.10) | collective-permute-done | bytes 2080 | tf_op jit(solution)/shard_map/ppermute | solution.py:299
  143.1 6.0 %collective-permute-done.11 = bf16[2,1024]{1,0:T(2,128)(2,1)S(1)} collective-permute-done((bf16[2,1024]{1,0:T(2,128)(2,1)S(1)}, bf16[2,1024]{1,0:T(2,128)(2,1)S(1)}, u32[]{:S(2)}, u32[]{:S(2)}) %collective-permute-start.11) | collective-permute-done | bytes 4128 | tf_op jit(solution)/shard_map/ppermute | solution.py:300
  149.1 0.8 maximum_maximum_fusion.ky_ref
  149.8 9.8 %all-to-all-done.2.mixed_ref = bf16[16,320,256]{2,1,0:T(8,128)(2,1)S(1)} async-done(((bf16[16,320,256]{2,1,0:T(8,128)(2,1)}), bf16[16,320,256]{2,1,0:T(8,128)(2,1)S(1)}, u32[]{:S(2)}, u32[]{:S(2)}) %all-to-all-start.2) | async-done | bytes 2621472 | tf_op jit(solution)/shard_map/all_to_all | solution.py:317
  159.6 1.5 copy-done
  161.1 10.7 %gather.1 = bf16[8,8192]{1,0:T(8,128)(2,1)} custom-call(s32[1,1]{1,0:T(1,128)S(6)} %copy.8.count_ref, f32[4,4]{1,0:T(4,128)} %kt_ref.1, bf16[16,320,256]{2,1,0:T(8,128)(2,1)} %copy-done, bf16[80,1024]{1,0:T(8,128)(2,1)} %maximum_maximum_fusion.ky_ref, s32[3,8192]{1,0:T(4,128)} %cells_ref.3, f32[3,8192]{1,0:T(4,128)} %fractions_ref.3), custom_call_target="tpu_custom_call" | custom-call | tf_op jit(solution)/shard_map/gather/pallas_call | solution.py:272
  (39 shorter events, 4.8 us)
Async XLA Ops:
  0.0 46.4 %copy-start.3 = (bf16[32,1024]{1,0:T(8,128)(2,1)S(1)}, bf16[32,1024]{1,0:T(8,128)(2,1)}, u32[]{:S(2)}) copy-start(bf16[32,1024]{1,0:T(8,128)(2,1)} %param.11) | copy-start | bytes 196612
  11.3 5.8 %collective-permute-start = (f32[8,320]{1,0:T(8,128)S(1)}, f32[8,320]{1,0:T(8,128)S(1)}, u32[]{:S(2)}, u32[]{:S(2)}) collective-permute-start(f32[8,320]{1,0:T(8,128)S(1)} %get-tuple-element.16), channel_id=1, source_target_pairs={{1,0},{2,1},{3,2},{4,3},{5,4},{6,5},{7,6},{8,7},{9,8},{10,9},{11,1... | collective-permute-start | bytes 30728 | tf_op jit(solution)/shard_map/ppermute | solution.py:306
  12.6 5.9 %collective-permute-start.1 = (f32[8,320]{1,0:T(8,128)S(1)}, f32[8,320]{1,0:T(8,128)S(1)}, u32[]{:S(2)}, u32[]{:S(2)}) collective-permute-start(f32[8,320]{1,0:T(8,128)S(1)} %get-tuple-element.15), channel_id=1, source_target_pairs={{0,1},{1,2},{2,3},{3,4},{4,5},{5,6},{6,7},{7,8},{8,9},{9,10},{10,1... | collective-permute-start | bytes 30728 | tf_op jit(solution)/shard_map/ppermute | solution.py:307
  17.2 1.4 copy-start.9
  18.6 0.6 copy-start.10
  21.4 8.3 %collective-permute-start.3 = (f32[16,256]{1,0:T(8,128)}, f32[16,256]{1,0:T(8,128)S(1)}, u32[]{:S(2)}, u32[]{:S(2)}) collective-permute-start(f32[16,256]{1,0:T(8,128)} %get-tuple-element.14), channel_id=1, source_target_pairs={{0,16},{16,32},{32,48},{48,64},{64,80},{80,96},{96,112},{112,128},... | collective-permute-start | bytes 49160 | tf_op jit(solution)/shard_map/ppermute | solution.py:310
  23.3 6.4 %collective-permute-start.2 = (f32[8,256]{1,0:T(8,128)}, f32[8,256]{1,0:T(8,128)S(1)}, u32[]{:S(2)}, u32[]{:S(2)}) collective-permute-start(f32[8,256]{1,0:T(8,128)} %get-tuple-element.13), channel_id=1, source_target_pairs={{16,0},{32,16},{48,32},{64,48},{80,64},{96,80},{112,96},{128,112},... | collective-permute-start | bytes 24584 | tf_op jit(solution)/shard_map/ppermute | solution.py:309
  29.7 0.6 copy-start.11
  29.7 0.6 copy-start.8
  32.2 64.3 %all-to-all-start = ((bf16[32,32,256]{2,1,0:T(8,128)(2,1)}), bf16[32,32,256]{2,1,0:T(8,128)(2,1)S(1)}, u32[]{:S(2)}, u32[]{:S(2)}) async-start(bf16[32,32,256]{2,1,0:T(8,128)(2,1)} %add_rows.1), calls=%async_computation | async-start | bytes 1048576 | tf_op jit(solution)/shard_map/all_to_all | solution.py:312
  46.5 29.1 %collective-permute-start.5 = (bf16[2,1024]{1,0:T(2,128)(2,1)S(1)}, bf16[2,1024]{1,0:T(2,128)(2,1)S(1)}, u32[]{:S(2)}, u32[]{:S(2)}) collective-permute-start(bf16[2,1024]{1,0:T(2,128)(2,1)S(1)} %slice.21), channel_id=1, source_target_pairs={{128,0},{256,128},{384,256},{129,1},{257,129},{385,257},{130,2},{2... | collective-permute-start | bytes 12296 | tf_op jit(solution)/shard_map/ppermute | solution.py:292
  48.6 20.9 %collective-permute-start.4 = (bf16[1,1024]{1,0:T(2,128)(2,1)S(1)}, bf16[1,1024]{1,0:T(2,128)(2,1)S(1)}, u32[]{:S(2)}, u32[]{:S(2)}) collective-permute-start(bf16[1,1024]{1,0:T(2,128)(2,1)S(1)} %slice.20), channel_id=1, source_target_pairs={{0,128},{128,256},{256,384},{1,129},{129,257},{257,385},{2,130},{1... | collective-permute-start | bytes 6152 | tf_op jit(solution)/shard_map/ppermute | solution.py:291
  75.6 3.2 %collective-permute-start.6 = (bf16[40,1024]{1,0:T(8,128)(2,1)S(1)}, bf16[40,1024]{1,0:T(8,128)(2,1)S(1)}, u32[]{:S(2)}, u32[]{:S(2)}) collective-permute-start(bf16[40,1024]{1,0:T(8,128)(2,1)S(1)} %pad_maximum_fusion), channel_id=1, source_target_pairs={{0,16},{16,0},{1,17},{17,1},{2,18},{18,2},{3,19},{19,3},{4,20},{20... | collective-permute-start | bytes 245768 | tf_op jit(solution)/shard_map/ppermute | solution.py:294
  78.8 17.7 %copy-start.2 = (bf16[80,1024]{1,0:T(8,128)(2,1)}, bf16[80,1024]{1,0:T(8,128)(2,1)S(1)}, u32[]{:S(2)}) copy-start(bf16[80,1024]{1,0:T(8,128)(2,1)S(1)} %concatenate.11.k0_ref) | copy-start | bytes 491524
  78.8 10.9 %collective-permute-start.7 = (bf16[80,1024]{1,0:T(8,128)(2,1)S(1)}, bf16[80,1024]{1,0:T(8,128)(2,1)S(1)}, u32[]{:S(2)}, u32[]{:S(2)}) collective-permute-start(bf16[80,1024]{1,0:T(8,128)(2,1)S(1)} %concatenate.11.k0_ref), channel_id=1, source_target_pairs={{0,32},{32,64},{64,96},{96,0},{1,33},{33,65},{65,97},{97,1},{2,34}... | collective-permute-start | bytes 491528 | tf_op jit(solution)/shard_map/ppermute | solution.py:298
  81.2 14.8 %collective-permute-start.8 = (bf16[80,1024]{1,0:T(8,128)(2,1)S(1)}, bf16[80,1024]{1,0:T(8,128)(2,1)S(1)}, u32[]{:S(2)}, u32[]{:S(2)}) collective-permute-start(bf16[80,1024]{1,0:T(8,128)(2,1)S(1)} %concatenate.11.k0_ref), channel_id=1, source_target_pairs={{0,64},{32,96},{64,0},{96,32},{1,65},{33,97},{65,1},{97,33},{2,66}... | collective-permute-start | bytes 491528 | tf_op jit(solution)/shard_map/ppermute | solution.py:298
  83.1 13.4 %collective-permute-start.9 = (bf16[80,1024]{1,0:T(8,128)(2,1)S(1)}, bf16[80,1024]{1,0:T(8,128)(2,1)S(1)}, u32[]{:S(2)}, u32[]{:S(2)}) collective-permute-start(bf16[80,1024]{1,0:T(8,128)(2,1)S(1)} %concatenate.11.k0_ref), channel_id=1, source_target_pairs={{0,96},{32,0},{64,32},{96,64},{1,97},{33,1},{65,33},{97,65},{2,98}... | collective-permute-start | bytes 491528 | tf_op jit(solution)/shard_map/ppermute | solution.py:298
  89.7 6.8 %copy-start.4 = (bf16[80,1024]{1,0:T(8,128)(2,1)}, bf16[80,1024]{1,0:T(8,128)(2,1)S(1)}, u32[]{:S(2)}) copy-start(bf16[80,1024]{1,0:T(8,128)(2,1)S(1)} %collective-permute-done.7.k1_ref) | copy-start | bytes 491524
  96.0 0.7 copy-start.5
  96.5 0.7 copy-start.6
  96.5 0.9 copy-start.1
  113.5 9.9 %copy-start.7 = (bf16[64,1024]{1,0:T(8,128)(2,1)S(1)}, bf16[64,1024]{1,0:T(8,128)(2,1)}, u32[]{:S(2)}) copy-start(bf16[64,1024]{1,0:T(8,128)(2,1)} %param.12) | copy-start | bytes 393220
  113.5 46.1 %all-to-all-start.2 = ((bf16[16,320,256]{2,1,0:T(8,128)(2,1)}), bf16[16,320,256]{2,1,0:T(8,128)(2,1)S(1)}, u32[]{:S(2)}, u32[]{:S(2)}) async-start(bf16[16,320,256]{2,1,0:T(8,128)(2,1)} %broadcast_in_dim.15), calls=%async_computation.2 | async-start | bytes 5242880 | tf_op jit(solution)/shard_map/all_to_all | solution.py:317
  123.5 25.6 %collective-permute-start.11 = (bf16[2,1024]{1,0:T(2,128)(2,1)S(1)}, bf16[2,1024]{1,0:T(2,128)(2,1)S(1)}, u32[]{:S(2)}, u32[]{:S(2)}) collective-permute-start(bf16[2,1024]{1,0:T(2,128)(2,1)S(1)} %slice.23), channel_id=1, source_target_pairs={{1,0},{2,1},{3,2},{4,3},{5,4},{6,5},{7,6},{8,7},{9,8},{10,9},{11,1... | collective-permute-start | bytes 12296 | tf_op jit(solution)/shard_map/ppermute | solution.py:300
  124.8 18.3 %collective-permute-start.10 = (bf16[1,1024]{1,0:T(2,128)(2,1)S(1)}, bf16[1,1024]{1,0:T(2,128)(2,1)S(1)}, u32[]{:S(2)}, u32[]{:S(2)}) collective-permute-start(bf16[1,1024]{1,0:T(2,128)(2,1)S(1)} %slice.22), channel_id=1, source_target_pairs={{0,1},{1,2},{2,3},{3,4},{4,5},{5,6},{6,7},{7,8},{8,9},{9,10},{10,1... | collective-permute-start | bytes 6152 | tf_op jit(solution)/shard_map/ppermute | solution.py:299
  159.6 1.5 copy-start

commit v2 on v1

--- a/solution.py
+++ b/solution.py
@@ -57,7 +57,9 @@
     return slot // BLOCK < count_ref[0, 0]
 
 
-def scatter_kernel(count_ref, probes_ref, cells_ref, fractions_ref, core_ref, rim_ref, acc_ref):
+def scatter_kernel(
+    count_ref, probes_ref, cells_ref, fractions_ref, core_ref, low_ref, high_ref, acc_ref
+):
     points = probes_ref.shape[1]
     acc_ref[...] = jnp.zeros_like(acc_ref)
 
@@ -96,9 +98,11 @@
     high_row = out_row - 8
     high = (high_row >= 0) & (in_lane == YP * (high_row // 2) + (COLS + 1) + high_row % 2)
     pick = jnp.where(low | high, 1.0, 0.0)
-    rim_ref[...] = lax.dot_general(
+    rims = lax.dot_general(
         pick, total, (((1,), (1,)), ((), ())), precision=HIGH, preferred_element_type=jnp.float32
     )
+    low_ref[...] = rims[0:8]
+    high_ref[...] = rims[8:16]
 
 
 def scatter(counts, probes, cells, fractions):
@@ -107,7 +111,8 @@
         scatter_kernel,
         out_shape=(
             jax.ShapeDtypeStruct((rows, 256), jnp.float32),
-            jax.ShapeDtypeStruct((16, rows), jnp.float32),
+            jax.ShapeDtypeStruct((8, rows), jnp.float32),
+            jax.ShapeDtypeStruct((8, rows), jnp.float32),
         ),
         in_specs=[
             pl.BlockSpec(memory_space=pltpu.SMEM),
@@ -174,30 +179,16 @@
     )(core, first, last)
 
 
-def mix_x_kernel(place_ref, grid_ref, k0_ref, k1_ref, k2_ref, k3_ref, out_ref, rows_ref):
+def mix_x_kernel(place_ref, grid_ref, k0_ref, k1_ref, k2_ref, k3_ref, out_ref):
     zl, core = place_ref[0], place_ref[1]
     kernel = jnp.concatenate([k0_ref[...], k1_ref[...], k2_ref[...], k3_ref[...]], axis=0)
     mixed = jnp.dot(kernel, grid_ref[...], preferred_element_type=jnp.float32)
-    rows_ref[0:8, :] = jnp.zeros((8, 256), jnp.float32)
-    rows_ref[264:272, :] = jnp.zeros((8, 256), jnp.float32)
     for shift in range(4):
-        source = (zl + 4 - shift) % 4
+        tile = 2 * ((zl + 4 - shift) % 4)
         for half in range(2):
-            from_core = core if half == 0 else 1 - core
             base = (2 * shift + half) * XP
-            target = pl.multiple_of(8 + ROWS * (2 * source + from_core), 8)
-            rows_ref[pl.ds(target, ROWS), :] = mixed[base : base + ROWS]
-
-            @pl.when((source == 3) & (from_core == 1))
-            def _():
-                rows_ref[7:8, :] = mixed[base + ROWS : base + ROWS + 1]
-
-            @pl.when((source == 0) & (from_core == 0))
-            def _():
-                rows_ref[264:266, :] = mixed[base + ROWS + 1 : base + ROWS + 3]
-
-    for tile in range(8):
-        out_ref[tile] = rows_ref[7 + ROWS * tile : 7 + ROWS * tile + XP, :].astype(jnp.bfloat16)
+            part = mixed[base : base + XP].astype(jnp.bfloat16)
+            out_ref[tile + (core if half == 0 else 1 - core)] = part
 
 
 def mix_x(place, grid, pieces):
@@ -206,43 +197,62 @@
         out_shape=jax.ShapeDtypeStruct((8, XP, 256), jnp.bfloat16),
         in_specs=[pl.BlockSpec(memory_space=pltpu.SMEM)]
         + [pl.BlockSpec(memory_space=pltpu.VMEM)] * 5,
-        scratch_shapes=[pltpu.VMEM((272, 256), jnp.float32)],
         name="mix_x",
     )(place, grid, *pieces)
 
 
-def gather_kernel(
-    count_ref, kt_ref, mixed_ref, ky_ref, cells_ref, fractions_ref, out_ref, window_ref
-):
+def mix_y_kernel(place_ref, kt_ref, mixed_ref, k0_ref, k1_ref, k2_ref, k3_ref, out_ref):
+    rows = 2 * XP
+    low = lax.broadcasted_iota(jnp.int32, (rows, 128), 1) < COLS
+    left = [[] for _ in range(DAYS)]
+    for pair in range(8):
+        even = mixed_ref[2 * pair].astype(jnp.float32)
+        odd = mixed_ref[2 * pair + 1].astype(jnp.float32)
+        for side in range(2):
+            here = slice(128 * side, 128 * side + 128)
+            e, o = even[:, here], odd[:, here]
+            left[2 * side].append(jnp.where(low, e, pltpu.roll(o, COLS, 1)))
+            left[2 * side + 1].append(jnp.where(low, pltpu.roll(e, COLS, 1), o))
+    left = jnp.concatenate([jnp.concatenate(part, axis=1) for part in left], axis=0)
+    left = left.astype(jnp.bfloat16)
+    gap = jnp.zeros((128 - YP, 1024), jnp.bfloat16)
+    for half, (one, two) in enumerate(((k0_ref, k1_ref), (k2_ref, k3_ref))):
+        kernel = jnp.concatenate([one[...], gap, two[...], gap], axis=0)
+        crossed = lax.dot_general(
+            left, kernel, (((1,), (1,)), ((), ())), preferred_element_type=jnp.float32
+        )
+        by_day = [crossed[t * rows : (t + 1) * rows] for t in range(DAYS)]
+        smooth = []
+        for s in range(DAYS):
+            total = kt_ref[s, 0] * by_day[0]
+            for t in range(1, DAYS):
+                total = total + kt_ref[s, t] * by_day[t]
+            smooth.append(total)
+        smooth = jnp.concatenate(smooth, axis=0).astype(jnp.bfloat16)
+        for which in range(2):
+            target = (place_ref[2] + 4 - (2 * half + which)) % 4
+            out_ref[target] = smooth[:, 128 * which : 128 * which + 128]
+
+
+def mix_y(place, kt, mixed, pieces):
+    return pl.pallas_call(
+        mix_y_kernel,
+        out_shape=jax.ShapeDtypeStruct((4, DAYS * 2 * XP, 128), jnp.bfloat16),
+        in_specs=[pl.BlockSpec(memory_space=pltpu.SMEM)] * 2
+        + [pl.BlockSpec(memory_space=pltpu.VMEM)] * 5,
+        name="mix_y",
+    )(place, kt, mixed, *pieces)
+
+
+def gather_kernel(count_ref, smooth_ref, cells_ref, fractions_ref, out_ref, window_ref):
     points = out_ref.shape[1]
     rows = PROBES * XP
-    lane = lax.broadcasted_iota(jnp.int32, (YP, 128), 1)
-    gap = jnp.zeros((128 - YP, 256), jnp.float32)
-    crossed = [jnp.zeros((rows, 256), jnp.float32) for _ in range(2)]
-    for pair in range(8):
-        here = ky_ref[:, 128 * pair : 128 * pair + 128].astype(jnp.float32)
-        turned = pltpu.roll(here, COLS, 1)
-        low, high = lane < COLS, lane >= COLS
-        even = jnp.concatenate([jnp.where(low, here, 0.0), jnp.where(low, turned, 0.0)], axis=1)
-        odd = jnp.concatenate([jnp.where(high, turned, 0.0), jnp.where(high, here, 0.0)], axis=1)
-        kernel = jnp.concatenate([even, gap, odd, gap], axis=0).astype(jnp.bfloat16)
-        for half in range(2):
-            side = slice(128 * half, 128 * half + 128)
-            left = jnp.concatenate(
-                [mixed_ref[2 * pair, :, side], mixed_ref[2 * pair + 1, :, side]], axis=1
-            )
-            crossed[half] += lax.dot_general(
-                left, kernel, (((1,), (1,)), ((), ())), preferred_element_type=jnp.float32
-            )
-    by_day = [crossed[t // 2][:, 128 * (t % 2) : 128 * (t % 2) + 128] for t in range(DAYS)]
+    days = []
+    for s in range(DAYS):
+        part = [smooth_ref[source, s * 2 * XP : (s + 1) * 2 * XP, :] for source in range(4)]
+        days.append(jnp.concatenate(part, axis=0).astype(jnp.float32))
     blank = jnp.zeros((rows, 128), jnp.float32)
-    smooth = []
-    for s in range(DAYS):
-        total = kt_ref[s, 0] * by_day[0]
-        for t in range(1, DAYS):
-            total = total + kt_ref[s, t] * by_day[t]
-        total = total.astype(jnp.bfloat16).astype(jnp.float32)
-        smooth.append(jnp.concatenate([total, blank], axis=1))
+    smooth = [jnp.concatenate([day, blank], axis=1) for day in days]
     for late in range(2):
         window = smooth[late] + pltpu.roll(smooth[late + 1], YP, 1)
         window = window + pltpu.roll(smooth[late + 2], 2 * YP, 1)
@@ -267,16 +277,16 @@
     lax.fori_loop(0, points // CHUNK, step, 0)
 
 
-def gather(counts, kt, mixed, ky, cells, fractions):
+def gather(counts, smooth, cells, fractions):
     rows = PROBES * XP
     return pl.pallas_call(
         gather_kernel,
         out_shape=jax.ShapeDtypeStruct((PROBES, cells.shape[1]), jnp.bfloat16),
-        in_specs=[pl.BlockSpec(memory_space=pltpu.SMEM)] * 2
-        + [pl.BlockSpec(memory_space=pltpu.VMEM)] * 4,
+        in_specs=[pl.BlockSpec(memory_space=pltpu.SMEM)]
+        + [pl.BlockSpec(memory_space=pltpu.VMEM)] * 3,
         scratch_shapes=[pltpu.VMEM((2 * rows, 256), jnp.bfloat16)],
         name="gather",
-    )(counts, kt, mixed, ky, cells, fractions)
+    )(counts, smooth, cells, fractions)
 
 
 def up(count):
@@ -287,35 +297,46 @@
     return [(i + 1, i) for i in range(count - 1)]
 
 
+def around(kernel, axis, count, rows):
+    before = lax.ppermute(kernel[-1:], axis, up(count))
+    after = lax.ppermute(kernel[0:2], axis, down(count))
+    blank = jnp.zeros((rows - 3 - kernel.shape[0], kernel.shape[1]), kernel.dtype)
+    return jnp.concatenate([before, kernel, after, blank], axis=0)
+
+
+def turns(piece, axis):
+    return [piece] + [
+        lax.ppermute(piece, axis, [(i, (i + shift) % 4) for i in range(4)]) for shift in (1, 2, 3)
+    ]
+
+
 def body(probes, cells, fractions, counts, kx, ky, kt):
-    before = lax.ppermute(kx[ROWS - 1 : ROWS], "zh", up(4))
-    after = lax.ppermute(kx[0:2], "zh", down(4))
-    own = jnp.concatenate([kx, before, after, jnp.zeros((XP - ROWS - 3, 1024), kx.dtype)], axis=0)
+    own = around(kx, GX, 32, XP)
     other = lax.ppermute(own, "c", [(0, 1), (1, 0)])
     pair = jnp.concatenate([own, other], axis=0)
-    pieces = [pair]
-    for shift in range(1, 4):
-        pieces.append(lax.ppermute(pair, "zl", [(i, (i + shift) % 4) for i in range(4)]))
-    left = lax.ppermute(ky[COLS - 1 : COLS], GY, up(16))
-    right = lax.ppermute(ky[0:2], GY, down(16))
-    ky_wide = jnp.concatenate(
-        [left, ky, right, jnp.zeros((YP - COLS - 3, 1024), ky.dtype)], axis=0
-    )
-
-    core, rim = scatter(counts, probes, cells, fractions)
-    low = lax.ppermute(rim[0:8], GY, down(16))
-    high = lax.ppermute(rim[8:16], GY, up(16))
+    pair, probes = lax.optimization_barrier((pair, probes))
+    kx_pieces = turns(pair, "zl")
+
+    core, low, high = scatter(counts, probes, cells, fractions)
+    low = lax.ppermute(low, GY, down(16))
+    high = lax.ppermute(high, GY, up(16))
     core, first, last = add_cols(core, low, high)
+    first, last, kx_pieces = lax.optimization_barrier((first, last, kx_pieces))
     first = lax.ppermute(first, GX, down(32))
     last = lax.ppermute(last, GX, up(32))
     grid = add_rows(core, first, last)
+    grid, ky = lax.optimization_barrier((grid, ky))
     grid = lax.all_to_all(grid, GX, 0, 0, tiled=True)
-    place = jnp.stack([lax.axis_index("zl"), lax.axis_index("c")]).astype(jnp.int32)
-    mixed = mix_x(place, grid.reshape(32 * ROWS, 256), pieces)
+    ky_pieces = turns(around(ky, GY, 16, YP), "y")
+    place = [lax.axis_index(axis) for axis in ("zl", "c", "y")]
+    place = jnp.stack(place).astype(jnp.int32)
+    grid, ky_pieces, place = lax.optimization_barrier((grid, ky_pieces, place))
+    mixed = mix_x(place, grid.reshape(32 * ROWS, 256), kx_pieces)
     mixed = lax.all_to_all(mixed, NEAR, 0, 0, tiled=True)
-    mixed = jnp.broadcast_to(mixed.reshape(1, PROBES * XP, 256), (16, PROBES * XP, 256))
-    mixed = lax.all_to_all(mixed, GY, 0, 0, tiled=True)
-    return gather(counts, kt, mixed, ky_wide, cells, fractions)
+    mixed = jnp.broadcast_to(mixed.reshape(1, 4, 2 * XP, 256), (4, 4, 2 * XP, 256))
+    mixed = lax.all_to_all(mixed.reshape(16, 2 * XP, 256), GY, 0, 0, tiled=True)
+    smooth = lax.all_to_all(mix_y(place, kt, mixed, ky_pieces), "y", 0, 0, tiled=True)
+    return gather(counts, smooth, cells, fractions)
 
 
 def solution(mesh):

time: 173 us -> 163 us (0.942)
  the two profiles are of different devices: /device:TPU:128 before, /device:TPU:1 now
where the time goes in v2:
time: 163 us; the launch traced here: 160 us
  starting transfers between devices  65.3 us (40%)
  blocking collectives  40.4 us (25%)
  Pallas kernels  28 us (17%)
  waiting for transfers between devices  20 us (12%)
  local copies, waits for them, and re-layouts  3.85 us (2%)
  other arithmetic  1.65 us (1%)
    ppermute x6, starting transfers between devices, turns(): lax.ppermute(piece, axis, [(i, (i + shift) % 4) for i in range(4)])  21.8 us
    all_to_all x1, blocking collectives, body(): mixed = lax.all_to_all(mixed.reshape(16, 2 * XP, 256), GY, 0, 0, tiled=True)  20.5 us
    all_to_all x1, starting transfers between devices, body(): grid = lax.all_to_all(grid, GX, 0, 0, tiled=True)  12.6 us
    all_to_all x1, blocking collectives, body(): lax.all_to_all(mix_y(place, kt, mixed, ky_pieces), 'y', 0, 0, tiled=True)  10 us
    ppermute x2, starting transfers between devices, around(): after = lax.ppermute(kernel[0:2], axis, down(count))  10 us
    pallas_call x1, Pallas kernels, scatter(): pl.pallas_call(scatter_kernel, out_shape=(jax.ShapeDtypeStruct((rows, 256...  9.92 us
    all_to_all x1, blocking collectives, body(): mixed = lax.all_to_all(mixed, NEAR, 0, 0, tiled=True)  9.85 us
    pallas_call x1, Pallas kernels, gather(): pl.pallas_call(gather_kernel, out_shape=jax.ShapeDtypeStruct((PROBES, cel...  8.97 us
  transfers between devices with their start and end apart: 16, of which 8 were waited for; matrix products, arithmetic and copies ran while one was open for 1% of the time, Pallas kernels for 8%

profile of v2, /device:TPU:1, one launch (start us, length us, event | category | flops | bytes accessed | tf_op | source)
XLA Modules:
  0.0 160.1 jit_solution(8526495232957566689)
XLA Ops:
  0.7 8.7 %collective-permute-start.1 = (bf16[2,1024]{1,0:T(2,128)(2,1)S(1)}, bf16[2,1024]{1,0:T(2,128)(2,1)S(1)}, u32[]{:S(2)}, u32[]{:S(2)}) collective-permute-start(bf16[2,1024]{1,0:T(2,128)(2,1)S(1)} %slice.13), channel_id=1, source_target_pairs={{16,0},{32,16},{48,32},{64,48},{80,64},{96,80},{112,96},{128,112},... | collective-permute-start | bytes 12296 | tf_op jit(solution)/shard_map/ppermute | solution.py:302
  10.2 1.9 %collective-permute-start = (bf16[1,1024]{1,0:T(2,128)(2,1)S(1)}, bf16[1,1024]{1,0:T(2,128)(2,1)S(1)}, u32[]{:S(2)}, u32[]{:S(2)}) collective-permute-start(bf16[1,1024]{1,0:T(2,128)(2,1)S(1)} %slice.12), channel_id=1, source_target_pairs={{0,16},{16,32},{32,48},{48,64},{64,80},{80,96},{96,112},{112,128},... | collective-permute-start | bytes 6152 | tf_op jit(solution)/shard_map/ppermute | solution.py:301
  12.1 1.1 collective-permute-done
  14.2 2.1 %collective-permute-start.2 = (bf16[40,1024]{1,0:T(8,128)(2,1)S(1)}, bf16[40,1024]{1,0:T(8,128)(2,1)S(1)}, u32[]{:S(2)}, u32[]{:S(2)}) collective-permute-start(bf16[40,1024]{1,0:T(8,128)(2,1)S(1)} %pad_maximum_fusion), channel_id=1, source_target_pairs={{0,16},{16,0},{1,17},{17,1},{2,18},{18,2},{3,19},{19,3},{4,20},{20... | collective-permute-start | bytes 245768 | tf_op jit(solution)/shard_map/ppermute | solution.py:315
  16.3 1.1 collective-permute-done.2
  17.6 3.2 %collective-permute-start.7 = (bf16[80,1024]{1,0:T(8,128)(2,1)S(1)}, bf16[80,1024]{1,0:T(8,128)(2,1)S(1)}, u32[]{:S(2)}, u32[]{:S(2)}) collective-permute-start(bf16[80,1024]{1,0:T(8,128)(2,1)S(1)} %concatenate.11.k0_ref), channel_id=1, source_target_pairs={{0,96},{32,0},{64,32},{96,64},{1,97},{33,1},{65,33},{97,65},{2,98}... | collective-permute-start | bytes 491528 | tf_op jit(solution)/shard_map/ppermute | solution.py:309
  20.8 3.4 %collective-permute-start.6 = (bf16[80,1024]{1,0:T(8,128)(2,1)S(1)}, bf16[80,1024]{1,0:T(8,128)(2,1)S(1)}, u32[]{:S(2)}, u32[]{:S(2)}) collective-permute-start(bf16[80,1024]{1,0:T(8,128)(2,1)S(1)} %concatenate.11.k0_ref), channel_id=1, source_target_pairs={{0,64},{32,96},{64,0},{96,32},{1,65},{33,97},{65,1},{97,33},{2,66}... | collective-permute-start | bytes 491528 | tf_op jit(solution)/shard_map/ppermute | solution.py:309
  24.2 1.9 %collective-permute-start.5 = (bf16[80,1024]{1,0:T(8,128)(2,1)S(1)}, bf16[80,1024]{1,0:T(8,128)(2,1)S(1)}, u32[]{:S(2)}, u32[]{:S(2)}) collective-permute-start(bf16[80,1024]{1,0:T(8,128)(2,1)S(1)} %concatenate.11.k0_ref), channel_id=1, source_target_pairs={{0,32},{32,64},{64,96},{96,0},{1,33},{33,65},{65,97},{97,1},{2,34}... | collective-permute-start | bytes 491528 | tf_op jit(solution)/shard_map/ppermute | solution.py:309
  26.8 9.9 %scatter.1 = (f32[320,256]{1,0:T(8,128)}, f32[8,320]{1,0:T(8,128)}, f32[8,320]{1,0:T(8,128)}) custom-call(s32[1,1]{1,0:T(1,128)S(6)} %copy.8.count_ref, bf16[8,8192]{1,0:T(8,128)(2,1)} %probes_ref, s32[3,8192]{1,0:T(4,128)} %cells_ref.3, f32[3,8192]{1,0:T(4,128)} %fractions_ref.3), custom_call_target="tpu_custom_call" | custom-call | tf_op jit(solution)/shard_map/scatter/pallas_call | solution.py:110
  36.7 1.3 collective-permute-start.3
  38.0 4.0 %collective-permute-start.4 = (f32[8,320]{1,0:T(8,128)}, f32[8,320]{1,0:T(8,128)S(1)}, u32[]{:S(2)}, u32[]{:S(2)}) collective-permute-start(f32[8,320]{1,0:T(8,128)} %get-tuple-element.30), channel_id=1, source_target_pairs={{0,1},{1,2},{2,3},{3,4},{4,5},{5,6},{6,7},{7,8},{8,9},{9,10},{10,1... | collective-permute-start | bytes 30728 | tf_op jit(solution)/shard_map/ppermute | solution.py:322
  42.1 1.0 collective-permute-done.4.high_ref
  43.7 2.2 %add_cols.1 = (f32[320,256]{1,0:T(8,128)}, f32[8,256]{1,0:T(8,128)}, f32[16,256]{1,0:T(8,128)}) custom-call(f32[320,256]{1,0:T(8,128)} %get-tuple-element.28.core_ref, f32[8,320]{1,0:T(8,128)} %copy-done.12, f32[8,320]{1,0:T(8,128)} %copy-done.13), custom_call_target="tpu_custom_call" | custom-call | tf_op jit(solution)/shard_map/add_cols/pallas_call | solution.py:151
  45.9 5.1 %collective-permute-start.9 = (f32[16,256]{1,0:T(8,128)}, f32[16,256]{1,0:T(8,128)S(1)}, u32[]{:S(2)}, u32[]{:S(2)}) collective-permute-start(f32[16,256]{1,0:T(8,128)} %get-tuple-element.36), channel_id=1, source_target_pairs={{0,16},{16,32},{32,48},{48,64},{64,80},{80,96},{96,112},{112,128},... | collective-permute-start | bytes 49160 | tf_op jit(solution)/shard_map/ppermute | solution.py:326
  51.0 1.9 %collective-permute-start.8 = (f32[8,256]{1,0:T(8,128)}, f32[8,256]{1,0:T(8,128)S(1)}, u32[]{:S(2)}, u32[]{:S(2)}) collective-permute-start(f32[8,256]{1,0:T(8,128)} %get-tuple-element.35), channel_id=1, source_target_pairs={{16,0},{32,16},{48,32},{64,48},{80,64},{96,80},{112,96},{128,112},... | collective-permute-start | bytes 24584 | tf_op jit(solution)/shard_map/ppermute | solution.py:325
  52.9 3.3 %collective-permute-done.8.first_ref = f32[8,256]{1,0:T(8,128)S(1)} collective-permute-done((f32[8,256]{1,0:T(8,128)}, f32[8,256]{1,0:T(8,128)S(1)}, u32[]{:S(2)}, u32[]{:S(2)}) %collective-permute-start.8) | collective-permute-done | bytes 8224 | tf_op jit(solution)/shard_map/ppermute | solution.py:325
  56.8 1.9 %add_rows.1 = bf16[32,32,256]{2,1,0:T(8,128)(2,1)} custom-call(f32[320,256]{1,0:T(8,128)} %get-tuple-element.31.core_ref, f32[8,256]{1,0:T(8,128)} %copy-done.14, f32[16,256]{1,0:T(8,128)} %copy-done.11), custom_call_target="tpu_custom_call" | custom-call | tf_op jit(solution)/shard_map/add_rows/pallas_call | solution.py:175
  58.7 12.6 %all-to-all-start = ((bf16[32,32,256]{2,1,0:T(8,128)(2,1)}), bf16[32,32,256]{2,1,0:T(8,128)(2,1)S(1)}, u32[]{:S(2)}, u32[]{:S(2)}) async-start(bf16[32,32,256]{2,1,0:T(8,128)(2,1)} %add_rows.1), calls=%async_computation | async-start | bytes 1048576 | tf_op jit(solution)/shard_map/all_to_all | solution.py:329
  71.3 1.3 collective-permute-start.11
  72.7 4.5 %collective-permute-start.10 = (bf16[1,1024]{1,0:T(2,128)(2,1)S(1)}, bf16[1,1024]{1,0:T(2,128)(2,1)S(1)}, u32[]{:S(2)}, u32[]{:S(2)}) collective-permute-start(bf16[1,1024]{1,0:T(2,128)(2,1)S(1)} %slice.14), channel_id=1, source_target_pairs={{0,1},{1,2},{2,3},{3,4},{4,5},{5,6},{6,7},{7,8},{8,9},{9,10},{10,1... | collective-permute-start | bytes 6152 | tf_op jit(solution)/shard_map/ppermute | solution.py:301
  78.1 8.9 %collective-permute-start.14 = (bf16[80,1024]{1,0:T(8,128)(2,1)S(1)}, bf16[80,1024]{1,0:T(8,128)(2,1)S(1)}, u32[]{:S(2)}, u32[]{:S(2)}) collective-permute-start(bf16[80,1024]{1,0:T(8,128)(2,1)S(1)} %maximum_maximum_fusion.k0_ref), channel_id=1, source_target_pairs={{0,3},{1,0},{2,1},{3,2},{4,7},{5,4},{6,5},{7,6},{8,11},{9,8},{10,9... | collective-permute-start | bytes 491528 | tf_op jit(solution)/shard_map/ppermute | solution.py:309
  86.9 1.9 %collective-permute-start.13 = (bf16[80,1024]{1,0:T(8,128)(2,1)S(1)}, bf16[80,1024]{1,0:T(8,128)(2,1)S(1)}, u32[]{:S(2)}, u32[]{:S(2)}) collective-permute-start(bf16[80,1024]{1,0:T(8,128)(2,1)S(1)} %maximum_maximum_fusion.k0_ref), channel_id=1, source_target_pairs={{0,2},{1,3},{2,0},{3,1},{4,6},{5,7},{6,4},{7,5},{8,10},{9,11},{10,... | collective-permute-start | bytes 491528 | tf_op jit(solution)/shard_map/ppermute | solution.py:309
  88.8 2.5 %collective-permute-start.12 = (bf16[80,1024]{1,0:T(8,128)(2,1)S(1)}, bf16[80,1024]{1,0:T(8,128)(2,1)S(1)}, u32[]{:S(2)}, u32[]{:S(2)}) collective-permute-start(bf16[80,1024]{1,0:T(8,128)(2,1)S(1)} %maximum_maximum_fusion.k0_ref), channel_id=1, source_target_pairs={{0,1},{1,2},{2,3},{3,0},{4,5},{5,6},{6,7},{7,4},{8,9},{9,10},{10,1... | collective-permute-start | bytes 491528 | tf_op jit(solution)/shard_map/ppermute | solution.py:309
  92.0 2.8 %collective-permute-done.13.k2_ref = bf16[80,1024]{1,0:T(8,128)(2,1)S(1)} collective-permute-done((bf16[80,1024]{1,0:T(8,128)(2,1)S(1)}, bf16[80,1024]{1,0:T(8,128)(2,1)S(1)}, u32[]{:S(2)}, u32[]{:S(2)}) %collective-permute-start.13) | collective-permute-done | bytes 163872 | tf_op jit(solution)/shard_map/ppermute | solution.py:309
  94.8 4.4 %collective-permute-done.12.k1_ref = bf16[80,1024]{1,0:T(8,128)(2,1)S(1)} collective-permute-done((bf16[80,1024]{1,0:T(8,128)(2,1)S(1)}, bf16[80,1024]{1,0:T(8,128)(2,1)S(1)}, u32[]{:S(2)}, u32[]{:S(2)}) %collective-permute-start.12) | collective-permute-done | bytes 163872 | tf_op jit(solution)/shard_map/ppermute | solution.py:309
  99.2 5.6 %all-to-all-done = bf16[32,32,256]{2,1,0:T(8,128)(2,1)S(1)} async-done(((bf16[32,32,256]{2,1,0:T(8,128)(2,1)}), bf16[32,32,256]{2,1,0:T(8,128)(2,1)S(1)}, u32[]{:S(2)}, u32[]{:S(2)}) %all-to-all-start) | async-done | bytes 524320 | tf_op jit(solution)/shard_map/all_to_all | solution.py:329
  105.7 2.3 %mix_x.1 = bf16[8,40,256]{2,1,0:T(8,128)(2,1)} custom-call(s32[3]{0:T(128)} %pad_add_fusion.place_ref, bf16[1024,256]{1,0:T(8,128)(2,1)} %bitcast.7, bf16[80,1024]{1,0:T(8,128)(2,1)} %copy-done.1, bf16[80,1024]{1,0:T(8,128)(2,1)} %copy-done.6, bf16[80,1024]{1,0:T(8,128)(2,1)} %copy-done.5, bf16[80,1024]{1,0:T(8,128)(2,1)} %copy-done.4), custom_call_target="tpu_custom_call" | custom-call | tf_op jit(solution)/shard_map/mix_x/pallas_call | solution.py:195
  108.0 9.9 %all_to_all.20 = bf16[8,40,256]{2,1,0:T(8,128)(2,1)S(1)} all-to-all(bf16[8,40,256]{2,1,0:T(8,128)(2,1)} %mix_x.1), channel_id=1, replica_groups=mesh['zh'=4,'zl'=4,'c'=2,'x'=4,'y'=4] {'zl','c'}, dimensions={0} | all-to-all | bytes 327680 | tf_op jit(solution)/shard_map/all_to_all | solution.py:335
  117.9 20.5 %all_to_all.21.mixed_ref = bf16[16,80,256]{2,1,0:T(8,128)(2,1)} all-to-all(bf16[16,80,256]{2,1,0:T(8,128)(2,1)S(1)} %bitcast.6), channel_id=1, replica_groups=mesh['zh'=4,'zl'=4,'c'=2,'x'=4,'y'=4] {'x','y'}, dimensions={0} | all-to-all | bytes 1310720 | tf_op jit(solution)/shard_map/all_to_all | solution.py:337
  138.3 2.8 %mix_y.1 = bf16[4,320,128]{2,1,0:T(8,128)(2,1)} custom-call(s32[3]{0:T(128)} %pad_add_fusion.place_ref, f32[4,4]{1,0:T(4,128)} %kt_ref.1, bf16[16,80,256]{2,1,0:T(8,128)(2,1)} %all_to_all.21.mixed_ref, bf16[80,1024]{1,0:T(8,128)(2,1)} %copy-done.2, bf16[80,1024]{1,0:T(8,128)(2,1)} %copy-done.9, bf16[80,1024]{1,0:T(8,128)(2,1)} %copy-done.8, ...), custom_call_target="tpu_custom_call" | custom-call | tf_op jit(solution)/shard_map/mix_y/pallas_call | solution.py:238
  141.1 10.0 %all_to_all.22.smooth_ref = bf16[4,320,128]{2,1,0:T(8,128)(2,1)} all-to-all(bf16[4,320,128]{2,1,0:T(8,128)(2,1)} %mix_y.1), channel_id=1, replica_groups=mesh['zh'=4,'zl'=4,'c'=2,'x'=4,'y'=4] {'y'}, dimensions={0} | all-to-all | bytes 655360 | tf_op jit(solution)/shard_map/all_to_all | solution.py:338
  151.1 9.0 %gather.1 = bf16[8,8192]{1,0:T(8,128)(2,1)} custom-call(s32[1,1]{1,0:T(1,128)S(6)} %copy.8.count_ref, bf16[4,320,128]{2,1,0:T(8,128)(2,1)} %all_to_all.22.smooth_ref, s32[3,8192]{1,0:T(4,128)} %cells_ref.3, f32[3,8192]{1,0:T(4,128)} %fractions_ref.3), custom_call_target="tpu_custom_call" | custom-call | tf_op jit(solution)/shard_map/gather/pallas_call | solution.py:282
  (51 shorter events, 6.2 us)
Async XLA Ops:
  0.7 12.5 %collective-permute-start.1 = (bf16[2,1024]{1,0:T(2,128)(2,1)S(1)}, bf16[2,1024]{1,0:T(2,128)(2,1)S(1)}, u32[]{:S(2)}, u32[]{:S(2)}) collective-permute-start(bf16[2,1024]{1,0:T(2,128)(2,1)S(1)} %slice.13), channel_id=1, source_target_pairs={{16,0},{32,16},{48,32},{64,48},{80,64},{96,80},{112,96},{128,112},... | collective-permute-start | bytes 12296 | tf_op jit(solution)/shard_map/ppermute | solution.py:302
  10.2 3.0 %collective-permute-start = (bf16[1,1024]{1,0:T(2,128)(2,1)S(1)}, bf16[1,1024]{1,0:T(2,128)(2,1)S(1)}, u32[]{:S(2)}, u32[]{:S(2)}) collective-permute-start(bf16[1,1024]{1,0:T(2,128)(2,1)S(1)} %slice.12), channel_id=1, source_target_pairs={{0,16},{16,32},{32,48},{48,64},{64,80},{80,96},{96,112},{112,128},... | collective-permute-start | bytes 6152 | tf_op jit(solution)/shard_map/ppermute | solution.py:301
  13.2 4.1 %copy-start.3 = (bf16[32,1024]{1,0:T(8,128)(2,1)S(1)}, bf16[32,1024]{1,0:T(8,128)(2,1)}, u32[]{:S(2)}) copy-start(bf16[32,1024]{1,0:T(8,128)(2,1)} %param.11) | copy-start | bytes 196612
  14.2 3.2 %collective-permute-start.2 = (bf16[40,1024]{1,0:T(8,128)(2,1)S(1)}, bf16[40,1024]{1,0:T(8,128)(2,1)S(1)}, u32[]{:S(2)}, u32[]{:S(2)}) collective-permute-start(bf16[40,1024]{1,0:T(8,128)(2,1)S(1)} %pad_maximum_fusion), channel_id=1, source_target_pairs={{0,16},{16,0},{1,17},{17,1},{2,18},{18,2},{3,19},{19,3},{4,20},{20... | collective-permute-start | bytes 245768 | tf_op jit(solution)/shard_map/ppermute | solution.py:315
  17.6 19.2 %copy-start.1 = (bf16[80,1024]{1,0:T(8,128)(2,1)}, bf16[80,1024]{1,0:T(8,128)(2,1)S(1)}, u32[]{:S(2)}) copy-start(bf16[80,1024]{1,0:T(8,128)(2,1)S(1)} %concatenate.11.k0_ref) | copy-start | bytes 491524
  17.6 28.3 %collective-permute-start.7 = (bf16[80,1024]{1,0:T(8,128)(2,1)S(1)}, bf16[80,1024]{1,0:T(8,128)(2,1)S(1)}, u32[]{:S(2)}, u32[]{:S(2)}) collective-permute-start(bf16[80,1024]{1,0:T(8,128)(2,1)S(1)} %concatenate.11.k0_ref), channel_id=1, source_target_pairs={{0,96},{32,0},{64,32},{96,64},{1,97},{33,1},{65,33},{97,65},{2,98}... | collective-permute-start | bytes 491528 | tf_op jit(solution)/shard_map/ppermute | solution.py:309
  20.8 25.0 %collective-permute-start.6 = (bf16[80,1024]{1,0:T(8,128)(2,1)S(1)}, bf16[80,1024]{1,0:T(8,128)(2,1)S(1)}, u32[]{:S(2)}, u32[]{:S(2)}) collective-permute-start(bf16[80,1024]{1,0:T(8,128)(2,1)S(1)} %concatenate.11.k0_ref), channel_id=1, source_target_pairs={{0,64},{32,96},{64,0},{96,32},{1,65},{33,97},{65,1},{97,33},{2,66}... | collective-permute-start | bytes 491528 | tf_op jit(solution)/shard_map/ppermute | solution.py:309
  24.2 21.6 %collective-permute-start.5 = (bf16[80,1024]{1,0:T(8,128)(2,1)S(1)}, bf16[80,1024]{1,0:T(8,128)(2,1)S(1)}, u32[]{:S(2)}, u32[]{:S(2)}) collective-permute-start(bf16[80,1024]{1,0:T(8,128)(2,1)S(1)} %concatenate.11.k0_ref), channel_id=1, source_target_pairs={{0,32},{32,64},{64,96},{96,0},{1,33},{33,65},{65,97},{97,1},{2,34}... | collective-permute-start | bytes 491528 | tf_op jit(solution)/shard_map/ppermute | solution.py:309
  36.7 5.3 %collective-permute-start.3 = (f32[8,320]{1,0:T(8,128)}, f32[8,320]{1,0:T(8,128)S(1)}, u32[]{:S(2)}, u32[]{:S(2)}) collective-permute-start(f32[8,320]{1,0:T(8,128)} %get-tuple-element.29), channel_id=1, source_target_pairs={{1,0},{2,1},{3,2},{4,3},{5,4},{6,5},{7,6},{8,7},{9,8},{10,9},{11,1... | collective-permute-start | bytes 30728 | tf_op jit(solution)/shard_map/ppermute | solution.py:321
  38.0 5.0 %collective-permute-start.4 = (f32[8,320]{1,0:T(8,128)}, f32[8,320]{1,0:T(8,128)S(1)}, u32[]{:S(2)}, u32[]{:S(2)}) collective-permute-start(f32[8,320]{1,0:T(8,128)} %get-tuple-element.30), channel_id=1, source_target_pairs={{0,1},{1,2},{2,3},{3,4},{4,5},{5,6},{6,7},{7,8},{8,9},{9,10},{10,1... | collective-permute-start | bytes 30728 | tf_op jit(solution)/shard_map/ppermute | solution.py:322
  42.0 1.0 copy-start.12
  43.1 0.6 copy-start.13
  45.9 12.8 %copy-start.4 = (bf16[80,1024]{1,0:T(8,128)(2,1)}, bf16[80,1024]{1,0:T(8,128)(2,1)S(1)}, u32[]{:S(2)}) copy-start(bf16[80,1024]{1,0:T(8,128)(2,1)S(1)} %collective-permute-done.7.k3_ref) | copy-start | bytes 491524
  45.9 12.8 %copy-start.5 = (bf16[80,1024]{1,0:T(8,128)(2,1)}, bf16[80,1024]{1,0:T(8,128)(2,1)S(1)}, u32[]{:S(2)}) copy-start(bf16[80,1024]{1,0:T(8,128)(2,1)S(1)} %collective-permute-done.6.k2_ref) | copy-start | bytes 491524
  45.9 12.8 %copy-start.6 = (bf16[80,1024]{1,0:T(8,128)(2,1)}, bf16[80,1024]{1,0:T(8,128)(2,1)S(1)}, u32[]{:S(2)}) copy-start(bf16[80,1024]{1,0:T(8,128)(2,1)S(1)} %collective-permute-done.5.k1_ref) | copy-start | bytes 491524
  45.9 10.3 %collective-permute-start.9 = (f32[16,256]{1,0:T(8,128)}, f32[16,256]{1,0:T(8,128)S(1)}, u32[]{:S(2)}, u32[]{:S(2)}) collective-permute-start(f32[16,256]{1,0:T(8,128)} %get-tuple-element.36), channel_id=1, source_target_pairs={{0,16},{16,32},{32,48},{48,64},{64,80},{80,96},{96,112},{112,128},... | collective-permute-start | bytes 49160 | tf_op jit(solution)/shard_map/ppermute | solution.py:326
  51.0 5.2 %collective-permute-start.8 = (f32[8,256]{1,0:T(8,128)}, f32[8,256]{1,0:T(8,128)S(1)}, u32[]{:S(2)}, u32[]{:S(2)}) collective-permute-start(f32[8,256]{1,0:T(8,128)} %get-tuple-element.35), channel_id=1, source_target_pairs={{16,0},{32,16},{48,32},{64,48},{80,64},{96,80},{112,96},{128,112},... | collective-permute-start | bytes 24584 | tf_op jit(solution)/shard_map/ppermute | solution.py:325
  56.2 0.6 copy-start.14
  56.2 0.6 copy-start.11
  58.7 12.7 %copy-start.10 = (bf16[64,1024]{1,0:T(8,128)(2,1)S(1)}, bf16[64,1024]{1,0:T(8,128)(2,1)}, u32[]{:S(2)}) copy-start(bf16[64,1024]{1,0:T(8,128)(2,1)} %param.12) | copy-start | bytes 393220
  58.7 46.2 %all-to-all-start = ((bf16[32,32,256]{2,1,0:T(8,128)(2,1)}), bf16[32,32,256]{2,1,0:T(8,128)(2,1)S(1)}, u32[]{:S(2)}, u32[]{:S(2)}) async-start(bf16[32,32,256]{2,1,0:T(8,128)(2,1)} %add_rows.1), calls=%async_computation | async-start | bytes 1048576 | tf_op jit(solution)/shard_map/all_to_all | solution.py:329
  71.3 6.6 %collective-permute-start.11 = (bf16[2,1024]{1,0:T(2,128)(2,1)S(1)}, bf16[2,1024]{1,0:T(2,128)(2,1)S(1)}, u32[]{:S(2)}, u32[]{:S(2)}) collective-permute-start(bf16[2,1024]{1,0:T(2,128)(2,1)S(1)} %slice.15), channel_id=1, source_target_pairs={{1,0},{2,1},{3,2},{4,3},{5,4},{6,5},{7,6},{8,7},{9,8},{10,9},{11,1... | collective-permute-start | bytes 12296 | tf_op jit(solution)/shard_map/ppermute | solution.py:302
  72.7 5.3 %collective-permute-start.10 = (bf16[1,1024]{1,0:T(2,128)(2,1)S(1)}, bf16[1,1024]{1,0:T(2,128)(2,1)S(1)}, u32[]{:S(2)}, u32[]{:S(2)}) collective-permute-start(bf16[1,1024]{1,0:T(2,128)(2,1)S(1)} %slice.14), channel_id=1, source_target_pairs={{0,1},{1,2},{2,3},{3,4},{4,5},{5,6},{6,7},{7,8},{8,9},{9,10},{10,1... | collective-permute-start | bytes 6152 | tf_op jit(solution)/shard_map/ppermute | solution.py:301
  78.0 29.9 %copy-start.2 = (bf16[80,1024]{1,0:T(8,128)(2,1)}, bf16[80,1024]{1,0:T(8,128)(2,1)S(1)}, u32[]{:S(2)}) copy-start(bf16[80,1024]{1,0:T(8,128)(2,1)S(1)} %maximum_maximum_fusion.k0_ref) | copy-start | bytes 491524
  78.1 13.9 %collective-permute-start.14 = (bf16[80,1024]{1,0:T(8,128)(2,1)S(1)}, bf16[80,1024]{1,0:T(8,128)(2,1)S(1)}, u32[]{:S(2)}, u32[]{:S(2)}) collective-permute-start(bf16[80,1024]{1,0:T(8,128)(2,1)S(1)} %maximum_maximum_fusion.k0_ref), channel_id=1, source_target_pairs={{0,3},{1,0},{2,1},{3,2},{4,7},{5,4},{6,5},{7,6},{8,11},{9,8},{10,9... | collective-permute-start | bytes 491528 | tf_op jit(solution)/shard_map/ppermute | solution.py:309
  86.9 7.9 %collective-permute-start.13 = (bf16[80,1024]{1,0:T(8,128)(2,1)S(1)}, bf16[80,1024]{1,0:T(8,128)(2,1)S(1)}, u32[]{:S(2)}, u32[]{:S(2)}) collective-permute-start(bf16[80,1024]{1,0:T(8,128)(2,1)S(1)} %maximum_maximum_fusion.k0_ref), channel_id=1, source_target_pairs={{0,2},{1,3},{2,0},{3,1},{4,6},{5,7},{6,4},{7,5},{8,10},{9,11},{10,... | collective-permute-start | bytes 491528 | tf_op jit(solution)/shard_map/ppermute | solution.py:309
  88.8 10.4 %collective-permute-start.12 = (bf16[80,1024]{1,0:T(8,128)(2,1)S(1)}, bf16[80,1024]{1,0:T(8,128)(2,1)S(1)}, u32[]{:S(2)}, u32[]{:S(2)}) collective-permute-start(bf16[80,1024]{1,0:T(8,128)(2,1)S(1)} %maximum_maximum_fusion.k0_ref), channel_id=1, source_target_pairs={{0,1},{1,2},{2,3},{3,0},{4,5},{5,6},{6,7},{7,4},{8,9},{9,10},{10,1... | collective-permute-start | bytes 491528 | tf_op jit(solution)/shard_map/ppermute | solution.py:309
  92.0 16.0 %copy-start.7 = (bf16[80,1024]{1,0:T(8,128)(2,1)}, bf16[80,1024]{1,0:T(8,128)(2,1)S(1)}, u32[]{:S(2)}) copy-start(bf16[80,1024]{1,0:T(8,128)(2,1)S(1)} %collective-permute-done.14.k3_ref) | copy-start | bytes 491524
  94.8 13.2 %copy-start.8 = (bf16[80,1024]{1,0:T(8,128)(2,1)}, bf16[80,1024]{1,0:T(8,128)(2,1)S(1)}, u32[]{:S(2)}) copy-start(bf16[80,1024]{1,0:T(8,128)(2,1)S(1)} %collective-permute-done.13.k2_ref) | copy-start | bytes 491524
  99.2 8.8 %copy-start.9 = (bf16[80,1024]{1,0:T(8,128)(2,1)}, bf16[80,1024]{1,0:T(8,128)(2,1)S(1)}, u32[]{:S(2)}) copy-start(bf16[80,1024]{1,0:T(8,128)(2,1)S(1)} %collective-permute-done.12.k1_ref) | copy-start | bytes 491524
  104.8 0.8 copy-start

commit v3 on v2

--- a/solution.py
+++ b/solution.py
@@ -13,6 +13,7 @@
 COLS = 64
 XP = 40
 YP = 80
+RIM = 384
 CHUNK = 512
 AXES = ("zh", "zl", "c", "x", "y")
 GX = ("zh", "zl", "c")
@@ -58,7 +59,7 @@
 
 
 def scatter_kernel(
-    count_ref, probes_ref, cells_ref, fractions_ref, core_ref, low_ref, high_ref, acc_ref
+    count_ref, probes_ref, cells_ref, fractions_ref, ky_ref, core_ref, low_ref, high_ref, acc_ref
 ):
     points = probes_ref.shape[1]
     acc_ref[...] = jnp.zeros_like(acc_ref)
@@ -101,28 +102,34 @@
     rims = lax.dot_general(
         pick, total, (((1,), (1,)), ((), ())), precision=HIGH, preferred_element_type=jnp.float32
     )
-    low_ref[...] = rims[0:8]
-    high_ref[...] = rims[8:16]
-
-
-def scatter(counts, probes, cells, fractions):
+    top = ky_ref[0:16, :].astype(jnp.float32)
+    end = ky_ref[COLS - 16 : COLS, :].astype(jnp.float32)
+    low_ref[:, 0:rows] = rims[0:8]
+    high_ref[:, 0:rows] = rims[8:16]
+    for n in range(4):
+        here = slice(256 * n, 256 * n + 256)
+        for r in range(2):
+            low_ref[4 * r + n : 4 * r + n + 1, RIM:] = top[r : r + 1, here]
+        high_ref[n : n + 1, RIM:] = end[15:16, here]
+    high_ref[4:8, RIM:] = jnp.zeros((4, 256), jnp.float32)
+    low_ref[:, rows:RIM] = jnp.zeros((8, RIM - rows), jnp.float32)
+    high_ref[:, rows:RIM] = jnp.zeros((8, RIM - rows), jnp.float32)
+
+
+def scatter(counts, probes, cells, fractions, ky):
     rows = PROBES * XP
     return pl.pallas_call(
         scatter_kernel,
         out_shape=(
             jax.ShapeDtypeStruct((rows, 256), jnp.float32),
-            jax.ShapeDtypeStruct((8, rows), jnp.float32),
-            jax.ShapeDtypeStruct((8, rows), jnp.float32),
+            jax.ShapeDtypeStruct((8, RIM + 256), jnp.float32),
+            jax.ShapeDtypeStruct((8, RIM + 256), jnp.float32),
         ),
-        in_specs=[
-            pl.BlockSpec(memory_space=pltpu.SMEM),
-            pl.BlockSpec(memory_space=pltpu.VMEM),
-            pl.BlockSpec(memory_space=pltpu.VMEM),
-            pl.BlockSpec(memory_space=pltpu.VMEM),
-        ],
+        in_specs=[pl.BlockSpec(memory_space=pltpu.SMEM)]
+        + [pl.BlockSpec(memory_space=pltpu.VMEM)] * 4,
         scratch_shapes=[pltpu.VMEM((2 * rows, 256), jnp.float32)],
         name="scatter",
-    )(counts, probes, cells, fractions)
+    )(counts, probes, cells, fractions, ky)
 
 
 def add_cols_kernel(core_ref, low_ref, high_ref, out_ref, first_ref, last_ref):
@@ -131,7 +138,8 @@
     high_row = row - 8
     put = (row < DAYS) & (lane == COLS * row + (COLS - 1))
     put = put | ((high_row >= 0) & (lane == COLS * (high_row // 2) + high_row % 2))
-    received = jnp.concatenate([low_ref[...], high_ref[...]], axis=0)
+    width = core_ref.shape[0]
+    received = jnp.concatenate([low_ref[:, 0:width], high_ref[:, 0:width]], axis=0)
     out_ref[...] = core_ref[...] + lax.dot_general(
         received,
         jnp.where(put, 1.0, 0.0),
@@ -179,26 +187,27 @@
     )(core, first, last)
 
 
-def mix_x_kernel(place_ref, grid_ref, k0_ref, k1_ref, k2_ref, k3_ref, out_ref):
-    zl, core = place_ref[0], place_ref[1]
-    kernel = jnp.concatenate([k0_ref[...], k1_ref[...], k2_ref[...], k3_ref[...]], axis=0)
-    mixed = jnp.dot(kernel, grid_ref[...], preferred_element_type=jnp.float32)
-    for shift in range(4):
-        tile = 2 * ((zl + 4 - shift) % 4)
-        for half in range(2):
-            base = (2 * shift + half) * XP
-            part = mixed[base : base + XP].astype(jnp.bfloat16)
-            out_ref[tile + (core if half == 0 else 1 - core)] = part
-
-
-def mix_x(place, grid, pieces):
+def mix_x_kernel(grid_ref, kernel_ref, before_ref, after_ref, out_ref, rows_ref):
+    blank = jnp.zeros((5, 1024), jnp.float32)
+    outer = [after_ref[...].astype(jnp.float32), blank, before_ref[...].astype(jnp.float32)]
+    outer = jnp.concatenate(outer, axis=0).astype(jnp.bfloat16)
+    outer = jnp.dot(outer, grid_ref[...], preferred_element_type=jnp.float32)
+    rows_ref[0:8, :] = outer
+    rows_ref[264:272, :] = outer
+    rows_ref[8:264, :] = jnp.dot(
+        kernel_ref[...], grid_ref[...], preferred_element_type=jnp.float32
+    )
+    for tile in range(8):
+        out_ref[tile] = rows_ref[7 + ROWS * tile : 7 + ROWS * tile + XP, :].astype(jnp.bfloat16)
+
+
+def mix_x(grid, kernel, before, after):
     return pl.pallas_call(
         mix_x_kernel,
         out_shape=jax.ShapeDtypeStruct((8, XP, 256), jnp.bfloat16),
-        in_specs=[pl.BlockSpec(memory_space=pltpu.SMEM)]
-        + [pl.BlockSpec(memory_space=pltpu.VMEM)] * 5,
+        scratch_shapes=[pltpu.VMEM((272, 256), jnp.float32)],
         name="mix_x",
-    )(place, grid, *pieces)
+    )(grid, kernel, before, after)
 
 
 def mix_y_kernel(place_ref, kt_ref, mixed_ref, k0_ref, k1_ref, k2_ref, k3_ref, out_ref):
@@ -230,7 +239,7 @@
             smooth.append(total)
         smooth = jnp.concatenate(smooth, axis=0).astype(jnp.bfloat16)
         for which in range(2):
-            target = (place_ref[2] + 4 - (2 * half + which)) % 4
+            target = (place_ref[0] + 4 - (2 * half + which)) % 4
             out_ref[target] = smooth[:, 128 * which : 128 * which + 128]
 
 
@@ -297,13 +306,6 @@
     return [(i + 1, i) for i in range(count - 1)]
 
 
-def around(kernel, axis, count, rows):
-    before = lax.ppermute(kernel[-1:], axis, up(count))
-    after = lax.ppermute(kernel[0:2], axis, down(count))
-    blank = jnp.zeros((rows - 3 - kernel.shape[0], kernel.shape[1]), kernel.dtype)
-    return jnp.concatenate([before, kernel, after, blank], axis=0)
-
-
 def turns(piece, axis):
     return [piece] + [
         lax.ppermute(piece, axis, [(i, (i + shift) % 4) for i in range(4)]) for shift in (1, 2, 3)
@@ -311,27 +313,28 @@
 
 
 def body(probes, cells, fractions, counts, kx, ky, kt):
-    own = around(kx, GX, 32, XP)
-    other = lax.ppermute(own, "c", [(0, 1), (1, 0)])
-    pair = jnp.concatenate([own, other], axis=0)
-    pair, probes = lax.optimization_barrier((pair, probes))
-    kx_pieces = turns(pair, "zl")
-
-    core, low, high = scatter(counts, probes, cells, fractions)
+    kernel = jnp.broadcast_to(kx[None], (8,) + kx.shape)
+    kernel = lax.all_to_all(kernel, NEAR, 0, 0, tiled=True).reshape(8 * ROWS, 1024)
+    core, low, high = scatter(counts, probes, cells, fractions, ky)
+    low, kernel = lax.optimization_barrier((low, kernel))
     low = lax.ppermute(low, GY, down(16))
     high = lax.ppermute(high, GY, up(16))
     core, first, last = add_cols(core, low, high)
-    first, last, kx_pieces = lax.optimization_barrier((first, last, kx_pieces))
     first = lax.ppermute(first, GX, down(32))
     last = lax.ppermute(last, GX, up(32))
     grid = add_rows(core, first, last)
-    grid, ky = lax.optimization_barrier((grid, ky))
+    grid, ky, kernel = lax.optimization_barrier((grid, ky, kernel))
     grid = lax.all_to_all(grid, GX, 0, 0, tiled=True)
-    ky_pieces = turns(around(ky, GY, 16, YP), "y")
-    place = [lax.axis_index(axis) for axis in ("zl", "c", "y")]
-    place = jnp.stack(place).astype(jnp.int32)
-    grid, ky_pieces, place = lax.optimization_barrier((grid, ky_pieces, place))
-    mixed = mix_x(place, grid.reshape(32 * ROWS, 256), kx_pieces)
+    before = lax.ppermute(kernel[8 * ROWS - 1 :], "zh", up(4))
+    after = lax.ppermute(kernel[0:2], "zh", down(4))
+    right = low[:, RIM:].reshape(2, 1024).astype(ky.dtype)
+    left = high[0:4, RIM:].reshape(1, 1024).astype(ky.dtype)
+    blank = jnp.zeros((YP - COLS - 3, 1024), ky.dtype)
+    ky_pieces = turns(jnp.concatenate([left, ky, right, blank], axis=0), "y")
+    place = lax.axis_index("y").astype(jnp.int32).reshape(1)
+    rest = (grid, ky_pieces, place, before, after)
+    grid, ky_pieces, place, before, after = lax.optimization_barrier(rest)
+    mixed = mix_x(grid.reshape(32 * ROWS, 256), kernel, before, after)
     mixed = lax.all_to_all(mixed, NEAR, 0, 0, tiled=True)
     mixed = jnp.broadcast_to(mixed.reshape(1, 4, 2 * XP, 256), (4, 4, 2 * XP, 256))
     mixed = lax.all_to_all(mixed.reshape(16, 2 * XP, 256), GY, 0, 0, tiled=True)

time: 163 us -> 148 us (0.908)
  starting transfers between devices: 65.3 us -> 51.5 us
    ppermute x6 -> x3, starting transfers between devices: 21.8 us -> 11.2 us  [turns(): lax.ppermute(piece, axis, [(i, (i + shift) % 4) for i in range(4)])]
    all_to_all x0 -> x1, starting transfers between devices: none -> 10.2 us  [body(): lax.all_to_all(kernel, NEAR, 0, 0, tiled=True).reshape(8 * ROWS, 1024)]
    ppermute x5 -> x2, starting transfers between devices: 18.6 us -> 9.19 us  [the longest x1 7.89 us: body(): before = lax.ppermute(kernel[8 * ROWS - 1:], 'zh', up(4))]
    ppermute x6 -> x3, waiting for transfers between devices: 7.24 us -> 0.01 us  [turns(): lax.ppermute(piece, axis, [(i, (i + shift) % 4) for i in range(4)])]
    all_to_all x1, waiting for transfers between devices: 5.64 us -> 10.6 us  [body(): grid = lax.all_to_all(grid, GX, 0, 0, tiled=True)]
    ppermute x1, waiting for transfers between devices: 0.01 us -> 3.42 us  [body(): low = lax.ppermute(low, GY, down(16))]
    ppermute x1, starting transfers between devices: 3.99 us -> 1.28 us  [body(): high = lax.ppermute(high, GY, up(16))]
    ppermute x1, starting transfers between devices: 5.07 us -> 2.43 us  [body(): last = lax.ppermute(last, GX, up(32))]
  transfers between devices with their start and end apart: 16 -> 11, of which waited for: 8 -> 6; matrix products, arithmetic and copies ran while one was open for 1% -> 1% of each run, Pallas kernels for 8% -> 7%
where the time goes in v3:
time: 148 us; the launch traced here: 145 us
  starting transfers between devices  51.5 us (35%)
  blocking collectives  39.7 us (27%)
  Pallas kernels  28 us (19%)
  waiting for transfers between devices  19.6 us (13%)
  local copies, waits for them, and re-layouts  5.31 us (4%)
    all_to_all x1, blocking collectives, body(): mixed = lax.all_to_all(mixed.reshape(16, 2 * XP, 256), GY, 0, 0, tiled=True)  19.7 us
    all_to_all x1, starting transfers between devices, body(): grid = lax.all_to_all(grid, GX, 0, 0, tiled=True)  13.1 us
    ppermute x3, starting transfers between devices, turns(): lax.ppermute(piece, axis, [(i, (i + shift) % 4) for i in range(4)])  11.2 us
    all_to_all x1, waiting for transfers between devices, body(): grid = lax.all_to_all(grid, GX, 0, 0, tiled=True)  10.6 us
    all_to_all x1, starting transfers between devices, body(): lax.all_to_all(kernel, NEAR, 0, 0, tiled=True).reshape(8 * ROWS, 1024)  10.2 us
    all_to_all x1, blocking collectives, body(): lax.all_to_all(mix_y(place, kt, mixed, ky_pieces), 'y', 0, 0, tiled=True)  10 us
    all_to_all x1, blocking collectives, body(): mixed = lax.all_to_all(mixed, NEAR, 0, 0, tiled=True)  10 us
    pallas_call x1, Pallas kernels, scatter(): pl.pallas_call(scatter_kernel, out_shape=(jax.ShapeDtypeStruct((rows, 256...  9.99 us
  transfers between devices with their start and end apart: 11, of which 6 were waited for; matrix products, arithmetic and copies ran while one was open for 1% of the time, Pallas kernels for 7%

profile of v3, /device:TPU:1, one launch (start us, length us, event | category | flops | bytes accessed | tf_op | source)
XLA Modules:
  0.0 145.2 jit_solution(15096449653789421191)
XLA Ops:
  0.0 1.7 %broadcast_in_dim.16 = bf16[8,32,1024]{2,1,0:T(8,128)(2,1)} broadcast(bf16[32,1024]{1,0:T(8,128)(2,1)} %param.11), dimensions={1,2} | broadcast | bytes 589824 | tf_op jit(solution)/shard_map/broadcast_in_dim | solution.py:316
  1.7 10.2 %all-to-all-start = ((bf16[8,32,1024]{2,1,0:T(8,128)(2,1)}), bf16[8,32,1024]{2,1,0:T(8,128)(2,1)S(1)}, u32[]{:S(2)}, u32[]{:S(2)}) async-start(bf16[8,32,1024]{2,1,0:T(8,128)(2,1)} %broadcast_in_dim.16), calls=%async_computation | async-start | bytes 1048576 | tf_op jit(solution)/shard_map/all_to_all | solution.py:317
  12.6 10.0 %scatter.1 = (f32[320,256]{1,0:T(8,128)}, f32[8,640]{1,0:T(8,128)}, f32[8,640]{1,0:T(8,128)}) custom-call(s32[1,1]{1,0:T(1,128)S(6)} %copy.9.count_ref, bf16[8,8192]{1,0:T(8,128)(2,1)} %probes_ref.1, s32[3,8192]{1,0:T(4,128)} %cells_ref.3, f32[3,8192]{1,0:T(4,128)} %fractions_ref.3, bf16[64,1024]{1,0:T(8,128)(2,1)} %ky_ref.1), custom_call_target="tpu_custom_call" | custom-call | tf_op jit(solution)/shard_map/scatter/pallas_call | solution.py:121
  22.6 1.3 collective-permute-start.1
  23.9 2.5 %all-to-all-done = bf16[8,32,1024]{2,1,0:T(8,128)(2,1)S(1)} async-done(((bf16[8,32,1024]{2,1,0:T(8,128)(2,1)}), bf16[8,32,1024]{2,1,0:T(8,128)(2,1)S(1)}, u32[]{:S(2)}, u32[]{:S(2)}) %all-to-all-start) | async-done | bytes 524320 | tf_op jit(solution)/shard_map/all_to_all | solution.py:317
  26.3 1.3 collective-permute-start
  27.6 3.4 %collective-permute-done.low_ref = f32[8,640]{1,0:T(8,128)S(1)} collective-permute-done((f32[8,640]{1,0:T(8,128)}, f32[8,640]{1,0:T(8,128)S(1)}, u32[]{:S(2)}, u32[]{:S(2)}) %collective-permute-start) | collective-permute-done | bytes 20512 | tf_op jit(solution)/shard_map/ppermute | solution.py:320
  31.1 0.6 copy-done.7
  31.7 2.2 %add_cols.1 = (f32[320,256]{1,0:T(8,128)}, f32[8,256]{1,0:T(8,128)}, f32[16,256]{1,0:T(8,128)}) custom-call(f32[320,256]{1,0:T(8,128)} %get-tuple-element.24.core_ref, f32[8,640]{1,0:T(8,128)} %copy-done.7, f32[8,640]{1,0:T(8,128)} %copy-done.8), custom_call_target="tpu_custom_call" | custom-call | tf_op jit(solution)/shard_map/add_cols/pallas_call | solution.py:159
  33.9 2.4 %collective-permute-start.3 = (f32[16,256]{1,0:T(8,128)}, f32[16,256]{1,0:T(8,128)S(1)}, u32[]{:S(2)}, u32[]{:S(2)}) collective-permute-start(f32[16,256]{1,0:T(8,128)} %get-tuple-element.30), channel_id=1, source_target_pairs={{0,16},{16,32},{32,48},{48,64},{64,80},{80,96},{96,112},{112,128},... | collective-permute-start | bytes 49160 | tf_op jit(solution)/shard_map/ppermute | solution.py:324
  36.3 2.9 %collective-permute-start.2 = (f32[8,256]{1,0:T(8,128)}, f32[8,256]{1,0:T(8,128)S(1)}, u32[]{:S(2)}, u32[]{:S(2)}) collective-permute-start(f32[8,256]{1,0:T(8,128)} %get-tuple-element.29), channel_id=1, source_target_pairs={{16,0},{32,16},{48,32},{64,48},{80,64},{96,80},{112,96},{128,112},... | collective-permute-start | bytes 24584 | tf_op jit(solution)/shard_map/ppermute | solution.py:323
  39.2 2.3 %collective-permute-done.2.first_ref = f32[8,256]{1,0:T(8,128)S(1)} collective-permute-done((f32[8,256]{1,0:T(8,128)}, f32[8,256]{1,0:T(8,128)S(1)}, u32[]{:S(2)}, u32[]{:S(2)}) %collective-permute-start.2) | collective-permute-done | bytes 8224 | tf_op jit(solution)/shard_map/ppermute | solution.py:323
  41.5 0.6 copy-done.10
  42.1 1.9 %add_rows.1 = bf16[32,32,256]{2,1,0:T(8,128)(2,1)} custom-call(f32[320,256]{1,0:T(8,128)} %get-tuple-element.28.core_ref, f32[8,256]{1,0:T(8,128)} %copy-done.10, f32[16,256]{1,0:T(8,128)} %copy-done.9), custom_call_target="tpu_custom_call" | custom-call | tf_op jit(solution)/shard_map/add_rows/pallas_call | solution.py:183
  44.0 13.1 %all-to-all-start.1 = ((bf16[32,32,256]{2,1,0:T(8,128)(2,1)}), bf16[32,32,256]{2,1,0:T(8,128)(2,1)S(1)}, u32[]{:S(2)}, u32[]{:S(2)}) async-start(bf16[32,32,256]{2,1,0:T(8,128)(2,1)} %add_rows.1), calls=%async_computation.1 | async-start | bytes 1048576 | tf_op jit(solution)/shard_map/all_to_all | solution.py:327
  57.2 0.7 fusion
  57.9 0.7 slice.24
  58.7 6.8 %collective-permute-start.6 = (bf16[80,1024]{1,0:T(8,128)(2,1)S(1)}, bf16[80,1024]{1,0:T(8,128)(2,1)S(1)}, u32[]{:S(2)}, u32[]{:S(2)}) collective-permute-start(bf16[80,1024]{1,0:T(8,128)(2,1)S(1)} %maximum_maximum_fusion.k0_ref), channel_id=1, source_target_pairs={{0,3},{1,0},{2,1},{3,2},{4,7},{5,4},{6,5},{7,6},{8,11},{9,8},{10,9... | collective-permute-start | bytes 491528 | tf_op jit(solution)/shard_map/ppermute | solution.py:311
  65.5 1.9 %collective-permute-start.5 = (bf16[80,1024]{1,0:T(8,128)(2,1)S(1)}, bf16[80,1024]{1,0:T(8,128)(2,1)S(1)}, u32[]{:S(2)}, u32[]{:S(2)}) collective-permute-start(bf16[80,1024]{1,0:T(8,128)(2,1)S(1)} %maximum_maximum_fusion.k0_ref), channel_id=1, source_target_pairs={{0,2},{1,3},{2,0},{3,1},{4,6},{5,7},{6,4},{7,5},{8,10},{9,11},{10,... | collective-permute-start | bytes 491528 | tf_op jit(solution)/shard_map/ppermute | solution.py:311
  67.4 2.5 %collective-permute-start.4 = (bf16[80,1024]{1,0:T(8,128)(2,1)S(1)}, bf16[80,1024]{1,0:T(8,128)(2,1)S(1)}, u32[]{:S(2)}, u32[]{:S(2)}) collective-permute-start(bf16[80,1024]{1,0:T(8,128)(2,1)S(1)} %maximum_maximum_fusion.k0_ref), channel_id=1, source_target_pairs={{0,1},{1,2},{2,3},{3,0},{4,5},{5,6},{6,7},{7,4},{8,9},{9,10},{10,1... | collective-permute-start | bytes 491528 | tf_op jit(solution)/shard_map/ppermute | solution.py:311
  69.9 1.3 collective-permute-start.8
  71.2 7.9 %collective-permute-start.7 = (bf16[1,1024]{1,0:T(2,128)(2,1)S(1)}, bf16[1,1024]{1,0:T(2,128)(2,1)S(1)}, u32[]{:S(2)}, u32[]{:S(2)}) collective-permute-start(bf16[1,1024]{1,0:T(2,128)(2,1)S(1)} %slice.16), channel_id=1, source_target_pairs={{0,128},{128,256},{256,384},{1,129},{129,257},{257,385},{2,130},{1... | collective-permute-start | bytes 6152 | tf_op jit(solution)/shard_map/ppermute | solution.py:328
  79.1 0.7 collective-permute-done.7.before_ref
  79.9 0.1 collective-permute-done.8.after_ref
  80.0 10.6 %all-to-all-done.1 = bf16[32,32,256]{2,1,0:T(8,128)(2,1)S(1)} async-done(((bf16[32,32,256]{2,1,0:T(8,128)(2,1)}), bf16[32,32,256]{2,1,0:T(8,128)(2,1)S(1)}, u32[]{:S(2)}, u32[]{:S(2)}) %all-to-all-start.1) | async-done | bytes 524320 | tf_op jit(solution)/shard_map/all_to_all | solution.py:327
  90.6 0.8 copy-done.1
  91.4 2.3 %mix_x.1 = bf16[8,40,256]{2,1,0:T(8,128)(2,1)} custom-call(bf16[1024,256]{1,0:T(8,128)(2,1)} %bitcast.13, bf16[256,1024]{1,0:T(8,128)(2,1)} %bitcast.12, bf16[1,1024]{1,0:T(2,128)(2,1)} %copy-done.12, bf16[2,1024]{1,0:T(2,128)(2,1)} %copy-done.11), custom_call_target="tpu_custom_call" | custom-call | tf_op jit(solution)/shard_map/mix_x/pallas_call | solution.py:205
  93.7 10.0 %all_to_all.25 = bf16[8,40,256]{2,1,0:T(8,128)(2,1)S(1)} all-to-all(bf16[8,40,256]{2,1,0:T(8,128)(2,1)} %mix_x.1), channel_id=1, replica_groups=mesh['zh'=4,'zl'=4,'c'=2,'x'=4,'y'=4] {'zl','c'}, dimensions={0} | all-to-all | bytes 327680 | tf_op jit(solution)/shard_map/all_to_all | solution.py:338
  103.7 19.7 %all_to_all.26.mixed_ref = bf16[16,80,256]{2,1,0:T(8,128)(2,1)} all-to-all(bf16[16,80,256]{2,1,0:T(8,128)(2,1)S(1)} %bitcast.9), channel_id=1, replica_groups=mesh['zh'=4,'zl'=4,'c'=2,'x'=4,'y'=4] {'x','y'}, dimensions={0} | all-to-all | bytes 1310720 | tf_op jit(solution)/shard_map/all_to_all | solution.py:340
  123.4 2.7 %mix_y.1 = bf16[4,320,128]{2,1,0:T(8,128)(2,1)} custom-call(s32[1]{0:T(128)} %bitcast.1.place_ref, f32[4,4]{1,0:T(4,128)} %kt_ref.1, bf16[16,80,256]{2,1,0:T(8,128)(2,1)} %all_to_all.26.mixed_ref, bf16[80,1024]{1,0:T(8,128)(2,1)} %copy-done.2, bf16[80,1024]{1,0:T(8,128)(2,1)} %copy-done.6, bf16[80,1024]{1,0:T(8,128)(2,1)} %copy-done.5, ...), custom_call_target="tpu_custom_call" | custom-call | tf_op jit(solution)/shard_map/mix_y/pallas_call | solution.py:247
  126.2 10.0 %all_to_all.27.smooth_ref = bf16[4,320,128]{2,1,0:T(8,128)(2,1)} all-to-all(bf16[4,320,128]{2,1,0:T(8,128)(2,1)} %mix_y.1), channel_id=1, replica_groups=mesh['zh'=4,'zl'=4,'c'=2,'x'=4,'y'=4] {'y'}, dimensions={0} | all-to-all | bytes 655360 | tf_op jit(solution)/shard_map/all_to_all | solution.py:341
  136.2 9.0 %gather.1 = bf16[8,8192]{1,0:T(8,128)(2,1)} custom-call(s32[1,1]{1,0:T(1,128)S(6)} %copy.9.count_ref, bf16[4,320,128]{2,1,0:T(8,128)(2,1)} %all_to_all.27.smooth_ref, s32[3,8192]{1,0:T(4,128)} %cells_ref.3, f32[3,8192]{1,0:T(4,128)} %fractions_ref.3), custom_call_target="tpu_custom_call" | custom-call | tf_op jit(solution)/shard_map/gather/pallas_call | solution.py:291
  (36 shorter events, 0.3 us)
Async XLA Ops:
  1.7 24.6 %all-to-all-start = ((bf16[8,32,1024]{2,1,0:T(8,128)(2,1)}), bf16[8,32,1024]{2,1,0:T(8,128)(2,1)S(1)}, u32[]{:S(2)}, u32[]{:S(2)}) async-start(bf16[8,32,1024]{2,1,0:T(8,128)(2,1)} %broadcast_in_dim.16), calls=%async_computation | async-start | bytes 1048576 | tf_op jit(solution)/shard_map/all_to_all | solution.py:317
  22.6 5.0 %collective-permute-start.1 = (f32[8,640]{1,0:T(8,128)}, f32[8,640]{1,0:T(8,128)S(1)}, u32[]{:S(2)}, u32[]{:S(2)}) collective-permute-start(f32[8,640]{1,0:T(8,128)} %get-tuple-element.27), channel_id=1, source_target_pairs={{0,1},{1,2},{2,3},{3,4},{4,5},{5,6},{6,7},{7,8},{8,9},{9,10},{10,1... | collective-permute-start | bytes 61448 | tf_op jit(solution)/shard_map/ppermute | solution.py:321
  26.3 44.9 %copy-start = (bf16[8,32,1024]{2,1,0:T(8,128)(2,1)}, bf16[8,32,1024]{2,1,0:T(8,128)(2,1)S(1)}, u32[]{:S(2)}) copy-start(bf16[8,32,1024]{2,1,0:T(8,128)(2,1)S(1)} %all-to-all-done) | copy-start | bytes 1572868
  26.3 4.7 %collective-permute-start = (f32[8,640]{1,0:T(8,128)}, f32[8,640]{1,0:T(8,128)S(1)}, u32[]{:S(2)}, u32[]{:S(2)}) collective-permute-start(f32[8,640]{1,0:T(8,128)} %get-tuple-element.26), channel_id=1, source_target_pairs={{1,0},{2,1},{3,2},{4,3},{5,4},{6,5},{7,6},{8,7},{9,8},{10,9},{11,1... | collective-permute-start | bytes 61448 | tf_op jit(solution)/shard_map/ppermute | solution.py:320
  27.6 3.4 %copy-start.8 = (f32[8,640]{1,0:T(8,128)}, f32[8,640]{1,0:T(8,128)S(1)}, u32[]{:S(2)}) copy-start(f32[8,640]{1,0:T(8,128)S(1)} %collective-permute-done.1.high_ref) | copy-start | bytes 61444
  31.1 0.6 copy-start.7
  33.9 7.6 %collective-permute-start.3 = (f32[16,256]{1,0:T(8,128)}, f32[16,256]{1,0:T(8,128)S(1)}, u32[]{:S(2)}, u32[]{:S(2)}) collective-permute-start(f32[16,256]{1,0:T(8,128)} %get-tuple-element.30), channel_id=1, source_target_pairs={{0,16},{16,32},{32,48},{48,64},{64,80},{80,96},{96,112},{112,128},... | collective-permute-start | bytes 49160 | tf_op jit(solution)/shard_map/ppermute | solution.py:324
  36.3 5.2 %collective-permute-start.2 = (f32[8,256]{1,0:T(8,128)}, f32[8,256]{1,0:T(8,128)S(1)}, u32[]{:S(2)}, u32[]{:S(2)}) collective-permute-start(f32[8,256]{1,0:T(8,128)} %get-tuple-element.29), channel_id=1, source_target_pairs={{16,0},{32,16},{48,32},{64,48},{80,64},{96,80},{112,96},{128,112},... | collective-permute-start | bytes 24584 | tf_op jit(solution)/shard_map/ppermute | solution.py:323
  41.5 0.6 copy-start.10
  41.5 0.6 copy-start.9
  44.0 14.6 %copy-start.3 = (bf16[64,1024]{1,0:T(8,128)(2,1)S(1)}, bf16[64,1024]{1,0:T(8,128)(2,1)}, u32[]{:S(2)}) copy-start(bf16[64,1024]{1,0:T(8,128)(2,1)} %ky_ref.1) | copy-start | bytes 393220
  44.0 46.6 %all-to-all-start.1 = ((bf16[32,32,256]{2,1,0:T(8,128)(2,1)}), bf16[32,32,256]{2,1,0:T(8,128)(2,1)S(1)}, u32[]{:S(2)}, u32[]{:S(2)}) async-start(bf16[32,32,256]{2,1,0:T(8,128)(2,1)} %add_rows.1), calls=%async_computation.1 | async-start | bytes 1048576 | tf_op jit(solution)/shard_map/all_to_all | solution.py:327
  58.7 35.0 %copy-start.2 = (bf16[80,1024]{1,0:T(8,128)(2,1)}, bf16[80,1024]{1,0:T(8,128)(2,1)S(1)}, u32[]{:S(2)}) copy-start(bf16[80,1024]{1,0:T(8,128)(2,1)S(1)} %maximum_maximum_fusion.k0_ref) | copy-start | bytes 491524
  58.7 21.3 %collective-permute-start.6 = (bf16[80,1024]{1,0:T(8,128)(2,1)S(1)}, bf16[80,1024]{1,0:T(8,128)(2,1)S(1)}, u32[]{:S(2)}, u32[]{:S(2)}) collective-permute-start(bf16[80,1024]{1,0:T(8,128)(2,1)S(1)} %maximum_maximum_fusion.k0_ref), channel_id=1, source_target_pairs={{0,3},{1,0},{2,1},{3,2},{4,7},{5,4},{6,5},{7,6},{8,11},{9,8},{10,9... | collective-permute-start | bytes 491528 | tf_op jit(solution)/shard_map/ppermute | solution.py:311
  65.5 14.5 %collective-permute-start.5 = (bf16[80,1024]{1,0:T(8,128)(2,1)S(1)}, bf16[80,1024]{1,0:T(8,128)(2,1)S(1)}, u32[]{:S(2)}, u32[]{:S(2)}) collective-permute-start(bf16[80,1024]{1,0:T(8,128)(2,1)S(1)} %maximum_maximum_fusion.k0_ref), channel_id=1, source_target_pairs={{0,2},{1,3},{2,0},{3,1},{4,6},{5,7},{6,4},{7,5},{8,10},{9,11},{10,... | collective-permute-start | bytes 491528 | tf_op jit(solution)/shard_map/ppermute | solution.py:311
  67.4 12.6 %collective-permute-start.4 = (bf16[80,1024]{1,0:T(8,128)(2,1)S(1)}, bf16[80,1024]{1,0:T(8,128)(2,1)S(1)}, u32[]{:S(2)}, u32[]{:S(2)}) collective-permute-start(bf16[80,1024]{1,0:T(8,128)(2,1)S(1)} %maximum_maximum_fusion.k0_ref), channel_id=1, source_target_pairs={{0,1},{1,2},{2,3},{3,0},{4,5},{5,6},{6,7},{7,4},{8,9},{9,10},{10,1... | collective-permute-start | bytes 491528 | tf_op jit(solution)/shard_map/ppermute | solution.py:311
  69.9 10.1 %collective-permute-start.8 = (bf16[2,1024]{1,0:T(2,128)(2,1)S(1)}, bf16[2,1024]{1,0:T(2,128)(2,1)S(1)}, u32[]{:S(2)}, u32[]{:S(2)}) collective-permute-start(bf16[2,1024]{1,0:T(2,128)(2,1)S(1)} %slice.17), channel_id=1, source_target_pairs={{128,0},{256,128},{384,256},{129,1},{257,129},{385,257},{130,2},{2... | collective-permute-start | bytes 12296 | tf_op jit(solution)/shard_map/ppermute | solution.py:329
  71.2 8.6 %collective-permute-start.7 = (bf16[1,1024]{1,0:T(2,128)(2,1)S(1)}, bf16[1,1024]{1,0:T(2,128)(2,1)S(1)}, u32[]{:S(2)}, u32[]{:S(2)}) collective-permute-start(bf16[1,1024]{1,0:T(2,128)(2,1)S(1)} %slice.16), channel_id=1, source_target_pairs={{0,128},{128,256},{256,384},{1,129},{129,257},{257,385},{2,130},{1... | collective-permute-start | bytes 6152 | tf_op jit(solution)/shard_map/ppermute | solution.py:328
  79.9 10.7 %copy-start.12 = (bf16[1,1024]{1,0:T(2,128)(2,1)}, bf16[1,1024]{1,0:T(2,128)(2,1)S(1)}, u32[]{:S(2)}) copy-start(bf16[1,1024]{1,0:T(2,128)(2,1)S(1)} %collective-permute-done.7.before_ref) | copy-start | bytes 6148
  80.0 10.6 %copy-start.11 = (bf16[2,1024]{1,0:T(2,128)(2,1)}, bf16[2,1024]{1,0:T(2,128)(2,1)S(1)}, u32[]{:S(2)}) copy-start(bf16[2,1024]{1,0:T(2,128)(2,1)S(1)} %collective-permute-done.8.after_ref) | copy-start | bytes 12292
  80.0 13.7 %copy-start.4 = (bf16[80,1024]{1,0:T(8,128)(2,1)}, bf16[80,1024]{1,0:T(8,128)(2,1)S(1)}, u32[]{:S(2)}) copy-start(bf16[80,1024]{1,0:T(8,128)(2,1)S(1)} %collective-permute-done.6.k3_ref) | copy-start | bytes 491524
  80.0 13.7 %copy-start.5 = (bf16[80,1024]{1,0:T(8,128)(2,1)}, bf16[80,1024]{1,0:T(8,128)(2,1)S(1)}, u32[]{:S(2)}) copy-start(bf16[80,1024]{1,0:T(8,128)(2,1)S(1)} %collective-permute-done.5.k2_ref) | copy-start | bytes 491524
  80.0 13.6 %copy-start.6 = (bf16[80,1024]{1,0:T(8,128)(2,1)}, bf16[80,1024]{1,0:T(8,128)(2,1)S(1)}, u32[]{:S(2)}) copy-start(bf16[80,1024]{1,0:T(8,128)(2,1)S(1)} %collective-permute-done.4.k1_ref) | copy-start | bytes 491524
  90.6 0.8 copy-start.1

commit v4 on v3

--- a/solution.py
+++ b/solution.py
@@ -12,12 +12,15 @@
 ROWS = 32
 COLS = 64
 XP = 40
+PART = 9
+STEP = 10
 YP = 80
 RIM = 384
 CHUNK = 512
 AXES = ("zh", "zl", "c", "x", "y")
 GX = ("zh", "zl", "c")
 NEAR = ("zl", "c")
+HOME = ("zl", "c", "y")
 GY = ("x", "y")
 HIGH = lax.Precision.HIGHEST
 
@@ -30,21 +33,18 @@
     return (first, second, third, fourth)
 
 
-def spread(cell, weights, extent):
-    row = lax.broadcasted_iota(jnp.int32, (extent, cell.shape[1]), 0) - cell
+def spread(cell, weights, row):
+    row = row - cell
     result = jnp.where(row == 3, weights[3], 0.0)
     for k in (2, 1, 0):
         result = jnp.where(row == k, weights[k], result)
     return result
 
 
-def point_factors(cells_ref, fractions_ref, where):
-    x_part = spread(
-        cells_ref[0:1, where] % ROWS, keys_weights(fractions_ref[0:1, where]), XP
-    )
-    y_part = spread(
-        cells_ref[1:2, where] % COLS, keys_weights(fractions_ref[1:2, where]), YP
-    )
+def point_factors(cells_ref, fractions_ref, where, row):
+    col = lax.broadcasted_iota(jnp.int32, (YP, CHUNK), 0)
+    x_part = spread(cells_ref[0:1, where] % ROWS, keys_weights(fractions_ref[0:1, where]), row)
+    y_part = spread(cells_ref[1:2, where] % COLS, keys_weights(fractions_ref[1:2, where]), col)
     day = cells_ref[2:3, where]
     y_days = [jnp.where(day == d, y_part, 0.0) for d in range(DAYS - 1)]
     y_days.append(jnp.zeros((256 - 3 * YP, y_part.shape[1]), jnp.float32))
@@ -67,7 +67,8 @@
     def step(number, carry):
         start = pl.multiple_of(number * CHUNK, CHUNK)
         where = pl.ds(start, CHUNK)
-        x_part, y_days, early, late = point_factors(cells_ref, fractions_ref, where)
+        row = lax.broadcasted_iota(jnp.int32, (XP, CHUNK), 0)
+        x_part, y_days, early, late = point_factors(cells_ref, fractions_ref, where, row)
         values = jnp.where(
             live_lanes(count_ref, start, CHUNK), probes_ref[:, where].astype(jnp.float32), 0.0
         )
@@ -192,26 +193,34 @@
     outer = [after_ref[...].astype(jnp.float32), blank, before_ref[...].astype(jnp.float32)]
     outer = jnp.concatenate(outer, axis=0).astype(jnp.bfloat16)
     outer = jnp.dot(outer, grid_ref[...], preferred_element_type=jnp.float32)
-    rows_ref[0:8, :] = outer
-    rows_ref[264:272, :] = outer
-    rows_ref[8:264, :] = jnp.dot(
-        kernel_ref[...], grid_ref[...], preferred_element_type=jnp.float32
-    )
-    for tile in range(8):
-        out_ref[tile] = rows_ref[7 + ROWS * tile : 7 + ROWS * tile + XP, :].astype(jnp.bfloat16)
+    inner = jnp.dot(kernel_ref[...], grid_ref[...], preferred_element_type=jnp.float32)
+    for side in range(2):
+        here = slice(128 * side, 128 * side + 128)
+        rows_ref[side, 0:8, :] = outer[:, here]
+        rows_ref[side, 264:272, :] = outer[:, here]
+        rows_ref[side, 8:264, :] = inner[:, here]
+    for part in range(4):
+        rows = []
+        for r in range(STEP):
+            start = 7 + PART * part + r
+            wide = [rows_ref[side, pl.ds(start, 8, stride=ROWS), :] for side in range(2)]
+            rows.append(jnp.concatenate(wide, axis=1))
+        out_ref[part] = jnp.concatenate(rows, axis=0).astype(jnp.bfloat16)
 
 
 def mix_x(grid, kernel, before, after):
     return pl.pallas_call(
         mix_x_kernel,
-        out_shape=jax.ShapeDtypeStruct((8, XP, 256), jnp.bfloat16),
-        scratch_shapes=[pltpu.VMEM((272, 256), jnp.float32)],
+        out_shape=jax.ShapeDtypeStruct((4, 8 * STEP, 256), jnp.bfloat16),
+        scratch_shapes=[pltpu.VMEM((2, 272, 128), jnp.float32)],
         name="mix_x",
     )(grid, kernel, before, after)
 
 
-def mix_y_kernel(place_ref, kt_ref, mixed_ref, k0_ref, k1_ref, k2_ref, k3_ref, out_ref):
-    rows = 2 * XP
+def mix_y_kernel(
+    place_ref, kt_ref, mixed_ref, k0_ref, k1_ref, k2_ref, k3_ref, out_ref, smooth_ref
+):
+    rows = 8 * STEP
     low = lax.broadcasted_iota(jnp.int32, (rows, 128), 1) < COLS
     left = [[] for _ in range(DAYS)]
     for pair in range(8):
@@ -231,35 +240,43 @@
             left, kernel, (((1,), (1,)), ((), ())), preferred_element_type=jnp.float32
         )
         by_day = [crossed[t * rows : (t + 1) * rows] for t in range(DAYS)]
-        smooth = []
         for s in range(DAYS):
             total = kt_ref[s, 0] * by_day[0]
             for t in range(1, DAYS):
                 total = total + kt_ref[s, t] * by_day[t]
-            smooth.append(total)
-        smooth = jnp.concatenate(smooth, axis=0).astype(jnp.bfloat16)
+            for which in range(2):
+                here = slice(128 * which, 128 * which + 128)
+                smooth_ref[which, s * rows : (s + 1) * rows, :] = total[:, here]
         for which in range(2):
             target = (place_ref[0] + 4 - (2 * half + which)) % 4
-            out_ref[target] = smooth[:, 128 * which : 128 * which + 128]
+            for tile in range(8):
+                part = smooth_ref[which, pl.ds(tile, DAYS * STEP, stride=8), :]
+                out_ref[tile, target] = part.astype(jnp.bfloat16)
 
 
 def mix_y(place, kt, mixed, pieces):
     return pl.pallas_call(
         mix_y_kernel,
-        out_shape=jax.ShapeDtypeStruct((4, DAYS * 2 * XP, 128), jnp.bfloat16),
+        out_shape=jax.ShapeDtypeStruct((8, 4, DAYS * STEP, 128), jnp.bfloat16),
         in_specs=[pl.BlockSpec(memory_space=pltpu.SMEM)] * 2
         + [pl.BlockSpec(memory_space=pltpu.VMEM)] * 5,
+        scratch_shapes=[pltpu.VMEM((2, DAYS * 8 * STEP, 128), jnp.float32)],
         name="mix_y",
     )(place, kt, mixed, *pieces)
 
 
-def gather_kernel(count_ref, smooth_ref, cells_ref, fractions_ref, out_ref, window_ref):
+def gather_kernel(
+    count_ref, smooth_ref, cells_ref, fractions_ref, out_ref, wide_ref, window_ref, sums_ref
+):
     points = out_ref.shape[1]
-    rows = PROBES * XP
+    rows = STEP * 4 * PROBES
+    wide_ref[...] = smooth_ref[...].astype(jnp.float32)
     days = []
     for s in range(DAYS):
-        part = [smooth_ref[source, s * 2 * XP : (s + 1) * 2 * XP, :] for source in range(4)]
-        days.append(jnp.concatenate(part, axis=0).astype(jnp.float32))
+        part = [
+            wide_ref[pl.ds(s * STEP + r, 4 * PROBES, stride=DAYS * STEP), :] for r in range(STEP)
+        ]
+        days.append(jnp.concatenate(part, axis=0))
     blank = jnp.zeros((rows, 128), jnp.float32)
     smooth = [jnp.concatenate([day, blank], axis=1) for day in days]
     for late in range(2):
@@ -270,15 +287,24 @@
     def step(number, carry):
         start = pl.multiple_of(number * CHUNK, CHUNK)
         where = pl.ds(start, CHUNK)
-        x_part, y_days, early, late = point_factors(cells_ref, fractions_ref, where)
+        row = lax.broadcasted_iota(jnp.int32, (8 * STEP, CHUNK), 0)
+        row = jnp.where(row // 8 < PART, PART * (row % 4) + row // 8, 8 * XP)
+        x_part, y_days, early, late = point_factors(cells_ref, fractions_ref, where, row)
         hidden = jnp.dot(window_ref[...], y_days, preferred_element_type=jnp.float32)
-        timed = early * hidden[0:rows] + late * hidden[rows : 2 * rows]
-        sums = []
-        for q in range(PROBES):
-            sums.append(
-                jnp.sum(timed[q * XP : (q + 1) * XP] * x_part, axis=0, keepdims=True)
-            )
-        result = jnp.concatenate(sums, axis=0)
+        total = jnp.zeros((4 * PROBES, CHUNK), jnp.float32)
+        for r in range(STEP):
+            here = slice(r * 4 * PROBES, (r + 1) * 4 * PROBES)
+            timed = early * hidden[here] + late * hidden[rows + here.start : rows + here.stop]
+            factor = x_part[8 * r : 8 * r + 8]
+            total += timed * jnp.concatenate([factor] * 4, axis=0)
+        result = jnp.zeros((PROBES, CHUNK), jnp.float32)
+        for side in range(CHUNK // 128):
+            sums_ref[side] = total[:, 128 * side : 128 * side + 128]
+        for part in range(4):
+            piece = [
+                sums_ref[side, pl.ds(part, PROBES, stride=4), :] for side in range(CHUNK // 128)
+            ]
+            result += jnp.concatenate(piece, axis=1)
         result = jnp.where(live_lanes(count_ref, start, CHUNK), result, 0.0)
         out_ref[:, where] = result.astype(jnp.bfloat16)
         return carry
@@ -287,13 +313,17 @@
 
 
 def gather(counts, smooth, cells, fractions):
-    rows = PROBES * XP
+    rows = STEP * 4 * PROBES
     return pl.pallas_call(
         gather_kernel,
         out_shape=jax.ShapeDtypeStruct((PROBES, cells.shape[1]), jnp.bfloat16),
         in_specs=[pl.BlockSpec(memory_space=pltpu.SMEM)]
         + [pl.BlockSpec(memory_space=pltpu.VMEM)] * 3,
-        scratch_shapes=[pltpu.VMEM((2 * rows, 256), jnp.bfloat16)],
+        scratch_shapes=[
+            pltpu.VMEM((DAYS * rows, 128), jnp.float32),
+            pltpu.VMEM((2 * rows, 256), jnp.bfloat16),
+            pltpu.VMEM((CHUNK // 128, 4 * PROBES, 128), jnp.float32),
+        ],
         name="gather",
     )(counts, smooth, cells, fractions)
 
@@ -316,10 +346,10 @@
     kernel = jnp.broadcast_to(kx[None], (8,) + kx.shape)
     kernel = lax.all_to_all(kernel, NEAR, 0, 0, tiled=True).reshape(8 * ROWS, 1024)
     core, low, high = scatter(counts, probes, cells, fractions, ky)
-    low, kernel = lax.optimization_barrier((low, kernel))
     low = lax.ppermute(low, GY, down(16))
     high = lax.ppermute(high, GY, up(16))
     core, first, last = add_cols(core, low, high)
+    first, last, kernel = lax.optimization_barrier((first, last, kernel))
     first = lax.ppermute(first, GX, down(32))
     last = lax.ppermute(last, GX, up(32))
     grid = add_rows(core, first, last)
@@ -335,11 +365,11 @@
     rest = (grid, ky_pieces, place, before, after)
     grid, ky_pieces, place, before, after = lax.optimization_barrier(rest)
     mixed = mix_x(grid.reshape(32 * ROWS, 256), kernel, before, after)
-    mixed = lax.all_to_all(mixed, NEAR, 0, 0, tiled=True)
-    mixed = jnp.broadcast_to(mixed.reshape(1, 4, 2 * XP, 256), (4, 4, 2 * XP, 256))
-    mixed = lax.all_to_all(mixed.reshape(16, 2 * XP, 256), GY, 0, 0, tiled=True)
-    smooth = lax.all_to_all(mix_y(place, kt, mixed, ky_pieces), "y", 0, 0, tiled=True)
-    return gather(counts, smooth, cells, fractions)
+    mixed = jnp.broadcast_to(mixed[None], (4,) + mixed.shape)
+    mixed = lax.all_to_all(mixed.reshape(16, 8 * STEP, 256), GY, 0, 0, tiled=True)
+    smooth = mix_y(place, kt, mixed, ky_pieces).reshape(32, DAYS * STEP, 128)
+    smooth = lax.all_to_all(smooth, HOME, 0, 0, tiled=True)
+    return gather(counts, smooth.reshape(32 * DAYS * STEP, 128), cells, fractions)
 
 
 def solution(mesh):

time: 148 us -> 144 us (0.973); the launches traced: 145 us -> 143 us
  waiting for transfers between devices: 19.6 us -> 15.8 us
    ppermute x1, waiting for transfers between devices: 3.42 us -> 0.01 us  [body(): low = lax.ppermute(low, GY, down(16))]
    all_to_all x1, starting transfers between devices: 13.1 us -> 10.2 us  [body(): grid = lax.all_to_all(grid, GX, 0, 0, tiled=True)]
    ppermute x1, starting transfers between devices: 1.28 us -> 3.99 us  [body(): high = lax.ppermute(high, GY, up(16))]
    all_to_all x1, waiting for transfers between devices: 2.46 us -> 0.01 us  [body(): lax.all_to_all(kernel, NEAR, 0, 0, tiled=True).reshape(8 * ROWS, 1024)]
    ppermute x1, starting transfers between devices: 2.43 us -> 4.68 us  [body(): last = lax.ppermute(last, GX, up(32))]
    all_to_all x3 -> x2, blocking collectives: 39.7 us -> 39.6 us  [the longest x1 20.2 us: body(): lax.all_to_all(mixed.reshape(16, 8 * STEP, 256), GY, 0, 0, tiled=True)]
  transfers between devices with their start and end apart: 11 -> 11, of which waited for: 6 -> 5; matrix products, arithmetic and copies ran while one was open for 1% -> 1% of each run, Pallas kernels for 7% -> 9%
where the time goes in v4:
time: 144 us; the launch traced here: 143 us
  starting transfers between devices  52.6 us (37%)
  blocking collectives  39.6 us (28%)
  Pallas kernels  28 us (19%)
  waiting for transfers between devices  15.8 us (11%)
  local copies, waits for them, and re-layouts  6.22 us (4%)
    all_to_all x1, blocking collectives, body(): lax.all_to_all(mixed.reshape(16, 8 * STEP, 256), GY, 0, 0, tiled=True)  20.2 us
    all_to_all x1, blocking collectives, body(): smooth = lax.all_to_all(smooth, HOME, 0, 0, tiled=True)  19.4 us
    ppermute x3, starting transfers between devices, turns(): lax.ppermute(piece, axis, [(i, (i + shift) % 4) for i in range(4)])  11.2 us
    all_to_all x1, waiting for transfers between devices, body(): grid = lax.all_to_all(grid, GX, 0, 0, tiled=True)  10.5 us
    all_to_all x1, starting transfers between devices, body(): lax.all_to_all(kernel, NEAR, 0, 0, tiled=True).reshape(8 * ROWS, 1024)  10.2 us
    all_to_all x1, starting transfers between devices, body(): grid = lax.all_to_all(grid, GX, 0, 0, tiled=True)  10.2 us
    pallas_call x1, Pallas kernels, scatter(): pl.pallas_call(scatter_kernel, out_shape=(jax.ShapeDtypeStruct((rows, 256...  9.99 us
    pallas_call x1, Pallas kernels, gather(): pl.pallas_call(gather_kernel, out_shape=jax.ShapeDtypeStruct((PROBES, cel...  8.63 us
  transfers between devices with their start and end apart: 11, of which 5 were waited for; matrix products, arithmetic and copies ran while one was open for 1% of the time, Pallas kernels for 9%

profile of v4, /device:TPU:1, one launch (start us, length us, event | category | flops | bytes accessed | tf_op | source)
XLA Modules:
  0.0 143.1 jit_solution(5427355063876624455)
XLA Ops:
  0.0 1.7 %broadcast_in_dim.6 = bf16[8,32,1024]{2,1,0:T(8,128)(2,1)} broadcast(bf16[32,1024]{1,0:T(8,128)(2,1)} %param.11), dimensions={1,2} | broadcast | bytes 589824 | tf_op jit(solution)/shard_map/broadcast_in_dim | solution.py:346
  1.7 10.2 %all-to-all-start = ((bf16[8,32,1024]{2,1,0:T(8,128)(2,1)}), bf16[8,32,1024]{2,1,0:T(8,128)(2,1)S(1)}, u32[]{:S(2)}, u32[]{:S(2)}) async-start(bf16[8,32,1024]{2,1,0:T(8,128)(2,1)} %broadcast_in_dim.6), calls=%async_computation | async-start | bytes 1048576 | tf_op jit(solution)/shard_map/all_to_all | solution.py:347
  12.6 10.0 %scatter.1 = (f32[320,256]{1,0:T(8,128)}, f32[8,640]{1,0:T(8,128)}, f32[8,640]{1,0:T(8,128)}) custom-call(s32[1,1]{1,0:T(1,128)S(6)} %copy.9.count_ref, bf16[8,8192]{1,0:T(8,128)(2,1)} %probes_ref.1, s32[3,8192]{1,0:T(4,128)} %cells_ref.3, f32[3,8192]{1,0:T(4,128)} %fractions_ref.3, bf16[64,1024]{1,0:T(8,128)(2,1)} %ky_ref.1), custom_call_target="tpu_custom_call" | custom-call | tf_op jit(solution)/shard_map/scatter/pallas_call | solution.py:122
  22.6 1.3 collective-permute-start
  23.9 4.0 %collective-permute-start.1 = (f32[8,640]{1,0:T(8,128)}, f32[8,640]{1,0:T(8,128)S(1)}, u32[]{:S(2)}, u32[]{:S(2)}) collective-permute-start(f32[8,640]{1,0:T(8,128)} %get-tuple-element.27), channel_id=1, source_target_pairs={{0,1},{1,2},{2,3},{3,4},{4,5},{5,6},{6,7},{7,8},{8,9},{9,10},{10,1... | collective-permute-start | bytes 61448 | tf_op jit(solution)/shard_map/ppermute | solution.py:350
  27.9 1.1 collective-permute-done.1.high_ref
  29.0 0.6 copy-done.8
  29.6 2.2 %add_cols.1 = (f32[320,256]{1,0:T(8,128)}, f32[8,256]{1,0:T(8,128)}, f32[16,256]{1,0:T(8,128)}) custom-call(f32[320,256]{1,0:T(8,128)} %get-tuple-element.25.core_ref, f32[8,640]{1,0:T(8,128)} %copy-done.7, f32[8,640]{1,0:T(8,128)} %copy-done.8), custom_call_target="tpu_custom_call" | custom-call | tf_op jit(solution)/shard_map/add_cols/pallas_call | solution.py:160
  31.8 4.7 %collective-permute-start.3 = (f32[16,256]{1,0:T(8,128)}, f32[16,256]{1,0:T(8,128)S(1)}, u32[]{:S(2)}, u32[]{:S(2)}) collective-permute-start(f32[16,256]{1,0:T(8,128)} %get-tuple-element.32), channel_id=1, source_target_pairs={{0,16},{16,32},{32,48},{48,64},{64,80},{80,96},{96,112},{112,128},... | collective-permute-start | bytes 49160 | tf_op jit(solution)/shard_map/ppermute | solution.py:354
  36.5 1.9 %collective-permute-start.2 = (f32[8,256]{1,0:T(8,128)}, f32[8,256]{1,0:T(8,128)S(1)}, u32[]{:S(2)}, u32[]{:S(2)}) collective-permute-start(f32[8,256]{1,0:T(8,128)} %get-tuple-element.31), channel_id=1, source_target_pairs={{16,0},{32,16},{48,32},{64,48},{80,64},{96,80},{112,96},{128,112},... | collective-permute-start | bytes 24584 | tf_op jit(solution)/shard_map/ppermute | solution.py:353
  38.4 3.3 %collective-permute-done.2.first_ref = f32[8,256]{1,0:T(8,128)S(1)} collective-permute-done((f32[8,256]{1,0:T(8,128)}, f32[8,256]{1,0:T(8,128)S(1)}, u32[]{:S(2)}, u32[]{:S(2)}) %collective-permute-start.2) | collective-permute-done | bytes 8224 | tf_op jit(solution)/shard_map/ppermute | solution.py:353
  41.6 0.6 copy-done.10
  42.2 1.9 %add_rows.1 = bf16[32,32,256]{2,1,0:T(8,128)(2,1)} custom-call(f32[320,256]{1,0:T(8,128)} %get-tuple-element.28.core_ref, f32[8,256]{1,0:T(8,128)} %copy-done.10, f32[16,256]{1,0:T(8,128)} %copy-done.9), custom_call_target="tpu_custom_call" | custom-call | tf_op jit(solution)/shard_map/add_rows/pallas_call | solution.py:184
  44.1 10.2 %all-to-all-start.1 = ((bf16[32,32,256]{2,1,0:T(8,128)(2,1)}), bf16[32,32,256]{2,1,0:T(8,128)(2,1)S(1)}, u32[]{:S(2)}, u32[]{:S(2)}) async-start(bf16[32,32,256]{2,1,0:T(8,128)(2,1)} %add_rows.1), calls=%async_computation.1 | async-start | bytes 1048576 | tf_op jit(solution)/shard_map/all_to_all | solution.py:357
  54.4 0.7 slice.24
  55.1 0.7 fusion
  55.8 0.1 maximum_maximum_fusion.k0_ref
  55.9 6.7 %collective-permute-start.6 = (bf16[80,1024]{1,0:T(8,128)(2,1)S(1)}, bf16[80,1024]{1,0:T(8,128)(2,1)S(1)}, u32[]{:S(2)}, u32[]{:S(2)}) collective-permute-start(bf16[80,1024]{1,0:T(8,128)(2,1)S(1)} %maximum_maximum_fusion.k0_ref), channel_id=1, source_target_pairs={{0,3},{1,0},{2,1},{3,2},{4,7},{5,4},{6,5},{7,6},{8,11},{9,8},{10,9... | collective-permute-start | bytes 491528 | tf_op jit(solution)/shard_map/ppermute | solution.py:341
  62.7 1.9 %collective-permute-start.5 = (bf16[80,1024]{1,0:T(8,128)(2,1)S(1)}, bf16[80,1024]{1,0:T(8,128)(2,1)S(1)}, u32[]{:S(2)}, u32[]{:S(2)}) collective-permute-start(bf16[80,1024]{1,0:T(8,128)(2,1)S(1)} %maximum_maximum_fusion.k0_ref), channel_id=1, source_target_pairs={{0,2},{1,3},{2,0},{3,1},{4,6},{5,7},{6,4},{7,5},{8,10},{9,11},{10,... | collective-permute-start | bytes 491528 | tf_op jit(solution)/shard_map/ppermute | solution.py:341
  64.6 2.5 %collective-permute-start.4 = (bf16[80,1024]{1,0:T(8,128)(2,1)S(1)}, bf16[80,1024]{1,0:T(8,128)(2,1)S(1)}, u32[]{:S(2)}, u32[]{:S(2)}) collective-permute-start(bf16[80,1024]{1,0:T(8,128)(2,1)S(1)} %maximum_maximum_fusion.k0_ref), channel_id=1, source_target_pairs={{0,1},{1,2},{2,3},{3,0},{4,5},{5,6},{6,7},{7,4},{8,9},{9,10},{10,1... | collective-permute-start | bytes 491528 | tf_op jit(solution)/shard_map/ppermute | solution.py:341
  67.1 1.3 collective-permute-start.8
  68.4 7.9 %collective-permute-start.7 = (bf16[1,1024]{1,0:T(2,128)(2,1)S(1)}, bf16[1,1024]{1,0:T(2,128)(2,1)S(1)}, u32[]{:S(2)}, u32[]{:S(2)}) collective-permute-start(bf16[1,1024]{1,0:T(2,128)(2,1)S(1)} %slice.16), channel_id=1, source_target_pairs={{0,128},{128,256},{256,384},{1,129},{129,257},{257,385},{2,130},{1... | collective-permute-start | bytes 6152 | tf_op jit(solution)/shard_map/ppermute | solution.py:358
  76.3 0.7 collective-permute-done.7.before_ref
  77.1 0.1 collective-permute-done.8.after_ref
  77.2 10.5 %all-to-all-done.1 = bf16[32,32,256]{2,1,0:T(8,128)(2,1)S(1)} async-done(((bf16[32,32,256]{2,1,0:T(8,128)(2,1)}), bf16[32,32,256]{2,1,0:T(8,128)(2,1)S(1)}, u32[]{:S(2)}, u32[]{:S(2)}) %all-to-all-start.1) | async-done | bytes 524320 | tf_op jit(solution)/shard_map/all_to_all | solution.py:357
  87.8 0.8 copy-done.1
  88.6 2.4 %mix_x.1 = bf16[4,80,256]{2,1,0:T(8,128)(2,1)} custom-call(bf16[1024,256]{1,0:T(8,128)(2,1)} %bitcast.14, bf16[256,1024]{1,0:T(8,128)(2,1)} %bitcast.13, bf16[1,1024]{1,0:T(2,128)(2,1)} %copy-done.12, bf16[2,1024]{1,0:T(2,128)(2,1)} %copy-done.11), custom_call_target="tpu_custom_call" | custom-call | tf_op jit(solution)/shard_map/mix_x/pallas_call | solution.py:212
  91.0 1.0 broadcast_in_dim.8
  92.0 20.2 %all_to_all.20.mixed_ref = bf16[16,80,256]{2,1,0:T(8,128)(2,1)} all-to-all(bf16[16,80,256]{2,1,0:T(8,128)(2,1)S(1)} %bitcast.10), channel_id=1, replica_groups=mesh['zh'=4,'zl'=4,'c'=2,'x'=4,'y'=4] {'x','y'}, dimensions={0} | all-to-all | bytes 1310720 | tf_op jit(solution)/shard_map/all_to_all | solution.py:369
  112.2 2.9 %mix_y.1 = bf16[8,4,40,128]{3,2,1,0:T(8,128)(2,1)} custom-call(s32[1]{0:T(128)} %bitcast.1.place_ref, f32[4,4]{1,0:T(4,128)} %kt_ref.1, bf16[16,80,256]{2,1,0:T(8,128)(2,1)} %all_to_all.20.mixed_ref, bf16[80,1024]{1,0:T(8,128)(2,1)} %copy-done.2, bf16[80,1024]{1,0:T(8,128)(2,1)} %copy-done.6, bf16[80,1024]{1,0:T(8,128)(2,1)} %copy-done.5, ...), custom_call_target="tpu_custom_call" | custom-call | tf_op jit(solution)/shard_map/mix_y/pallas_call | solution.py:258
  115.1 19.4 %all_to_all.21 = bf16[32,40,128]{2,1,0:T(8,128)(2,1)} all-to-all(bf16[32,40,128]{2,1,0:T(8,128)(2,1)} %bitcast.16), channel_id=1, replica_groups=mesh['zh'=4,'zl'=4,'c'=2,'x'=4,'y'=4] {'zl','c','y'}, dimensions={0} | all-to-all | bytes 655360 | tf_op jit(solution)/shard_map/all_to_all | solution.py:371
  134.5 8.6 %gather.1 = bf16[8,8192]{1,0:T(8,128)(2,1)} custom-call(s32[1,1]{1,0:T(1,128)S(6)} %copy.9.count_ref, bf16[1280,128]{1,0:T(8,128)(2,1)} %bitcast.15, s32[3,8192]{1,0:T(4,128)} %cells_ref.3, f32[3,8192]{1,0:T(4,128)} %fractions_ref.3), custom_call_target="tpu_custom_call" | custom-call | tf_op jit(solution)/shard_map/gather/pallas_call | solution.py:317
  (35 shorter events, 0.2 us)
Async XLA Ops:
  1.7 30.1 %all-to-all-start = ((bf16[8,32,1024]{2,1,0:T(8,128)(2,1)}), bf16[8,32,1024]{2,1,0:T(8,128)(2,1)S(1)}, u32[]{:S(2)}, u32[]{:S(2)}) async-start(bf16[8,32,1024]{2,1,0:T(8,128)(2,1)} %broadcast_in_dim.6), calls=%async_computation | async-start | bytes 1048576 | tf_op jit(solution)/shard_map/all_to_all | solution.py:347
  22.6 5.3 %collective-permute-start = (f32[8,640]{1,0:T(8,128)}, f32[8,640]{1,0:T(8,128)S(1)}, u32[]{:S(2)}, u32[]{:S(2)}) collective-permute-start(f32[8,640]{1,0:T(8,128)} %get-tuple-element.26), channel_id=1, source_target_pairs={{1,0},{2,1},{3,2},{4,3},{5,4},{6,5},{7,6},{8,7},{9,8},{10,9},{11,1... | collective-permute-start | bytes 61448 | tf_op jit(solution)/shard_map/ppermute | solution.py:349
  23.9 5.1 %collective-permute-start.1 = (f32[8,640]{1,0:T(8,128)}, f32[8,640]{1,0:T(8,128)S(1)}, u32[]{:S(2)}, u32[]{:S(2)}) collective-permute-start(f32[8,640]{1,0:T(8,128)} %get-tuple-element.27), channel_id=1, source_target_pairs={{0,1},{1,2},{2,3},{3,4},{4,5},{5,6},{6,7},{7,8},{8,9},{9,10},{10,1... | collective-permute-start | bytes 61448 | tf_op jit(solution)/shard_map/ppermute | solution.py:350
  27.9 1.1 copy-start.7
  29.0 0.6 copy-start.8
  31.8 36.6 %copy-start = (bf16[8,32,1024]{2,1,0:T(8,128)(2,1)}, bf16[8,32,1024]{2,1,0:T(8,128)(2,1)S(1)}, u32[]{:S(2)}) copy-start(bf16[8,32,1024]{2,1,0:T(8,128)(2,1)S(1)} %all-to-all-done) | copy-start | bytes 1572868
  31.8 9.9 %collective-permute-start.3 = (f32[16,256]{1,0:T(8,128)}, f32[16,256]{1,0:T(8,128)S(1)}, u32[]{:S(2)}, u32[]{:S(2)}) collective-permute-start(f32[16,256]{1,0:T(8,128)} %get-tuple-element.32), channel_id=1, source_target_pairs={{0,16},{16,32},{32,48},{48,64},{64,80},{80,96},{96,112},{112,128},... | collective-permute-start | bytes 49160 | tf_op jit(solution)/shard_map/ppermute | solution.py:354
  36.5 5.2 %collective-permute-start.2 = (f32[8,256]{1,0:T(8,128)}, f32[8,256]{1,0:T(8,128)S(1)}, u32[]{:S(2)}, u32[]{:S(2)}) collective-permute-start(f32[8,256]{1,0:T(8,128)} %get-tuple-element.31), channel_id=1, source_target_pairs={{16,0},{32,16},{48,32},{64,48},{80,64},{96,80},{112,96},{128,112},... | collective-permute-start | bytes 24584 | tf_op jit(solution)/shard_map/ppermute | solution.py:353
  41.6 0.6 copy-start.10
  41.6 0.6 copy-start.9
  44.1 11.7 %copy-start.3 = (bf16[64,1024]{1,0:T(8,128)(2,1)S(1)}, bf16[64,1024]{1,0:T(8,128)(2,1)}, u32[]{:S(2)}) copy-start(bf16[64,1024]{1,0:T(8,128)(2,1)} %ky_ref.1) | copy-start | bytes 393220
  44.1 43.7 %all-to-all-start.1 = ((bf16[32,32,256]{2,1,0:T(8,128)(2,1)}), bf16[32,32,256]{2,1,0:T(8,128)(2,1)S(1)}, u32[]{:S(2)}, u32[]{:S(2)}) async-start(bf16[32,32,256]{2,1,0:T(8,128)(2,1)} %add_rows.1), calls=%async_computation.1 | async-start | bytes 1048576 | tf_op jit(solution)/shard_map/all_to_all | solution.py:357
  55.9 35.1 %copy-start.2 = (bf16[80,1024]{1,0:T(8,128)(2,1)}, bf16[80,1024]{1,0:T(8,128)(2,1)S(1)}, u32[]{:S(2)}) copy-start(bf16[80,1024]{1,0:T(8,128)(2,1)S(1)} %maximum_maximum_fusion.k0_ref) | copy-start | bytes 491524
  55.9 21.3 %collective-permute-start.6 = (bf16[80,1024]{1,0:T(8,128)(2,1)S(1)}, bf16[80,1024]{1,0:T(8,128)(2,1)S(1)}, u32[]{:S(2)}, u32[]{:S(2)}) collective-permute-start(bf16[80,1024]{1,0:T(8,128)(2,1)S(1)} %maximum_maximum_fusion.k0_ref), channel_id=1, source_target_pairs={{0,3},{1,0},{2,1},{3,2},{4,7},{5,4},{6,5},{7,6},{8,11},{9,8},{10,9... | collective-permute-start | bytes 491528 | tf_op jit(solution)/shard_map/ppermute | solution.py:341
  62.7 14.5 %collective-permute-start.5 = (bf16[80,1024]{1,0:T(8,128)(2,1)S(1)}, bf16[80,1024]{1,0:T(8,128)(2,1)S(1)}, u32[]{:S(2)}, u32[]{:S(2)}) collective-permute-start(bf16[80,1024]{1,0:T(8,128)(2,1)S(1)} %maximum_maximum_fusion.k0_ref), channel_id=1, source_target_pairs={{0,2},{1,3},{2,0},{3,1},{4,6},{5,7},{6,4},{7,5},{8,10},{9,11},{10,... | collective-permute-start | bytes 491528 | tf_op jit(solution)/shard_map/ppermute | solution.py:341
  64.6 12.6 %collective-permute-start.4 = (bf16[80,1024]{1,0:T(8,128)(2,1)S(1)}, bf16[80,1024]{1,0:T(8,128)(2,1)S(1)}, u32[]{:S(2)}, u32[]{:S(2)}) collective-permute-start(bf16[80,1024]{1,0:T(8,128)(2,1)S(1)} %maximum_maximum_fusion.k0_ref), channel_id=1, source_target_pairs={{0,1},{1,2},{2,3},{3,0},{4,5},{5,6},{6,7},{7,4},{8,9},{9,10},{10,1... | collective-permute-start | bytes 491528 | tf_op jit(solution)/shard_map/ppermute | solution.py:341
  67.1 10.1 %collective-permute-start.8 = (bf16[2,1024]{1,0:T(2,128)(2,1)S(1)}, bf16[2,1024]{1,0:T(2,128)(2,1)S(1)}, u32[]{:S(2)}, u32[]{:S(2)}) collective-permute-start(bf16[2,1024]{1,0:T(2,128)(2,1)S(1)} %slice.17), channel_id=1, source_target_pairs={{128,0},{256,128},{384,256},{129,1},{257,129},{385,257},{130,2},{2... | collective-permute-start | bytes 12296 | tf_op jit(solution)/shard_map/ppermute | solution.py:359
  68.4 8.6 %collective-permute-start.7 = (bf16[1,1024]{1,0:T(2,128)(2,1)S(1)}, bf16[1,1024]{1,0:T(2,128)(2,1)S(1)}, u32[]{:S(2)}, u32[]{:S(2)}) collective-permute-start(bf16[1,1024]{1,0:T(2,128)(2,1)S(1)} %slice.16), channel_id=1, source_target_pairs={{0,128},{128,256},{256,384},{1,129},{129,257},{257,385},{2,130},{1... | collective-permute-start | bytes 6152 | tf_op jit(solution)/shard_map/ppermute | solution.py:358
  77.1 10.7 %copy-start.12 = (bf16[1,1024]{1,0:T(2,128)(2,1)}, bf16[1,1024]{1,0:T(2,128)(2,1)S(1)}, u32[]{:S(2)}) copy-start(bf16[1,1024]{1,0:T(2,128)(2,1)S(1)} %collective-permute-done.7.before_ref) | copy-start | bytes 6148
  77.2 10.6 %copy-start.11 = (bf16[2,1024]{1,0:T(2,128)(2,1)}, bf16[2,1024]{1,0:T(2,128)(2,1)S(1)}, u32[]{:S(2)}) copy-start(bf16[2,1024]{1,0:T(2,128)(2,1)S(1)} %collective-permute-done.8.after_ref) | copy-start | bytes 12292
  77.2 13.8 %copy-start.4 = (bf16[80,1024]{1,0:T(8,128)(2,1)}, bf16[80,1024]{1,0:T(8,128)(2,1)S(1)}, u32[]{:S(2)}) copy-start(bf16[80,1024]{1,0:T(8,128)(2,1)S(1)} %collective-permute-done.6.k3_ref) | copy-start | bytes 491524
  77.2 13.8 %copy-start.5 = (bf16[80,1024]{1,0:T(8,128)(2,1)}, bf16[80,1024]{1,0:T(8,128)(2,1)S(1)}, u32[]{:S(2)}) copy-start(bf16[80,1024]{1,0:T(8,128)(2,1)S(1)} %collective-permute-done.5.k2_ref) | copy-start | bytes 491524
  77.2 13.8 %copy-start.6 = (bf16[80,1024]{1,0:T(8,128)(2,1)}, bf16[80,1024]{1,0:T(8,128)(2,1)S(1)}, u32[]{:S(2)}) copy-start(bf16[80,1024]{1,0:T(8,128)(2,1)S(1)} %collective-permute-done.4.k1_ref) | copy-start | bytes 491524
  87.8 0.8 copy-start.1

commit v5 on v4

--- a/solution.py
+++ b/solution.py
@@ -25,6 +25,10 @@
 HIGH = lax.Precision.HIGHEST
 
 
+def near(*arrays):
+    return [pltpu.with_memory_space_constraint(array, pltpu.VMEM) for array in arrays]
+
+
 def keys_weights(fraction):
     first = ((-0.5 * fraction + 1.0) * fraction - 0.5) * fraction
     second = (1.5 * fraction - 2.5) * fraction * fraction + 1.0
@@ -59,12 +63,24 @@
 
 
 def scatter_kernel(
-    count_ref, probes_ref, cells_ref, fractions_ref, ky_ref, core_ref, low_ref, high_ref, acc_ref
+    count_ref,
+    probes_ref,
+    cells_ref,
+    fractions_ref,
+    ky_ref,
+    core_ref,
+    low_ref,
+    high_ref,
+    acc_ref,
+    left0_ref,
+    left1_ref,
+    right0_ref,
+    right1_ref,
 ):
-    points = probes_ref.shape[1]
+    chunks = probes_ref.shape[1] // CHUNK
     acc_ref[...] = jnp.zeros_like(acc_ref)
 
-    def step(number, carry):
+    def prepare(number, left_ref, right_ref):
         start = pl.multiple_of(number * CHUNK, CHUNK)
         where = pl.ds(start, CHUNK)
         row = lax.broadcasted_iota(jnp.int32, (XP, CHUNK), 0)
@@ -77,13 +93,26 @@
             timed = weight * values
             for q in range(PROBES):
                 parts.append(timed[q : q + 1] * x_part)
-        weighted = jnp.concatenate(parts, axis=0).astype(jnp.bfloat16)
+        left_ref[...] = jnp.concatenate(parts, axis=0).astype(jnp.bfloat16)
+        right_ref[...] = y_days
+
+    def product(left_ref, right_ref):
         acc_ref[...] += lax.dot_general(
-            weighted, y_days, (((1,), (1,)), ((), ())), preferred_element_type=jnp.float32
+            left_ref[...],
+            right_ref[...],
+            (((1,), (1,)), ((), ())),
+            preferred_element_type=jnp.float32,
         )
+
+    def step(number, carry):
+        product(left0_ref, right0_ref)
+        prepare(2 * number + 1, left1_ref, right1_ref)
+        product(left1_ref, right1_ref)
+        prepare(jnp.minimum(2 * number + 2, chunks - 1), left0_ref, right0_ref)
         return carry
 
-    lax.fori_loop(0, points // CHUNK, step, 0)
+    prepare(0, left0_ref, right0_ref)
+    lax.fori_loop(0, chunks // 2, step, 0)
     rows = PROBES * XP
     blank = jnp.zeros((rows, 128), jnp.float32)
     first = jnp.concatenate([acc_ref[0:rows, :], blank], axis=1)
@@ -122,13 +151,15 @@
     return pl.pallas_call(
         scatter_kernel,
         out_shape=(
-            jax.ShapeDtypeStruct((rows, 256), jnp.float32),
-            jax.ShapeDtypeStruct((8, RIM + 256), jnp.float32),
-            jax.ShapeDtypeStruct((8, RIM + 256), jnp.float32),
+            pltpu.VMEM((rows, 256), jnp.float32),
+            pltpu.VMEM((8, RIM + 256), jnp.float32),
+            pltpu.VMEM((8, RIM + 256), jnp.float32),
         ),
         in_specs=[pl.BlockSpec(memory_space=pltpu.SMEM)]
         + [pl.BlockSpec(memory_space=pltpu.VMEM)] * 4,
-        scratch_shapes=[pltpu.VMEM((2 * rows, 256), jnp.float32)],
+        scratch_shapes=[pltpu.VMEM((2 * rows, 256), jnp.float32)]
+        + [pltpu.VMEM((2 * rows, CHUNK), jnp.bfloat16)] * 2
+        + [pltpu.VMEM((256, CHUNK), jnp.bfloat16)] * 2,
         name="scatter",
     )(counts, probes, cells, fractions, ky)
 
@@ -160,12 +191,12 @@
     return pl.pallas_call(
         add_cols_kernel,
         out_shape=(
-            jax.ShapeDtypeStruct(core.shape, jnp.float32),
-            jax.ShapeDtypeStruct((PROBES, 256), jnp.float32),
-            jax.ShapeDtypeStruct((2 * PROBES, 256), jnp.float32),
+            pltpu.VMEM(core.shape, jnp.float32),
+            pltpu.VMEM((PROBES, 256), jnp.float32),
+            pltpu.VMEM((2 * PROBES, 256), jnp.float32),
         ),
         name="add_cols",
-    )(core, low, high)
+    )(*near(core, low, high))
 
 
 def add_rows_kernel(core_ref, first_ref, last_ref, out_ref):
@@ -183,9 +214,9 @@
 def add_rows(core, first, last):
     return pl.pallas_call(
         add_rows_kernel,
-        out_shape=jax.ShapeDtypeStruct((4 * PROBES, ROWS, 256), jnp.bfloat16),
+        out_shape=pltpu.VMEM((4 * PROBES, ROWS, 256), jnp.bfloat16),
         name="add_rows",
-    )(core, first, last)
+    )(*near(core, first, last))
 
 
 def mix_x_kernel(grid_ref, kernel_ref, before_ref, after_ref, out_ref, rows_ref):
@@ -205,16 +236,18 @@
             start = 7 + PART * part + r
             wide = [rows_ref[side, pl.ds(start, 8, stride=ROWS), :] for side in range(2)]
             rows.append(jnp.concatenate(wide, axis=1))
-        out_ref[part] = jnp.concatenate(rows, axis=0).astype(jnp.bfloat16)
+        rows = jnp.concatenate(rows, axis=0).astype(jnp.bfloat16)
+        for copy in range(4):
+            out_ref[4 * copy + part] = rows
 
 
 def mix_x(grid, kernel, before, after):
     return pl.pallas_call(
         mix_x_kernel,
-        out_shape=jax.ShapeDtypeStruct((4, 8 * STEP, 256), jnp.bfloat16),
+        out_shape=pltpu.VMEM((16, 8 * STEP, 256), jnp.bfloat16),
         scratch_shapes=[pltpu.VMEM((2, 272, 128), jnp.float32)],
         name="mix_x",
-    )(grid, kernel, before, after)
+    )(*near(grid, kernel, before, after))
 
 
 def mix_y_kernel(
@@ -257,16 +290,29 @@
 def mix_y(place, kt, mixed, pieces):
     return pl.pallas_call(
         mix_y_kernel,
-        out_shape=jax.ShapeDtypeStruct((8, 4, DAYS * STEP, 128), jnp.bfloat16),
+        out_shape=pltpu.VMEM((8, 4, DAYS * STEP, 128), jnp.bfloat16),
         in_specs=[pl.BlockSpec(memory_space=pltpu.SMEM)] * 2
         + [pl.BlockSpec(memory_space=pltpu.VMEM)] * 5,
         scratch_shapes=[pltpu.VMEM((2, DAYS * 8 * STEP, 128), jnp.float32)],
         name="mix_y",
-    )(place, kt, mixed, *pieces)
+    )(place, kt, *near(mixed, *pieces))
 
 
 def gather_kernel(
-    count_ref, smooth_ref, cells_ref, fractions_ref, out_ref, wide_ref, window_ref, sums_ref
+    count_ref,
+    smooth_ref,
+    cells_ref,
+    fractions_ref,
+    out_ref,
+    wide_ref,
+    window_ref,
+    sums_ref,
+    x0_ref,
+    x1_ref,
+    y0_ref,
+    y1_ref,
+    t0_ref,
+    t1_ref,
 ):
     points = out_ref.shape[1]
     rows = STEP * 4 * PROBES
@@ -284,18 +330,26 @@
         window = window + pltpu.roll(smooth[late + 2], 2 * YP, 1)
         window_ref[late * rows : (late + 1) * rows, :] = window.astype(jnp.bfloat16)
 
-    def step(number, carry):
+    row = lax.broadcasted_iota(jnp.int32, (8 * STEP, CHUNK), 0)
+    row = jnp.where(row // 8 < PART, PART * (row % 4) + row // 8, 8 * XP)
+
+    def prepare(number, x_ref, y_ref, t_ref):
+        where = pl.ds(pl.multiple_of(number * CHUNK, CHUNK), CHUNK)
+        x_part, y_days, early, late = point_factors(cells_ref, fractions_ref, where, row)
+        x_ref[...] = x_part
+        y_ref[...] = y_days
+        t_ref[0:1, :] = early
+        t_ref[1:2, :] = late
+
+    def product(number, x_ref, y_ref, t_ref):
         start = pl.multiple_of(number * CHUNK, CHUNK)
-        where = pl.ds(start, CHUNK)
-        row = lax.broadcasted_iota(jnp.int32, (8 * STEP, CHUNK), 0)
-        row = jnp.where(row // 8 < PART, PART * (row % 4) + row // 8, 8 * XP)
-        x_part, y_days, early, late = point_factors(cells_ref, fractions_ref, where, row)
-        hidden = jnp.dot(window_ref[...], y_days, preferred_element_type=jnp.float32)
+        early, late = t_ref[0:1, :], t_ref[1:2, :]
+        hidden = jnp.dot(window_ref[...], y_ref[...], preferred_element_type=jnp.float32)
         total = jnp.zeros((4 * PROBES, CHUNK), jnp.float32)
         for r in range(STEP):
             here = slice(r * 4 * PROBES, (r + 1) * 4 * PROBES)
             timed = early * hidden[here] + late * hidden[rows + here.start : rows + here.stop]
-            factor = x_part[8 * r : 8 * r + 8]
+            factor = x_ref[8 * r : 8 * r + 8, :]
             total += timed * jnp.concatenate([factor] * 4, axis=0)
         result = jnp.zeros((PROBES, CHUNK), jnp.float32)
         for side in range(CHUNK // 128):
@@ -306,10 +360,17 @@
             ]
             result += jnp.concatenate(piece, axis=1)
         result = jnp.where(live_lanes(count_ref, start, CHUNK), result, 0.0)
-        out_ref[:, where] = result.astype(jnp.bfloat16)
+        out_ref[:, pl.ds(start, CHUNK)] = result.astype(jnp.bfloat16)
+
+    def step(number, carry):
+        prepare(2 * number + 1, x1_ref, y1_ref, t1_ref)
+        product(2 * number, x0_ref, y0_ref, t0_ref)
+        prepare(jnp.minimum(2 * number + 2, points // CHUNK - 1), x0_ref, y0_ref, t0_ref)
+        product(2 * number + 1, x1_ref, y1_ref, t1_ref)
         return carry
 
-    lax.fori_loop(0, points // CHUNK, step, 0)
+    prepare(0, x0_ref, y0_ref, t0_ref)
+    lax.fori_loop(0, points // CHUNK // 2, step, 0)
 
 
 def gather(counts, smooth, cells, fractions):
@@ -323,9 +384,25 @@
             pltpu.VMEM((DAYS * rows, 128), jnp.float32),
             pltpu.VMEM((2 * rows, 256), jnp.bfloat16),
             pltpu.VMEM((CHUNK // 128, 4 * PROBES, 128), jnp.float32),
-        ],
+        ]
+        + [pltpu.VMEM((8 * STEP, CHUNK), jnp.float32)] * 2
+        + [pltpu.VMEM((256, CHUNK), jnp.bfloat16)] * 2
+        + [pltpu.VMEM((8, CHUNK), jnp.float32)] * 2,
         name="gather",
-    )(counts, smooth, cells, fractions)
+    )(counts, *near(smooth, cells, fractions))
+
+
+def copies_kernel(kernel_ref, out_ref):
+    for copy in range(8):
+        out_ref[copy] = kernel_ref[...]
+
+
+def copies(kernel):
+    return pl.pallas_call(
+        copies_kernel,
+        out_shape=pltpu.VMEM((8,) + kernel.shape, kernel.dtype),
+        name="copies",
+    )(kernel)
 
 
 def up(count):
@@ -343,8 +420,7 @@
 
 
 def body(probes, cells, fractions, counts, kx, ky, kt):
-    kernel = jnp.broadcast_to(kx[None], (8,) + kx.shape)
-    kernel = lax.all_to_all(kernel, NEAR, 0, 0, tiled=True).reshape(8 * ROWS, 1024)
+    kernel = lax.all_to_all(copies(kx), NEAR, 0, 0, tiled=True).reshape(8 * ROWS, 1024)
     core, low, high = scatter(counts, probes, cells, fractions, ky)
     low = lax.ppermute(low, GY, down(16))
     high = lax.ppermute(high, GY, up(16))
@@ -365,8 +441,7 @@
     rest = (grid, ky_pieces, place, before, after)
     grid, ky_pieces, place, before, after = lax.optimization_barrier(rest)
     mixed = mix_x(grid.reshape(32 * ROWS, 256), kernel, before, after)
-    mixed = jnp.broadcast_to(mixed[None], (4,) + mixed.shape)
-    mixed = lax.all_to_all(mixed.reshape(16, 8 * STEP, 256), GY, 0, 0, tiled=True)
+    mixed = lax.all_to_all(mixed, GY, 0, 0, tiled=True)
     smooth = mix_y(place, kt, mixed, ky_pieces).reshape(32, DAYS * STEP, 128)
     smooth = lax.all_to_all(smooth, HOME, 0, 0, tiled=True)
     return gather(counts, smooth.reshape(32 * DAYS * STEP, 128), cells, fractions)

time: 144 us -> 128 us (0.89)
  Pallas kernels: 28 us -> 18.7 us
  local copies, waits for them, and re-layouts: 6.22 us -> 0.14 us
    pallas_call x5 -> x6, Pallas kernels: 19.3 us -> 12.5 us  [the longest x1 7.4 us: scatter(): pl.pallas_call(scatter_kernel, out_shape=(pltpu.VMEM((rows, 256), jnp.flo...]
    unnamed x28 -> x8, local copies, waits for them, and re-layouts: 2.74 us -> 0.03 us
    broadcast_in_dim x2 -> x0, local copies, waits for them, and re-layouts: 2.67 us -> none  [the longest x1 1.71 us: body(): kernel = jnp.broadcast_to(kx[None], (8,) + kx.shape)]
    pallas_call x1, Pallas kernels: 8.63 us -> 6.26 us  [gather(): pl.pallas_call(gather_kernel, out_shape=jax.ShapeDtypeStruct((PROBES, cel...]
  transfers between devices with their start and end apart: 11 -> 11, of which waited for: 5 -> 5; matrix products, arithmetic and copies ran while one was open for 1% -> 0% of each run, Pallas kernels for 9% -> 6%
where the time goes in v5:
time: 128 us
  starting transfers between devices  52.6 us (41%)
  blocking collectives  38.4 us (30%)
  Pallas kernels  18.7 us (15%)
  waiting for transfers between devices  16.6 us (13%)
    all_to_all x1, blocking collectives, body(): mixed = lax.all_to_all(mixed, GY, 0, 0, tiled=True)  20.2 us
    all_to_all x1, blocking collectives, body(): smooth = lax.all_to_all(smooth, HOME, 0, 0, tiled=True)  18.2 us
    ppermute x3, starting transfers between devices, turns(): lax.ppermute(piece, axis, [(i, (i + shift) % 4) for i in range(4)])  11.2 us
    all_to_all x1, waiting for transfers between devices, body(): grid = lax.all_to_all(grid, GX, 0, 0, tiled=True)  10.4 us
    all_to_all x1, starting transfers between devices, body(): lax.all_to_all(copies(kx), NEAR, 0, 0, tiled=True).reshape(8 * ROWS, 1024)  10.2 us
    all_to_all x1, starting transfers between devices, body(): grid = lax.all_to_all(grid, GX, 0, 0, tiled=True)  10.2 us
    ppermute x1, starting transfers between devices, body(): before = lax.ppermute(kernel[8 * ROWS - 1:], 'zh', up(4))  7.89 us
    pallas_call x1, Pallas kernels, scatter(): pl.pallas_call(scatter_kernel, out_shape=(pltpu.VMEM((rows, 256), jnp.flo...  7.4 us
  transfers between devices with their start and end apart: 11, of which 5 were waited for; matrix products, arithmetic and copies ran while one was open for 0% of the time, Pallas kernels for 6%

profile of v5, /device:TPU:1, one launch (start us, length us, event | category | flops | bytes accessed | tf_op | source)
XLA Modules:
  0.0 127.5 jit_solution(9317508521316809647)
XLA Ops:
  0.0 1.7 %copies.1 = bf16[8,32,1024]{2,1,0:T(8,128)(2,1)} custom-call(bf16[32,1024]{1,0:T(8,128)(2,1)} %kernel_ref.1), custom_call_target="tpu_custom_call" | custom-call | tf_op jit(solution)/shard_map/copies/pallas_call | solution.py:401
  1.7 10.2 %all-to-all-start = ((bf16[8,32,1024]{2,1,0:T(8,128)(2,1)}), bf16[8,32,1024]{2,1,0:T(8,128)(2,1)S(1)}, u32[]{:S(2)}, u32[]{:S(2)}) async-start(bf16[8,32,1024]{2,1,0:T(8,128)(2,1)} %copies.1), calls=%async_computation | async-start | bytes 1048576 | tf_op jit(solution)/shard_map/all_to_all | solution.py:423
  12.5 7.4 %scatter.1 = (f32[320,256]{1,0:T(8,128)S(1)}, f32[8,640]{1,0:T(8,128)S(1)}, f32[8,640]{1,0:T(8,128)S(1)}) custom-call(s32[1,1]{1,0:T(1,128)S(6)} %copy.9.count_ref, bf16[8,8192]{1,0:T(8,128)(2,1)} %probes_ref.1, s32[3,8192]{1,0:T(4,128)} %cells_ref.3, f32[3,8192]{1,0:T(4,128)} %fractions_ref.3, bf16[64,1024]{1,0:T(8,128)(2,1)} %ky_ref.1), custom_call_target="tpu_custom_call" | custom-call | tf_op jit(solution)/shard_map/scatter/pallas_call | solution.py:151
  20.0 1.3 %collective-permute-start = (f32[8,640]{1,0:T(8,128)S(1)}, f32[8,640]{1,0:T(8,128)S(1)}, u32[]{:S(2)}, u32[]{:S(2)}) collective-permute-start(f32[8,640]{1,0:T(8,128)S(1)} %get-tuple-element.26), channel_id=1, source_target_pairs={{1,0},{2,1},{3,2},{4,3},{5,4},{6,5},{7,6},{8,7},{9,8},{10,9},{11,1... | collective-permute-start | bytes 61448 | tf_op jit(solution)/shard_map/ppermute | solution.py:425
  21.3 4.0 %collective-permute-start.1 = (f32[8,640]{1,0:T(8,128)S(1)}, f32[8,640]{1,0:T(8,128)S(1)}, u32[]{:S(2)}, u32[]{:S(2)}) collective-permute-start(f32[8,640]{1,0:T(8,128)S(1)} %get-tuple-element.27), channel_id=1, source_target_pairs={{0,1},{1,2},{2,3},{3,4},{4,5},{5,6},{6,7},{7,8},{8,9},{9,10},{10,1... | collective-permute-start | bytes 61448 | tf_op jit(solution)/shard_map/ppermute | solution.py:426
  25.2 0.0 collective-permute-done.low_ref
  25.3 0.9 collective-permute-done.1.high_ref
  26.1 0.5 add_cols.1
  26.6 0.0 all-to-all-done
  26.6 4.7 %collective-permute-start.3 = (f32[16,256]{1,0:T(8,128)S(1)}, f32[16,256]{1,0:T(8,128)S(1)}, u32[]{:S(2)}, u32[]{:S(2)}) collective-permute-start(f32[16,256]{1,0:T(8,128)S(1)} %get-tuple-element.32), channel_id=1, source_target_pairs={{0,16},{16,32},{32,48},{48,64},{64,80},{80,96},{96,112},{112,128},... | collective-permute-start | bytes 49160 | tf_op jit(solution)/shard_map/ppermute | solution.py:430
  31.3 1.9 %collective-permute-start.2 = (f32[8,256]{1,0:T(8,128)S(1)}, f32[8,256]{1,0:T(8,128)S(1)}, u32[]{:S(2)}, u32[]{:S(2)}) collective-permute-start(f32[8,256]{1,0:T(8,128)S(1)} %get-tuple-element.31), channel_id=1, source_target_pairs={{16,0},{32,16},{48,32},{64,48},{80,64},{96,80},{112,96},{128,112},... | collective-permute-start | bytes 24584 | tf_op jit(solution)/shard_map/ppermute | solution.py:429
  33.2 3.0 %collective-permute-done.2.first_ref = f32[8,256]{1,0:T(8,128)S(1)} collective-permute-done((f32[8,256]{1,0:T(8,128)S(1)}, f32[8,256]{1,0:T(8,128)S(1)}, u32[]{:S(2)}, u32[]{:S(2)}) %collective-permute-start.2) | collective-permute-done | bytes 8224 | tf_op jit(solution)/shard_map/ppermute | solution.py:429
  36.3 0.0 collective-permute-done.3.last_ref
  36.3 0.9 add_rows.1
  37.2 10.2 %all-to-all-start.1 = ((bf16[32,32,256]{2,1,0:T(8,128)(2,1)}), bf16[32,32,256]{2,1,0:T(8,128)(2,1)S(1)}, u32[]{:S(2)}, u32[]{:S(2)}) async-start(bf16[32,32,256]{2,1,0:T(8,128)(2,1)} %add_rows.1), calls=%async_computation.1 | async-start | bytes 1048576 | tf_op jit(solution)/shard_map/all_to_all | solution.py:433
  47.4 0.1 pad.3.clone
  47.5 0.1 maximum_maximum_fusion.k0_ref
  47.6 6.8 %collective-permute-start.6 = (bf16[80,1024]{1,0:T(8,128)(2,1)S(1)}, bf16[80,1024]{1,0:T(8,128)(2,1)S(1)}, u32[]{:S(2)}, u32[]{:S(2)}) collective-permute-start(bf16[80,1024]{1,0:T(8,128)(2,1)S(1)} %maximum_maximum_fusion.k0_ref), channel_id=1, source_target_pairs={{0,3},{1,0},{2,1},{3,2},{4,7},{5,4},{6,5},{7,6},{8,11},{9,8},{10,9... | collective-permute-start | bytes 491528 | tf_op jit(solution)/shard_map/ppermute | solution.py:418
  54.3 1.9 %collective-permute-start.5 = (bf16[80,1024]{1,0:T(8,128)(2,1)S(1)}, bf16[80,1024]{1,0:T(8,128)(2,1)S(1)}, u32[]{:S(2)}, u32[]{:S(2)}) collective-permute-start(bf16[80,1024]{1,0:T(8,128)(2,1)S(1)} %maximum_maximum_fusion.k0_ref), channel_id=1, source_target_pairs={{0,2},{1,3},{2,0},{3,1},{4,6},{5,7},{6,4},{7,5},{8,10},{9,11},{10,... | collective-permute-start | bytes 491528 | tf_op jit(solution)/shard_map/ppermute | solution.py:418
  56.3 2.5 %collective-permute-start.4 = (bf16[80,1024]{1,0:T(8,128)(2,1)S(1)}, bf16[80,1024]{1,0:T(8,128)(2,1)S(1)}, u32[]{:S(2)}, u32[]{:S(2)}) collective-permute-start(bf16[80,1024]{1,0:T(8,128)(2,1)S(1)} %maximum_maximum_fusion.k0_ref), channel_id=1, source_target_pairs={{0,1},{1,2},{2,3},{3,0},{4,5},{5,6},{6,7},{7,4},{8,9},{9,10},{10,1... | collective-permute-start | bytes 491528 | tf_op jit(solution)/shard_map/ppermute | solution.py:418
  58.8 1.3 %collective-permute-start.8 = (bf16[2,1024]{1,0:T(2,128)(2,1)S(1)}, bf16[2,1024]{1,0:T(2,128)(2,1)S(1)}, u32[]{:S(2)}, u32[]{:S(2)}) collective-permute-start(bf16[2,1024]{1,0:T(2,128)(2,1)S(1)} %slice.17), channel_id=1, source_target_pairs={{128,0},{256,128},{384,256},{129,1},{257,129},{385,257},{130,2},{2... | collective-permute-start | bytes 12296 | tf_op jit(solution)/shard_map/ppermute | solution.py:435
  60.1 7.9 %collective-permute-start.7 = (bf16[1,1024]{1,0:T(2,128)(2,1)S(1)}, bf16[1,1024]{1,0:T(2,128)(2,1)S(1)}, u32[]{:S(2)}, u32[]{:S(2)}) collective-permute-start(bf16[1,1024]{1,0:T(2,128)(2,1)S(1)} %slice.16), channel_id=1, source_target_pairs={{0,128},{128,256},{256,384},{1,129},{129,257},{257,385},{2,130},{1... | collective-permute-start | bytes 6152 | tf_op jit(solution)/shard_map/ppermute | solution.py:434
  68.0 0.7 collective-permute-done.7.before_ref
  68.7 1.5 %collective-permute-done.8.after_ref = bf16[2,1024]{1,0:T(2,128)(2,1)S(1)} collective-permute-done((bf16[2,1024]{1,0:T(2,128)(2,1)S(1)}, bf16[2,1024]{1,0:T(2,128)(2,1)S(1)}, u32[]{:S(2)}, u32[]{:S(2)}) %collective-permute-start.8) | collective-permute-done | bytes 4128 | tf_op jit(solution)/shard_map/ppermute | solution.py:435
  70.3 10.4 %all-to-all-done.1 = bf16[32,32,256]{2,1,0:T(8,128)(2,1)S(1)} async-done(((bf16[32,32,256]{2,1,0:T(8,128)(2,1)}), bf16[32,32,256]{2,1,0:T(8,128)(2,1)S(1)}, u32[]{:S(2)}, u32[]{:S(2)}) %all-to-all-start.1) | async-done | bytes 524320 | tf_op jit(solution)/shard_map/all_to_all | solution.py:433
  80.7 0.6 mix_x.1
  81.3 20.2 %all_to_all.20.mixed_ref = bf16[16,80,256]{2,1,0:T(8,128)(2,1)S(1)} all-to-all(bf16[16,80,256]{2,1,0:T(8,128)(2,1)S(1)} %mix_x.1), channel_id=1, replica_groups=mesh['zh'=4,'zl'=4,'c'=2,'x'=4,'y'=4] {'x','y'}, dimensions={0} | all-to-all | bytes 1310720 | tf_op jit(solution)/shard_map/all_to_all | solution.py:444
  101.5 1.5 %mix_y.1 = bf16[8,4,40,128]{3,2,1,0:T(8,128)(2,1)S(1)} custom-call(s32[1]{0:T(128)} %bitcast.1.place_ref, f32[4,4]{1,0:T(4,128)} %kt_ref.1, bf16[16,80,256]{2,1,0:T(8,128)(2,1)S(1)} %all_to_all.20.mixed_ref, bf16[80,1024]{1,0:T(8,128)(2,1)S(1)} %maximum_maximum_fusion.k0_ref, bf16[80,1024]{1,0:T(8,128)(2,1)S(1)} %collective-permute-done.4.k1_ref, ...), custom_call_target="tpu_custom_call" | custom-call | tf_op jit(solution)/shard_map/mix_y/pallas_call | solution.py:291
  103.0 0.0 copy-start
  103.0 0.0 copy-start.1
  103.0 18.2 %all_to_all.21 = bf16[32,40,128]{2,1,0:T(8,128)(2,1)S(1)} all-to-all(bf16[32,40,128]{2,1,0:T(8,128)(2,1)S(1)} %bitcast.14), channel_id=1, replica_groups=mesh['zh'=4,'zl'=4,'c'=2,'x'=4,'y'=4] {'zl','c','y'}, dimensions={0} | all-to-all | bytes 655360 | tf_op jit(solution)/shard_map/all_to_all | solution.py:446
  121.2 6.3 %gather.1 = bf16[8,8192]{1,0:T(8,128)(2,1)} custom-call(s32[1,1]{1,0:T(1,128)S(6)} %copy.9.count_ref, bf16[1280,128]{1,0:T(8,128)(2,1)S(1)} %bitcast.13, s32[3,8192]{1,0:T(4,128)S(1)} %copy-done, f32[3,8192]{1,0:T(4,128)S(1)} %copy-done.1), custom_call_target="tpu_custom_call" | custom-call | tf_op jit(solution)/shard_map/gather/pallas_call | solution.py:378
  (14 shorter events, 0.1 us)
Async XLA Ops:
  1.7 25.0 %all-to-all-start = ((bf16[8,32,1024]{2,1,0:T(8,128)(2,1)}), bf16[8,32,1024]{2,1,0:T(8,128)(2,1)S(1)}, u32[]{:S(2)}, u32[]{:S(2)}) async-start(bf16[8,32,1024]{2,1,0:T(8,128)(2,1)} %copies.1), calls=%async_computation | async-start | bytes 1048576 | tf_op jit(solution)/shard_map/all_to_all | solution.py:423
  20.0 5.3 %collective-permute-start = (f32[8,640]{1,0:T(8,128)S(1)}, f32[8,640]{1,0:T(8,128)S(1)}, u32[]{:S(2)}, u32[]{:S(2)}) collective-permute-start(f32[8,640]{1,0:T(8,128)S(1)} %get-tuple-element.26), channel_id=1, source_target_pairs={{1,0},{2,1},{3,2},{4,3},{5,4},{6,5},{7,6},{8,7},{9,8},{10,9},{11,1... | collective-permute-start | bytes 61448 | tf_op jit(solution)/shard_map/ppermute | solution.py:425
  21.3 4.9 %collective-permute-start.1 = (f32[8,640]{1,0:T(8,128)S(1)}, f32[8,640]{1,0:T(8,128)S(1)}, u32[]{:S(2)}, u32[]{:S(2)}) collective-permute-start(f32[8,640]{1,0:T(8,128)S(1)} %get-tuple-element.27), channel_id=1, source_target_pairs={{0,1},{1,2},{2,3},{3,4},{4,5},{5,6},{6,7},{7,8},{8,9},{9,10},{10,1... | collective-permute-start | bytes 61448 | tf_op jit(solution)/shard_map/ppermute | solution.py:426
  26.6 9.7 %collective-permute-start.3 = (f32[16,256]{1,0:T(8,128)S(1)}, f32[16,256]{1,0:T(8,128)S(1)}, u32[]{:S(2)}, u32[]{:S(2)}) collective-permute-start(f32[16,256]{1,0:T(8,128)S(1)} %get-tuple-element.32), channel_id=1, source_target_pairs={{0,16},{16,32},{32,48},{48,64},{64,80},{80,96},{96,112},{112,128},... | collective-permute-start | bytes 49160 | tf_op jit(solution)/shard_map/ppermute | solution.py:430
  31.3 5.0 %collective-permute-start.2 = (f32[8,256]{1,0:T(8,128)S(1)}, f32[8,256]{1,0:T(8,128)S(1)}, u32[]{:S(2)}, u32[]{:S(2)}) collective-permute-start(f32[8,256]{1,0:T(8,128)S(1)} %get-tuple-element.31), channel_id=1, source_target_pairs={{16,0},{32,16},{48,32},{64,48},{80,64},{96,80},{112,96},{128,112},... | collective-permute-start | bytes 24584 | tf_op jit(solution)/shard_map/ppermute | solution.py:429
  37.2 10.3 %copy-start.2 = (bf16[64,1024]{1,0:T(8,128)(2,1)S(1)}, bf16[64,1024]{1,0:T(8,128)(2,1)}, u32[]{:S(2)}) copy-start(bf16[64,1024]{1,0:T(8,128)(2,1)} %ky_ref.1) | copy-start | bytes 393220
  37.2 43.5 %all-to-all-start.1 = ((bf16[32,32,256]{2,1,0:T(8,128)(2,1)}), bf16[32,32,256]{2,1,0:T(8,128)(2,1)S(1)}, u32[]{:S(2)}, u32[]{:S(2)}) async-start(bf16[32,32,256]{2,1,0:T(8,128)(2,1)} %add_rows.1), calls=%async_computation.1 | async-start | bytes 1048576 | tf_op jit(solution)/shard_map/all_to_all | solution.py:433
  47.6 22.7 %collective-permute-start.6 = (bf16[80,1024]{1,0:T(8,128)(2,1)S(1)}, bf16[80,1024]{1,0:T(8,128)(2,1)S(1)}, u32[]{:S(2)}, u32[]{:S(2)}) collective-permute-start(bf16[80,1024]{1,0:T(8,128)(2,1)S(1)} %maximum_maximum_fusion.k0_ref), channel_id=1, source_target_pairs={{0,3},{1,0},{2,1},{3,2},{4,7},{5,4},{6,5},{7,6},{8,11},{9,8},{10,9... | collective-permute-start | bytes 491528 | tf_op jit(solution)/shard_map/ppermute | solution.py:418
  54.3 15.9 %collective-permute-start.5 = (bf16[80,1024]{1,0:T(8,128)(2,1)S(1)}, bf16[80,1024]{1,0:T(8,128)(2,1)S(1)}, u32[]{:S(2)}, u32[]{:S(2)}) collective-permute-start(bf16[80,1024]{1,0:T(8,128)(2,1)S(1)} %maximum_maximum_fusion.k0_ref), channel_id=1, source_target_pairs={{0,2},{1,3},{2,0},{3,1},{4,6},{5,7},{6,4},{7,5},{8,10},{9,11},{10,... | collective-permute-start | bytes 491528 | tf_op jit(solution)/shard_map/ppermute | solution.py:418
  56.3 14.0 %collective-permute-start.4 = (bf16[80,1024]{1,0:T(8,128)(2,1)S(1)}, bf16[80,1024]{1,0:T(8,128)(2,1)S(1)}, u32[]{:S(2)}, u32[]{:S(2)}) collective-permute-start(bf16[80,1024]{1,0:T(8,128)(2,1)S(1)} %maximum_maximum_fusion.k0_ref), channel_id=1, source_target_pairs={{0,1},{1,2},{2,3},{3,0},{4,5},{5,6},{6,7},{7,4},{8,9},{9,10},{10,1... | collective-permute-start | bytes 491528 | tf_op jit(solution)/shard_map/ppermute | solution.py:418
  58.8 11.5 %collective-permute-start.8 = (bf16[2,1024]{1,0:T(2,128)(2,1)S(1)}, bf16[2,1024]{1,0:T(2,128)(2,1)S(1)}, u32[]{:S(2)}, u32[]{:S(2)}) collective-permute-start(bf16[2,1024]{1,0:T(2,128)(2,1)S(1)} %slice.17), channel_id=1, source_target_pairs={{128,0},{256,128},{384,256},{129,1},{257,129},{385,257},{130,2},{2... | collective-permute-start | bytes 12296 | tf_op jit(solution)/shard_map/ppermute | solution.py:435
  60.1 8.6 %collective-permute-start.7 = (bf16[1,1024]{1,0:T(2,128)(2,1)S(1)}, bf16[1,1024]{1,0:T(2,128)(2,1)S(1)}, u32[]{:S(2)}, u32[]{:S(2)}) collective-permute-start(bf16[1,1024]{1,0:T(2,128)(2,1)S(1)} %slice.16), channel_id=1, source_target_pairs={{0,128},{128,256},{256,384},{1,129},{129,257},{257,385},{2,130},{1... | collective-permute-start | bytes 6152 | tf_op jit(solution)/shard_map/ppermute | solution.py:434
  103.0 18.2 %copy-start = (s32[3,8192]{1,0:T(4,128)S(1)}, s32[3,8192]{1,0:T(4,128)}, u32[]{:S(2)}) copy-start(s32[3,8192]{1,0:T(4,128)} %cells_ref.3) | copy-start | bytes 294916
  103.0 18.2 %copy-start.1 = (f32[3,8192]{1,0:T(4,128)S(1)}, f32[3,8192]{1,0:T(4,128)}, u32[]{:S(2)}) copy-start(f32[3,8192]{1,0:T(4,128)} %fractions_ref.3) | copy-start | bytes 294916
